TPU v7x, 32 devices: a whole 2x2x4 slice. The times are simulated.
32 devices in a mesh: dp: 8 (over y, x, core), seq: 4 (over z).
Axes of the slice: x: 2, y: 2, z: 4, core: 2. Of those that a mesh axis runs over, the one named last changes fastest.
Arguments:
- hidden_in: bfloat16 [8, 1024, 2048], P('dp', 'seq'), may hold values from -6 to 6
- doc_lengths: int32 [8, 3], P('dp'), may hold values from 1 to 768, 1024 in all within a row
- norm_gain: bfloat16 [2048], replicated, may hold values from 0.5 to 1.5
- in_weight: bfloat16 [8192, 2048], P(('dp', 'seq')), may hold values from -0.125 to 0.125
- conv_weight: bfloat16 [4, 4096], P(None, ('dp', 'seq')), may hold values from -3 to 3
- conv_bias: bfloat16 [4096], P(('dp', 'seq')), may hold values from -3 to 3
- x_weight: bfloat16 [4096, 160], P(('dp', 'seq'))
- dt_weight: bfloat16 [4096, 128], P(('dp', 'seq')), may hold values from -0.5 to 0.5
- dt_bias: bfloat16 [4096], P(('dp', 'seq')), may hold values from -8 to -1
- skip_gain: bfloat16 [4096], P(('dp', 'seq')), may hold values from 0.5 to 1.5
- out_weight: bfloat16 [4096, 2048], P(('dp', 'seq')), may hold values from -0.25 to 0.25
- out_cotangent: bfloat16 [8, 1024, 2048], P('dp', 'seq'), may hold values from -6 to 6
Outputs:
- output: bfloat16 [8, 1024, 2048], P('dp', 'seq')
- grad_in: bfloat16 [8, 1024, 2048], P('dp', 'seq')
- grad_norm_gain: float32 [2048], replicated
- grad_in_weight: float32 [8192, 2048], P(('dp', 'seq'))
- grad_conv_weight: float32 [4, 4096], P(None, ('dp', 'seq'))
- grad_conv_bias: float32 [4096], P(('dp', 'seq'))
- grad_x_weight: float32 [4096, 160], P(('dp', 'seq'))
- grad_dt_weight: float32 [4096, 128], P(('dp', 'seq'))
- grad_dt_bias: float32 [4096], P(('dp', 'seq'))
- grad_skip_gain: float32 [4096], P(('dp', 'seq'))
- grad_out_weight: float32 [4096, 2048], P(('dp', 'seq'))
Inputs may be any that keep to these rules, and one draw needn't show every extreme that they name: `doc_lengths`: each row holds the lengths of 3 packed documents in order, summing to 1024; the longest is 768.
All inputs are finite; a program needn't handle non-finite values.
Results may differ from a plain program's by a relative error of at most 0.012.
Values may be sent and summed in bfloat16 or wider, within the bound.
A program may use at most 320 MiB of HBM per device.

v0:
```python
import math

import jax
import jax.numpy as jnp
from jax import lax
from jax.sharding import PartitionSpec as P

E = 4096
N = 16
R = 128
KCONV = 4


norm_eps = 1e-05


def shifted(block, axis, distance):
    devices = range(lax.axis_size(axis))
    route = [(i - distance, i) for i in devices if i - distance in devices]
    return lax.ppermute(block, axis, route)


def carried_in(shard, axis, combine, identity, reverse):
    size, index = (lax.axis_size(axis), lax.axis_index(axis))
    everything = jax.tree.map(lambda part: lax.all_gather(part, axis), shard)
    start = jax.tree.map(
        lambda part, zero: jnp.broadcast_to(jnp.asarray(zero, part.dtype), part.shape),
        shard,
        identity,
    )

    def turn(k, before):
        at = size - 1 - k if reverse else k
        reached = at > index if reverse else at < index
        new = combine(before, jax.tree.map(lambda part: part[at], everything))
        return jax.tree.map(lambda a, b: jnp.where(reached, a, b), new, before)

    return lax.fori_loop(0, size, turn, start)


def silu_slope(pre_value):
    sigmoid_of = jax.nn.sigmoid(pre_value)
    return sigmoid_of * (1.0 + pre_value * (1.0 - sigmoid_of))


def token_begins(lengths, first_pos, position_count):
    doc_ends = jnp.cumsum(lengths, axis=1)
    doc_starts = doc_ends - lengths
    places = first_pos + jnp.arange(position_count, dtype=jnp.int32)
    inside = doc_starts[:, None, :] <= places[None, :, None]
    return (jnp.max(jnp.where(inside, doc_starts[:, None, :], 0), axis=2), places)


def decay_of(step_t, key_t, keep_t):
    return keep_t[:, :, None] * (1.0 - step_t[:, None, :] * (key_t * key_t)[:, :, None])


def run_block(state_in, step_b, inject_b, key_b, query_b, keep_b):

    def advance_one(carried, token_in):
        step_t, inject_t, key_t, query_t, keep_t = token_in
        carried = (
            decay_of(step_t, key_t, keep_t) * carried + inject_t[:, None, :] * key_t[:, :, None]
        )
        return (carried, jnp.sum(carried * query_t[:, :, None], axis=1))

    return lax.scan(advance_one, state_in, (step_b, inject_b, key_b, query_b, keep_b))


def link_pair(earlier_pair, later_pair):
    return (earlier_pair[0] * later_pair[0], later_pair[0] * earlier_pair[1] + later_pair[1])


def contract_rows(left_mat, right_mat):
    return lax.dot_general(
        left_mat, right_mat, (((0,), (0,)), ((), ())), preferred_element_type=jnp.float32
    )


def contract_cols(left_mat, right_mat):
    return lax.dot_general(
        left_mat, right_mat, (((1,), (1,)), ((), ())), preferred_element_type=jnp.float32
    )


def local(
    hidden_in,
    doc_lengths,
    norm_gain,
    in_weight,
    conv_weight,
    conv_bias,
    x_weight,
    dt_weight,
    dt_bias,
    skip_gain,
    out_weight,
    out_cotangent,
):
    seq_count, span_len, model_width = hidden_in.shape
    row_count = seq_count * span_len
    sub_len = math.gcd(span_len, 16)
    block_count = span_len // sub_len
    lag_max = KCONV - 1
    first_pos = lax.axis_index("seq") * span_len
    begins, places = token_begins(doc_lengths, first_pos, span_len)
    keep_mask = (places[None, :] != begins).astype(jnp.float32)
    conv_taps, conv_shift, proj_whole, rate_whole, rate_shift, skip_whole = (
        lax.all_gather(conv_weight, ("dp", "seq"), axis=1, tiled=True),
        lax.all_gather(conv_bias, ("dp", "seq"), axis=0, tiled=True),
        lax.all_gather(x_weight, ("dp", "seq"), axis=0, tiled=True),
        lax.all_gather(dt_weight, ("dp", "seq"), axis=0, tiled=True),
        lax.all_gather(dt_bias, ("dp", "seq"), axis=0, tiled=True),
        lax.all_gather(skip_gain, ("dp", "seq"), axis=0, tiled=True),
    )
    conv_taps = conv_taps.astype(jnp.float32)
    skip_full = skip_whole.astype(jnp.float32)

    def to_time(values):
        return jnp.swapaxes(values.reshape(seq_count, span_len, -1), 0, 1)

    def to_blocks(values):
        timed = to_time(values)
        return timed.reshape(block_count, sub_len, seq_count, timed.shape[-1])

    def from_blocks(values):
        return jnp.swapaxes(values.reshape(span_len, seq_count, -1), 0, 1).reshape(row_count, -1)

    x_full = hidden_in.reshape(row_count, model_width).astype(jnp.float32)
    inv_rms = lax.rsqrt(jnp.mean(x_full * x_full, axis=1, keepdims=True) + norm_eps)
    gain_full = norm_gain.astype(jnp.float32)
    normed = (x_full * inv_rms * gain_full).astype(jnp.bfloat16)
    pre_act = contract_cols(normed, lax.all_gather(in_weight, ("dp", "seq"), axis=0, tiled=True))
    pre_low = pre_act.astype(jnp.bfloat16)
    x_inner = pre_low[:, :E].reshape(seq_count, span_len, E)
    z_inner = pre_low[:, E:].astype(jnp.float32)
    edge_rows = shifted(x_inner[:, span_len - lag_max :, :], "seq", 1)
    padded = jnp.concatenate([edge_rows, x_inner], axis=1)
    conv_sum = jnp.broadcast_to(conv_shift.astype(jnp.float32), (seq_count, span_len, E))
    tap_masks = []
    for tap_idx in range(KCONV):
        lag_len = lag_max - tap_idx
        tap_valid = places[None, :] - lag_len >= begins
        tap_masks.append(tap_valid)
        window = padded[:, tap_idx : tap_idx + span_len, :].astype(jnp.float32)
        conv_sum = conv_sum + jnp.where(tap_valid[:, :, None], window * conv_taps[tap_idx], 0.0)
    conv_flat = conv_sum.reshape(row_count, E)
    xc_low = jax.nn.silu(conv_flat).astype(jnp.bfloat16)
    xc_full = xc_low.astype(jnp.float32)
    projected = jnp.dot(xc_low, proj_whole, preferred_element_type=jnp.float32)
    rate_low = projected[:, :R].astype(jnp.bfloat16)
    key_rows = projected[:, R : R + N]
    query_rows = projected[:, R + N :]
    beta_rate = jax.nn.sigmoid(contract_cols(rate_low, rate_whole) + rate_shift.astype(jnp.float32))
    denominator = 1.0 + beta_rate * jnp.sum(key_rows * key_rows, axis=1, keepdims=True)
    step_size = beta_rate / denominator
    inject = step_size * xc_full
    keep_rows = keep_mask.reshape(row_count, 1)
    step_seq = to_time(step_size)
    key_seq = to_time(key_rows)
    query_seq = to_time(query_rows)
    keep_seq = to_time(keep_rows)
    zero_state = jnp.zeros((seq_count, N, E), jnp.float32)
    unit_state = jnp.ones((seq_count, N, E), jnp.float32)
    block_inputs = (
        to_blocks(step_size),
        to_blocks(inject),
        to_blocks(key_rows),
        to_blocks(query_rows),
        to_blocks(keep_rows),
    )

    def chain_step(carried, token_in):
        state_now, product = carried
        step_t, inject_t, key_t, keep_t = token_in
        decay_now = decay_of(step_t, key_t, keep_t)
        return (
            (decay_now * state_now + inject_t[:, None, :] * key_t[:, :, None], decay_now * product),
            None,
        )

    def chain_block(carried, inputs_b):
        step_b, inject_b, key_b, query_b, keep_b = inputs_b
        advanced, unused_tok = lax.scan(chain_step, carried, (step_b, inject_b, key_b, keep_b))
        return (advanced, carried)

    (local_end, decay_all), (local_starts, product_starts) = lax.scan(
        chain_block, (zero_state, unit_state), block_inputs
    )
    start_state = carried_in(
        (decay_all, local_end), "seq", link_pair, (unit_state, zero_state), False
    )[1]
    saved_states = local_starts + product_starts * start_state[None]
    cot_low = out_cotangent.reshape(row_count, model_width)
    d_gated = contract_cols(cot_low, lax.all_gather(out_weight, ("dp", "seq"), axis=0, tiled=True))
    z_gate = jax.nn.silu(z_inner)
    d_mixed = d_gated * z_gate
    dy_seq = to_time(d_mixed)

    def pull_step(carried, token_in):
        step_t, key_t, query_t, keep_t, dy_t = token_in
        return (
            decay_of(step_t, key_t, keep_t) * (carried + dy_t[:, None, :] * query_t[:, :, None]),
            None,
        )

    local_pull, unused_pull = lax.scan(
        pull_step, zero_state, (step_seq, key_seq, query_seq, keep_seq, dy_seq), reverse=True
    )
    end_grad = carried_in(
        (decay_all, local_pull), "seq", link_pair, (unit_state, zero_state), True
    )[1]

    def backward_block(carried, inputs_b):
        state_at, step_b, inject_b, key_b, query_b, keep_b, dy_b = inputs_b

        def local_run(state_in, step_in, inject_in, key_in, query_in):
            return run_block(state_in, step_in, inject_in, key_in, query_in, keep_b)

        run_result, pullback = jax.vjp(local_run, state_at, step_b, inject_b, key_b, query_b)
        d_state, d_step_b, d_inject_b, d_key_b, d_query_b = pullback((carried, dy_b))
        return (d_state, (d_step_b, d_inject_b, d_key_b, d_query_b, run_result[1]))

    start_grad, (d_step_blocks, d_inject_blocks, d_key_blocks, d_query_blocks, mix_blocks) = (
        lax.scan(
            backward_block,
            end_grad,
            (saved_states,) + block_inputs + (to_blocks(d_mixed),),
            reverse=True,
        )
    )
    y_full = from_blocks(mix_blocks) + skip_full * xc_full
    gated_low = (y_full * z_gate).astype(jnp.bfloat16)
    part_cols = gated_low
    branch_out = jnp.dot(
        part_cols,
        lax.all_gather(out_weight, ("dp", "seq"), axis=0, tiled=True),
        preferred_element_type=jnp.float32,
    )
    output = (x_full + branch_out).astype(jnp.bfloat16).reshape(seq_count, span_len, model_width)
    part_cols = gated_low
    grad_out_weight = lax.psum_scatter(
        contract_rows(part_cols, cot_low), ("dp", "seq"), scatter_dimension=0, tiled=True
    )
    d_zin = d_gated * y_full * silu_slope(z_inner)
    d_inject = from_blocks(d_inject_blocks)
    d_step = from_blocks(d_step_blocks) + d_inject * xc_full
    den_square = denominator * denominator
    d_norm = -jnp.sum(d_step * beta_rate * beta_rate / den_square, axis=1, keepdims=True)
    d_keys = from_blocks(d_key_blocks) + 2.0 * key_rows * d_norm
    d_queries = from_blocks(d_query_blocks)
    d_rate = (d_step / den_square * beta_rate * (1.0 - beta_rate)).astype(jnp.bfloat16)
    grad_dt_bias = jnp.sum(d_rate.astype(jnp.float32), axis=0)
    grad_dt_weight = contract_rows(d_rate, rate_low)
    d_rate_low = jnp.dot(d_rate, rate_whole, preferred_element_type=jnp.float32)
    d_proj = jnp.concatenate([d_rate_low, d_keys, d_queries], axis=1).astype(jnp.bfloat16)
    grad_x_weight = contract_rows(xc_low, d_proj)
    grad_skip_gain = jnp.sum(d_mixed * xc_full, axis=0)
    d_conv_out = contract_cols(d_proj, proj_whole) + step_size * d_inject + skip_full * d_mixed
    d_conv = (d_conv_out * silu_slope(conv_flat)).reshape(seq_count, span_len, E)
    grad_conv_bias = jnp.sum(d_conv, axis=(0, 1))
    tap_grads = []
    for tap_idx in range(KCONV):
        window = padded[:, tap_idx : tap_idx + span_len, :].astype(jnp.float32)
        tap_grads.append(
            jnp.sum(jnp.where(tap_masks[tap_idx][:, :, None], d_conv * window, 0.0), axis=(0, 1))
        )
    grad_conv_weight = jnp.stack(tap_grads)
    edge_grads = shifted(d_conv[:, :lag_max, :].astype(jnp.bfloat16), "seq", -1).astype(jnp.float32)
    extended = jnp.concatenate([d_conv, edge_grads], axis=1)
    next_begins, next_places = token_begins(doc_lengths, first_pos + span_len, lag_max)
    ext_begins = jnp.concatenate([begins, next_begins], axis=1)
    ext_places = jnp.concatenate([places, next_places])
    d_x_inner = jnp.zeros((seq_count, span_len, E), jnp.float32)
    for tap_idx in range(KCONV):
        lag_len = lag_max - tap_idx
        reach_ok = ext_places[None, :] - lag_len >= ext_begins
        contrib = jnp.where(reach_ok[:, :, None], extended, 0.0) * conv_taps[tap_idx]
        d_x_inner = d_x_inner + contrib[:, lag_len : lag_len + span_len, :]
    d_pre = jnp.concatenate([d_x_inner.reshape(row_count, E), d_zin], axis=1).astype(jnp.bfloat16)
    part_cols = d_pre
    grad_in_weight = lax.psum_scatter(
        contract_rows(part_cols, normed), ("dp", "seq"), scatter_dimension=0, tiled=True
    )
    part_cols = d_pre
    d_normed = jnp.dot(
        part_cols,
        lax.all_gather(in_weight, ("dp", "seq"), axis=0, tiled=True),
        preferred_element_type=jnp.float32,
    )
    gain_local = jnp.sum(d_normed * x_full * inv_rms, axis=0)
    scaled = d_normed * gain_full
    grad_rows = (
        cot_low.astype(jnp.float32)
        + inv_rms * scaled
        - x_full * (inv_rms * inv_rms * inv_rms) * jnp.mean(x_full * scaled, axis=1, keepdims=True)
    )
    grad_in = grad_rows.astype(jnp.bfloat16).reshape(seq_count, span_len, model_width)
    (
        grad_conv_weight,
        grad_conv_bias,
        grad_x_weight,
        grad_dt_weight,
        grad_dt_bias,
        grad_skip_gain,
    ) = (
        lax.psum_scatter(grad_conv_weight, ("dp", "seq"), scatter_dimension=1, tiled=True),
        lax.psum_scatter(grad_conv_bias, ("dp", "seq"), scatter_dimension=0, tiled=True),
        lax.psum_scatter(grad_x_weight, ("dp", "seq"), scatter_dimension=0, tiled=True),
        lax.psum_scatter(grad_dt_weight, ("dp", "seq"), scatter_dimension=0, tiled=True),
        lax.psum_scatter(grad_dt_bias, ("dp", "seq"), scatter_dimension=0, tiled=True),
        lax.psum_scatter(grad_skip_gain, ("dp", "seq"), scatter_dimension=0, tiled=True),
    )
    grad_norm_gain = lax.psum(gain_local, ("dp", "seq"))
    return (
        output,
        grad_in,
        grad_norm_gain,
        grad_in_weight,
        grad_conv_weight,
        grad_conv_bias,
        grad_x_weight,
        grad_dt_weight,
        grad_dt_bias,
        grad_skip_gain,
        grad_out_weight,
    )


def solution(mesh):
    placed = (
        P("dp", "seq", None),
        P("dp", None),
        P(),
        P(("dp", "seq"), None),
        P(None, ("dp", "seq")),
        P(("dp", "seq")),
        P(("dp", "seq"), None),
        P(("dp", "seq"), None),
        P(("dp", "seq")),
        P(("dp", "seq")),
        P(("dp", "seq"), None),
        P("dp", "seq", None),
    )
    return jax.shard_map(
        local,
        mesh=mesh,
        in_specs=placed,
        out_specs=(
            P("dp", "seq", None),
            P("dp", "seq", None),
            P(),
            P(("dp", "seq"), None),
            P(None, ("dp", "seq")),
            P(("dp", "seq")),
            P(("dp", "seq"), None),
            P(("dp", "seq"), None),
            P(("dp", "seq")),
            P(("dp", "seq")),
            P(("dp", "seq"), None),
        ),
        check_vma=False,
    )
```

profile of v0, /device:TPU:9, one launch (start us, length us, event | category | flops | bytes accessed | tf_op | source)
XLA Modules:
  0.0 6645.4 jit_solution(3058400123558849200)
XLA Ops:
  76.1 69.4 %all-gather.3 = bf16[32,1,128]{2,1,0:T(2,128)(2,1)S(1)} all-gather(bf16[1,1,128]{2,1,0:T(2,128)(2,1)} %bitcast.391), channel_id=1, replica_groups=mesh['dp'=8,'seq'=4] {'dp','seq'}, dimensions={0}, use_global_device_ids=true | all-gather | bytes 8448 | tf_op jit(solution)/shard_map/all_gather | solution.py:110
  231.0 92.0 %all-gather.20.cloned.1.call-done = bf16[4096,2048]{1,0:T(8,128)(2,1)} async-done(((bf16[128,2048]{1,0:T(8,128)(2,1)}), bf16[4096,2048]{1,0:T(8,128)(2,1)}) %all-gather.20.cloned.1.call-update) | async-done | bytes 16777232 | tf_op jit(solution)/shard_map/all_gather | solution.py:195
  455.3 613.3 %while.216 = (s32[]{:T(128)}, f32[1,16,4096]{2,1,0:T(8,128)S(1)}, f32[1,16,4096]{2,1,0:T(8,128)S(1)}, f32[16,1,16,4096]{3,2,1,0:T(8,128)}, f32[16,1,16,4096]{3,2...) while((s32[]{:T(128)}, f32[1,16,4096]{2,1,0:T(8,128)S(1)}, ...), condition=%wide.region_7.8_spmd, body=%wide.region_4.7_spmd.sunk | while | flops 458772 | bytes 5344502 | solution.py:187
  1129.2 638.9 %while.220 = (s32[]{:T(128)}, f32[1,16,4096]{2,1,0:T(8,128)S(1)}, f32[256,1,1]{0,2,1:T(1,128)S(1)}, f32[256,1,4096]{2,0,1:T(8,128)}, f32[256,1,16]{2,1,0:T(1,128...) while((s32[]{:T(128)}, f32[1,16,4096]{2,1,0:T(8,128)S(1)}, ...), condition=%wide.region_9.10_spmd.clone, body=%wide.region_8.9_spmd.clone.sunk | while | flops 458772 | bytes 623123 | solution.py:207
  1820.9 2239.7 %while.219 = (s32[]{:T(128)}, f32[1,16,4096]{2,1,0:T(8,128)S(1)}, f32[16,16,1,4096]{3,1,2,0:T(8,128)}, f32[16,16,1,4096]{3,1,2,0:T(8,128)}, f32[16,16,1,16]{3,1,...) while((s32[]{:T(128)}, f32[1,16,4096]{2,1,0:T(8,128)S(1)}, ...), condition=%wide.region_25.26_spmd, body=%wide.region_14.25_spmd.sunk | while | flops 1757224 | bytes 8389971 | solution.py:225
  1889.8 68.5 %while.225 = (s32[]{:T(128)}, f32[1,16,4096]{2,1,0:T(8,128)S(1)}, f32[16,1,4096]{2,1,0:T(1,128)S(1)}, f32[16,1,4096]{2,1,0:T(1,128)S(1)}, f32[16,1,16]{2,1,0:T(1...) while((s32[]{:T(128)}, f32[1,16,4096]{2,1,0:T(8,128)S(1)}, ...), condition=%wide.region_24.24_spmd, body=%wide.region_18.23_spmd.sunk | while | flops 1040387 | bytes 1560557 | solution.py:67
  2029.8 68.5 %while.225 = (s32[]{:T(128)}, f32[1,16,4096]{2,1,0:T(8,128)S(1)}, f32[16,1,4096]{2,1,0:T(1,128)S(1)}, f32[16,1,4096]{2,1,0:T(1,128)S(1)}, f32[16,1,16]{2,1,0:T(1...) while((s32[]{:T(128)}, f32[1,16,4096]{2,1,0:T(8,128)S(1)}, ...), condition=%wide.region_24.24_spmd, body=%wide.region_18.23_spmd.sunk | while | flops 1040387 | bytes 1560557 | solution.py:67
  2169.8 68.5 %while.225 = (s32[]{:T(128)}, f32[1,16,4096]{2,1,0:T(8,128)S(1)}, f32[16,1,4096]{2,1,0:T(1,128)S(1)}, f32[16,1,4096]{2,1,0:T(1,128)S(1)}, f32[16,1,16]{2,1,0:T(1...) while((s32[]{:T(128)}, f32[1,16,4096]{2,1,0:T(8,128)S(1)}, ...), condition=%wide.region_24.24_spmd, body=%wide.region_18.23_spmd.sunk | while | flops 1040387 | bytes 1560557 | solution.py:67
  2309.8 68.5 %while.225 = (s32[]{:T(128)}, f32[1,16,4096]{2,1,0:T(8,128)S(1)}, f32[16,1,4096]{2,1,0:T(1,128)S(1)}, f32[16,1,4096]{2,1,0:T(1,128)S(1)}, f32[16,1,16]{2,1,0:T(1...) while((s32[]{:T(128)}, f32[1,16,4096]{2,1,0:T(8,128)S(1)}, ...), condition=%wide.region_24.24_spmd, body=%wide.region_18.23_spmd.sunk | while | flops 1040387 | bytes 1560557 | solution.py:67
  2449.8 68.5 %while.225 = (s32[]{:T(128)}, f32[1,16,4096]{2,1,0:T(8,128)S(1)}, f32[16,1,4096]{2,1,0:T(1,128)S(1)}, f32[16,1,4096]{2,1,0:T(1,128)S(1)}, f32[16,1,16]{2,1,0:T(1...) while((s32[]{:T(128)}, f32[1,16,4096]{2,1,0:T(8,128)S(1)}, ...), condition=%wide.region_24.24_spmd, body=%wide.region_18.23_spmd.sunk | while | flops 1040387 | bytes 1560557 | solution.py:67
  2589.8 68.5 %while.225 = (s32[]{:T(128)}, f32[1,16,4096]{2,1,0:T(8,128)S(1)}, f32[16,1,4096]{2,1,0:T(1,128)S(1)}, f32[16,1,4096]{2,1,0:T(1,128)S(1)}, f32[16,1,16]{2,1,0:T(1...) while((s32[]{:T(128)}, f32[1,16,4096]{2,1,0:T(8,128)S(1)}, ...), condition=%wide.region_24.24_spmd, body=%wide.region_18.23_spmd.sunk | while | flops 1040387 | bytes 1560557 | solution.py:67
  2729.7 68.5 %while.225 = (s32[]{:T(128)}, f32[1,16,4096]{2,1,0:T(8,128)S(1)}, f32[16,1,4096]{2,1,0:T(1,128)S(1)}, f32[16,1,4096]{2,1,0:T(1,128)S(1)}, f32[16,1,16]{2,1,0:T(1...) while((s32[]{:T(128)}, f32[1,16,4096]{2,1,0:T(8,128)S(1)}, ...), condition=%wide.region_24.24_spmd, body=%wide.region_18.23_spmd.sunk | while | flops 1040387 | bytes 1560557 | solution.py:67
  2869.7 68.5 %while.225 = (s32[]{:T(128)}, f32[1,16,4096]{2,1,0:T(8,128)S(1)}, f32[16,1,4096]{2,1,0:T(1,128)S(1)}, f32[16,1,4096]{2,1,0:T(1,128)S(1)}, f32[16,1,16]{2,1,0:T(1...) while((s32[]{:T(128)}, f32[1,16,4096]{2,1,0:T(8,128)S(1)}, ...), condition=%wide.region_24.24_spmd, body=%wide.region_18.23_spmd.sunk | while | flops 1040387 | bytes 1560557 | solution.py:67
  3009.6 68.5 %while.225 = (s32[]{:T(128)}, f32[1,16,4096]{2,1,0:T(8,128)S(1)}, f32[16,1,4096]{2,1,0:T(1,128)S(1)}, f32[16,1,4096]{2,1,0:T(1,128)S(1)}, f32[16,1,16]{2,1,0:T(1...) while((s32[]{:T(128)}, f32[1,16,4096]{2,1,0:T(8,128)S(1)}, ...), condition=%wide.region_24.24_spmd, body=%wide.region_18.23_spmd.sunk | while | flops 1040387 | bytes 1560557 | solution.py:67
  3149.6 68.5 %while.225 = (s32[]{:T(128)}, f32[1,16,4096]{2,1,0:T(8,128)S(1)}, f32[16,1,4096]{2,1,0:T(1,128)S(1)}, f32[16,1,4096]{2,1,0:T(1,128)S(1)}, f32[16,1,16]{2,1,0:T(1...) while((s32[]{:T(128)}, f32[1,16,4096]{2,1,0:T(8,128)S(1)}, ...), condition=%wide.region_24.24_spmd, body=%wide.region_18.23_spmd.sunk | while | flops 1040387 | bytes 1560557 | solution.py:67
  3289.6 68.5 %while.225 = (s32[]{:T(128)}, f32[1,16,4096]{2,1,0:T(8,128)S(1)}, f32[16,1,4096]{2,1,0:T(1,128)S(1)}, f32[16,1,4096]{2,1,0:T(1,128)S(1)}, f32[16,1,16]{2,1,0:T(1...) while((s32[]{:T(128)}, f32[1,16,4096]{2,1,0:T(8,128)S(1)}, ...), condition=%wide.region_24.24_spmd, body=%wide.region_18.23_spmd.sunk | while | flops 1040387 | bytes 1560557 | solution.py:67
  3429.6 68.5 %while.225 = (s32[]{:T(128)}, f32[1,16,4096]{2,1,0:T(8,128)S(1)}, f32[16,1,4096]{2,1,0:T(1,128)S(1)}, f32[16,1,4096]{2,1,0:T(1,128)S(1)}, f32[16,1,16]{2,1,0:T(1...) while((s32[]{:T(128)}, f32[1,16,4096]{2,1,0:T(8,128)S(1)}, ...), condition=%wide.region_24.24_spmd, body=%wide.region_18.23_spmd.sunk | while | flops 1040387 | bytes 1560557 | solution.py:67
  3569.5 68.5 %while.225 = (s32[]{:T(128)}, f32[1,16,4096]{2,1,0:T(8,128)S(1)}, f32[16,1,4096]{2,1,0:T(1,128)S(1)}, f32[16,1,4096]{2,1,0:T(1,128)S(1)}, f32[16,1,16]{2,1,0:T(1...) while((s32[]{:T(128)}, f32[1,16,4096]{2,1,0:T(8,128)S(1)}, ...), condition=%wide.region_24.24_spmd, body=%wide.region_18.23_spmd.sunk | while | flops 1040387 | bytes 1560557 | solution.py:67
  3849.5 68.5 %while.225 = (s32[]{:T(128)}, f32[1,16,4096]{2,1,0:T(8,128)S(1)}, f32[16,1,4096]{2,1,0:T(1,128)S(1)}, f32[16,1,4096]{2,1,0:T(1,128)S(1)}, f32[16,1,16]{2,1,0:T(1...) while((s32[]{:T(128)}, f32[1,16,4096]{2,1,0:T(8,128)S(1)}, ...), condition=%wide.region_24.24_spmd, body=%wide.region_18.23_spmd.sunk | while | flops 1040387 | bytes 1560557 | solution.py:67
  3989.5 68.5 %while.225 = (s32[]{:T(128)}, f32[1,16,4096]{2,1,0:T(8,128)S(1)}, f32[16,1,4096]{2,1,0:T(1,128)S(1)}, f32[16,1,4096]{2,1,0:T(1,128)S(1)}, f32[16,1,16]{2,1,0:T(1...) while((s32[]{:T(128)}, f32[1,16,4096]{2,1,0:T(8,128)S(1)}, ...), condition=%wide.region_24.24_spmd, body=%wide.region_18.23_spmd.sunk | while | flops 1040387 | bytes 1560557 | solution.py:67
  4241.0 125.7 %reduce-scatter.12.cloned.1.call-done = f32[128,128]{1,0:T(8,128)} async-done(((f32[4096,128]{1,0:T(8,128)}), f32[128,128]{1,0:T(8,128)}) %reduce-scatter.12.cloned.1.call-update) | async-done | bytes 65552 | tf_op jit(solution)/shard_map/reduce_scatter | solution.py:310
  4366.8 141.3 %reduce-scatter.10.cloned.1.call-done = f32[128,160]{0,1:T(8,128)} async-done(((f32[4096,160]{0,1:T(8,128)}), f32[128,160]{0,1:T(8,128)}) %reduce-scatter.10.cloned.1.call-update) | async-done | bytes 81936 | tf_op jit(solution)/shard_map/reduce_scatter | solution.py:309
  4508.0 716.1 %reduce-scatter.14.cloned.1.call-done = f32[128,2048]{1,0:T(8,128)} async-done(((f32[4096,2048]{1,0:T(8,128)}), f32[128,2048]{1,0:T(8,128)}) %reduce-scatter.14.cloned.1.call-update) | async-done | bytes 1048592 | tf_op jit(solution)/shard_map/reduce_scatter | solution.py:242
  5224.2 1414.0 %reduce-scatter.8.cloned.1.call-done = f32[256,2048]{1,0:T(8,128)} async-done(((f32[8192,2048]{1,0:T(8,128)}), f32[256,2048]{1,0:T(8,128)}) %reduce-scatter.8.cloned.1.call-update) | async-done | bytes 2097168 | tf_op jit(solution)/shard_map/reduce_scatter | solution.py:282
  (7953 shorter events, 5672.9 us)
Async XLA Ops:
  7.2 200.1 %all-gather.14.cloned.1.call-start = ((), (), s32[]{:S(2)}) async-start(), calls=%async_computation.5 | async-start | bytes 34603008 | tf_op jit(solution)/shard_map/all_gather | solution.py:133
  7.9 315.1 %all-gather.20.cloned.1.call-start = ((), (), s32[]{:S(2)}) async-start(), calls=%async_computation.8 | async-start | bytes 17301504 | tf_op jit(solution)/shard_map/all_gather | solution.py:195
  8.7 366.2 %all-gather.16.cloned.1.call-start = ((), (), s32[]{:S(2)}) async-start(), calls=%async_computation.6 | async-start | bytes 1351680 | tf_op jit(solution)/shard_map/all_gather | solution.py:111
  9.4 420.6 %all-gather.18.cloned.1.call-start = ((), (), s32[]{:S(2)}) async-start(), calls=%async_computation.7 | async-start | bytes 1081344 | tf_op jit(solution)/shard_map/all_gather | solution.py:112
  10.0 1759.0 %all-gather.22.cloned.1.call-start = ((), (), s32[]{:S(2)}) async-start(), calls=%async_computation.13 | async-start | bytes 1310720 | tf_op jit(solution)/shard_map/all_gather | solution.py:25
  11.6 1117.3 %copy-start.31 = (s32[256]{0:T(256)}, s32[256]{0:T(256)S(1)}, u32[]{:S(2)}) copy-start(s32[256]{0:T(256)S(1)} %fusion.95) | copy-start | bytes 3076
  11.6 321.6 %copy-start.37 = (pred[256]{0:T(512)(128)(4,1)}, pred[256]{0:T(512)(128)(4,1)S(1)}, u32[]{:S(2)}) copy-start(pred[256]{0:T(512)(128)(4,1)S(1)} %get-tuple-element.1753) | copy-start | bytes 772
  11.7 321.6 %copy-start.39 = (pred[256]{0:T(512)(128)(4,1)}, pred[256]{0:T(512)(128)(4,1)S(1)}, u32[]{:S(2)}) copy-start(pred[256]{0:T(512)(128)(4,1)S(1)} %get-tuple-element.1755) | copy-start | bytes 772
  11.7 321.6 %copy-start.41 = (pred[256]{0:T(512)(128)(4,1)}, pred[256]{0:T(512)(128)(4,1)S(1)}, u32[]{:S(2)}) copy-start(pred[256]{0:T(512)(128)(4,1)S(1)} %get-tuple-element.1756) | copy-start | bytes 772
  11.7 321.6 %copy-start.47 = (pred[256]{0:T(512)(128)(4,1)}, pred[256]{0:T(512)(128)(4,1)S(1)}, u32[]{:S(2)}) copy-start(pred[256]{0:T(512)(128)(4,1)S(1)} %get-tuple-element.1754) | copy-start | bytes 772
  13.9 210.9 %copy-start.34 = (f32[256]{0:T(256)}, f32[256]{0:T(256)S(1)}, u32[]{:S(2)}) copy-start(f32[256]{0:T(256)S(1)} %get-tuple-element.1752) | copy-start | bytes 3076
  76.0 257.3 %copy-start.15 = (f32[1,4096]{1,0:T(1,128)}, f32[1,4096]{1,0:T(1,128)S(1)}, u32[]{:S(2)}) copy-start(f32[1,4096]{1,0:T(1,128)S(1)} %get-tuple-element.1744) | copy-start | bytes 49156
  76.0 257.3 %copy-start.17 = (f32[1,4096]{1,0:T(1,128)}, f32[1,4096]{1,0:T(1,128)S(1)}, u32[]{:S(2)}) copy-start(f32[1,4096]{1,0:T(1,128)S(1)} %get-tuple-element.1745) | copy-start | bytes 49156
  76.0 257.3 %copy-start.19 = (f32[1,4096]{1,0:T(1,128)}, f32[1,4096]{1,0:T(1,128)S(1)}, u32[]{:S(2)}) copy-start(f32[1,4096]{1,0:T(1,128)S(1)} %get-tuple-element.1746) | copy-start | bytes 49156
  228.0 105.2 %collective-permute-start = (bf16[1,3,4096]{2,1,0:T(4,128)(2,1)S(1)}, bf16[1,3,4096]{2,1,0:T(4,128)(2,1)S(1)}, u32[]{:S(2)}, u32[]{:S(2)}) collective-permute-start(bf16[1,3,4096]{2,1,0:T(4,128)(2,1)S(1)} %slice.82), channel_id=1, source_target_pairs={{0,1},{1,2},{2,3},{4,5},{5,6},{6,7},{8,9},{9,10},{10,11},{12,13},{... | collective-permute-start | bytes 73736 | tf_op jit(solution)/shard_map/ppermute | solution.py:20
  455.2 614.2 %copy-start.48 = (bf16[128]{0:T(256)(128)(2,1)S(1)}, bf16[128]{0:T(256)(128)(2,1)}, u32[]{:S(2)}) copy-start(bf16[128]{0:T(256)(128)(2,1)} %param.37) | copy-start | bytes 772
  1069.3 699.7 %all-gather.26.cloned.1.call-start = ((), (), s32[]{:S(2)}) async-start(), calls=%async_computation.15 | async-start | bytes 1310720 | tf_op jit(solution)/shard_map/all_gather | solution.py:25
  1129.2 672.2 %all-gather.24.cloned.1.call-start = ((), (), s32[]{:S(2)}) async-start(), calls=%async_computation.14 | async-start | bytes 1310720 | tf_op jit(solution)/shard_map/all_gather | solution.py:25
  1769.0 2470.6 %reduce-scatter.16.cloned.1.call-start = ((), (), s32[]{:S(2)}) async-start(), calls=%async_computation.16 | async-start | bytes 2162688
  4097.3 269.5 %reduce-scatter.12.cloned.1.call-start = ((), (), s32[]{:S(2)}) async-start(), calls=%async_computation.11 | async-start | bytes 2162688 | tf_op jit(solution)/shard_map/reduce_scatter | solution.py:310
  4101.2 406.8 %reduce-scatter.10.cloned.1.call-start = ((), (), s32[]{:S(2)}) async-start(), calls=%async_computation.10 | async-start | bytes 2703360 | tf_op jit(solution)/shard_map/reduce_scatter | solution.py:309
  4103.3 1120.8 %reduce-scatter.14.cloned.1.call-start = ((), (), s32[]{:S(2)}) async-start(), calls=%async_computation.12 | async-start | bytes 34603008 | tf_op jit(solution)/shard_map/reduce_scatter | solution.py:242
  4118.2 2519.9 %reduce-scatter.8.cloned.1.call-start = ((), (), s32[]{:S(2)}) async-start(), calls=%async_computation.9 | async-start | bytes 69206016 | tf_op jit(solution)/shard_map/reduce_scatter | solution.py:282
  4120.0 4.8 collective-permute-start.1
  (41 other events, 1312.5 us)
Sparse Core Ops, SparseCore 0:
  10.9 195.1 all-gather.13
  209.1 113.8 all-gather.19
  325.9 48.8 all-gather.15
  377.7 52.3 all-gather.17
  1069.4 27.0 all-gather.21
  1129.3 32.2 all-gather.25
  1769.1 32.2 all-gather.23
  4097.4 130.5 reduce-scatter.15
  4230.8 135.8 reduce-scatter.11
  4369.5 138.5 reduce-scatter.9
  4510.9 713.2 reduce-scatter.13
  5227.0 1411.1 reduce-scatter.7
where the time goes:
time: 6740 us; the launch traced here: 6650 us
  waiting for transfers between devices  2600 us (39%)
  local copies, waits for them, and re-layouts  2070 us (31%)
  other arithmetic  1510 us (22%)
  blocking collectives  293 us (4%)
  matrix products  126 us (2%)
    reduce_scatter x1, waiting for transfers between devices, local(): lax.psum_scatter(contract_rows(part_cols, normed), ('dp', 'seq'), scatter...  1410 us
    reduce_scatter x1, waiting for transfers between devices, local(): lax.psum_scatter(contract_rows(part_cols, cot_low), ('dp', 'seq'), scatte...  716 us
    reduce_sum x256, other arithmetic, decay_of(): step_t[:, None, :] * (key_t * key_t)[:, :, None]  561 us
    dynamic_slice x768, local copies, waits for them, and re-layouts, run_block(): lax.scan(advance_one, state_in, (step_b, inject_b, key_b, query_b, keep_b))  518 us
    dynamic_slice x1280, local copies, waits for them, and re-layouts, chain_block(): lax.scan(chain_step, carried, (step_b, inject_b, key_b, keep_b))  506 us
    dynamic_slice x512, local copies, waits for them, and re-layouts, local(): lax.scan(pull_step, zero_state, (step_seq, key_seq, query_seq, keep_seq,...  424 us
    dynamic_update_slice x256, other arithmetic, local(): lax.scan(chain_block, (zero_state, unit_state), block_inputs)  417 us
    dynamic_update_slice x1024, local copies, waits for them, and re-layouts, run_block(): lax.scan(advance_one, state_in, (step_b, inject_b, key_b, query_b, keep_b))  369 us

commit v1 on v0

v1 whole, which is shorter than its diff:
```python
import functools
import math

import jax
import jax.numpy as jnp
from jax import lax
from jax.experimental import pallas as pl
from jax.experimental.pallas import tpu as pltpu
from jax.sharding import PartitionSpec as P

N = 16
R = 128
KCONV = 4
CHUNK = 16
LANES = 128

norm_eps = 1e-05
BF = jnp.bfloat16
F32 = jnp.float32


def silu_slope(pre_value):
    sigmoid_of = jax.nn.sigmoid(pre_value)
    return sigmoid_of * (1.0 + pre_value * (1.0 - sigmoid_of))


def token_begins(lengths, position_count):
    doc_ends = jnp.cumsum(lengths, axis=1)
    doc_starts = doc_ends - lengths
    places = jnp.arange(position_count, dtype=jnp.int32)
    inside = doc_starts[:, None, :] <= places[None, :, None]
    return (jnp.max(jnp.where(inside, doc_starts[:, None, :], 0), axis=2), places)


def mm(left, right, dims):
    return lax.dot_general(left, right, (dims, ((), ())), preferred_element_type=F32)


NN = ((1,), (0,))
NT = ((1,), (1,))
TN = ((0,), (0,))


def row(ref, i, lane):
    return jnp.broadcast_to(ref[i : i + 1, pl.ds(lane, LANES)], (8, LANES))


def lane_groups(channels):
    group = math.gcd(channels, 512)
    return [(g, group) for g in range(0, channels, group)]


def scan_forward(step_ref, inj_ref, key_ref, ksq_ref, keep_ref, wq_ref, s_ref, y_ref, carry):
    @pl.when(pl.program_id(1) == 0)
    def _():
        carry[...] = jnp.zeros_like(carry)

    tokens, channels = step_ref.shape
    for first, group in lane_groups(channels):
        tiles = list(range(first, first + group, LANES))

        def chunk(k, state):
            base = pl.multiple_of(k * CHUNK, CHUNK)
            state = list(state)
            steps, injs, keeps = (r.at[pl.ds(base, CHUNK)] for r in (step_ref, inj_ref, keep_ref))
            for i in range(CHUNK):
                at = base + i
                keep = row(keeps, i, 0)
                key = [key_ref[at, 0:8, :], key_ref[at, 8:16, :]]
                ksq = [ksq_ref[at, 0:8, :], ksq_ref[at, 8:16, :]]
                for j, lane in enumerate(tiles):
                    step = row(steps, i, lane)
                    inj = row(injs, i, lane)
                    for h in range(2):
                        state[2 * j + h] = (keep - step * ksq[h]) * state[2 * j + h] + inj * key[h]
                    both = jnp.concatenate([state[2 * j], state[2 * j + 1]], axis=0)
                    s_ref[pl.ds(pl.multiple_of(at * N, N), N), pl.ds(lane, LANES)] = both.astype(BF)
            rows = pl.ds(pl.multiple_of(k * CHUNK * N, CHUNK * N), CHUNK * N)
            y_ref[pl.ds(base, CHUNK), pl.ds(first, group)] = mm(
                wq_ref[pl.ds(base, CHUNK), :], s_ref[rows, pl.ds(first, group)], NN
            )
            return tuple(state)

        start = []
        for lane in tiles:
            start += [carry[0:8, pl.ds(lane, LANES)], carry[8:16, pl.ds(lane, LANES)]]
        end = lax.fori_loop(0, tokens // CHUNK, chunk, tuple(start))
        for j, lane in enumerate(tiles):
            carry[0:8, pl.ds(lane, LANES)] = end[2 * j]
            carry[8:16, pl.ds(lane, LANES)] = end[2 * j + 1]


def scan_backward(
    step_ref, inj_ref, dy_ref, ksq_ref, query_ref, keep_ref, wk_ref, wk2_ref, s_ref, before_ref,
    dinj_ref, pull_ref, dq_ref, dk1_ref, dk2_ref, carry, g_buf, sg_buf,
):
    @pl.when(pl.program_id(1) == 0)
    def _():
        carry[...] = jnp.zeros_like(carry)

    tokens, channels = step_ref.shape
    chunks = tokens // CHUNK
    span = CHUNK * N
    pick = lax.broadcasted_iota(jnp.int32, (CHUNK, span), 0) == (
        lax.broadcasted_iota(jnp.int32, (CHUNK, span), 1) // N
    )

    def diagonal(left, right):
        return jnp.sum(jnp.where(pick, mm(left.astype(BF), right, NT), 0.0), axis=0, keepdims=True)

    for first, group in lane_groups(channels):
        tiles = list(range(first, first + group, LANES))
        cols = pl.ds(first, group)

        def chunk(turn, pulled):
            k = chunks - 1 - turn
            base = pl.multiple_of(k * CHUNK, CHUNK)
            pulled = list(pulled)
            steps, dys, keeps = (r.at[pl.ds(base, CHUNK)] for r in (step_ref, dy_ref, keep_ref))
            for i in reversed(range(CHUNK)):
                at = base + i
                keep = row(keeps, i, 0)
                ksq = [ksq_ref[at, 0:8, :], ksq_ref[at, 8:16, :]]
                query = [query_ref[at, 0:8, :], query_ref[at, 8:16, :]]
                for j, lane in enumerate(tiles):
                    step = row(steps, i, lane)
                    dy = row(dys, i, lane)
                    here = []
                    for h in range(2):
                        grad = pulled[2 * j + h] + dy * query[h]
                        pulled[2 * j + h] = (keep - step * ksq[h]) * grad
                        here.append(grad)
                    g_buf[i * N : (i + 1) * N, pl.ds(lane, LANES)] = jnp.concatenate(here, axis=0).astype(BF)
            low = pl.multiple_of(k * span, span)
            now = s_ref[pl.ds(low, span), cols]
            grads = g_buf[:, cols]
            sg_buf[N:span, cols] = g_buf[N:span, cols] * s_ref[pl.ds(low, span - N), cols]

            @pl.when(k == 0)
            def _():
                sg_buf[0:N, cols] = g_buf[0:N, cols] * before_ref[:, cols]

            @pl.when(k > 0)
            def _():
                prior = s_ref[pl.ds(pl.multiple_of(jnp.maximum(low - N, 0), N), N), cols]
                sg_buf[0:N, cols] = g_buf[0:N, cols] * prior

            prods = sg_buf[:, cols]
            here = pl.ds(base, CHUNK)
            dinj_ref[here, cols] = mm(wk_ref[here, :], grads, NN)
            pull_ref[here, cols] = mm(wk2_ref[here, :], prods, NN)
            dq = diagonal(dy_ref[here, cols], now)
            dk1 = diagonal(inj_ref[here, cols], grads)
            dk2 = diagonal(step_ref[here, cols], prods)
            one = pl.ds(k, 1)
            if first == 0:
                dq_ref[one, :] = dq
                dk1_ref[one, :] = dk1
                dk2_ref[one, :] = dk2
            else:
                dq_ref[one, :] += dq
                dk1_ref[one, :] += dk1
                dk2_ref[one, :] += dk2
            return tuple(pulled)

        start = []
        for lane in tiles:
            start += [carry[0:8, pl.ds(lane, LANES)], carry[8:16, pl.ds(lane, LANES)]]
        end = lax.fori_loop(0, chunks, chunk, tuple(start))
        for j, lane in enumerate(tiles):
            carry[0:8, pl.ds(lane, LANES)] = end[2 * j]
            carry[8:16, pl.ds(lane, LANES)] = end[2 * j + 1]


def run_forward(seqs, length, step, inj, key_lanes, ksq_lanes, keep_lanes, wq):
    channels = step.shape[1]
    block = math.gcd(length, 128)
    blocks = length // block

    def at(b, t):
        return (b * blocks + t, 0)

    def at3(b, t):
        return (b * blocks + t, 0, 0)

    tokens = seqs * length
    return pl.pallas_call(
        scan_forward,
        grid=(seqs, blocks),
        in_specs=[
            pl.BlockSpec((block, channels), at),
            pl.BlockSpec((block, channels), at),
            pl.BlockSpec((block, N, LANES), at3),
            pl.BlockSpec((block, N, LANES), at3),
            pl.BlockSpec((block, LANES), at),
            pl.BlockSpec((block, CHUNK * N), at),
        ],
        out_specs=[
            pl.BlockSpec((block * N, channels), at),
            pl.BlockSpec((block, channels), at),
        ],
        out_shape=[
            jax.ShapeDtypeStruct((tokens * N, channels), BF),
            jax.ShapeDtypeStruct((tokens, channels), F32),
        ],
        scratch_shapes=[pltpu.VMEM((N, channels), F32)],
        cost_estimate=pl.CostEstimate(
            flops=tokens * channels * N * 40, bytes_accessed=tokens * channels * 44, transcendentals=0
        ),
        compiler_params=pltpu.CompilerParams(vmem_limit_bytes=48 << 20),
        name="scan_forward",
    )(step, inj, key_lanes, ksq_lanes, keep_lanes, wq)


def run_backward(seqs, length, step, inj, dy, ksq_lanes, query_lanes, keep_lanes, wk, wk2, states):
    channels = step.shape[1]
    block = math.gcd(length, 128)
    blocks = length // block

    def at(b, t):
        return (b * blocks + blocks - 1 - t, 0)

    def at3(b, t):
        return (b * blocks + blocks - 1 - t, 0, 0)

    def prior(b, t):
        return (jnp.maximum((b * blocks + blocks - 1 - t) * block - 1, 0), 0)

    tokens = seqs * length
    span = CHUNK * N
    rows = pl.BlockSpec((block, channels), at)
    lanes = pl.BlockSpec((block, N, LANES), at3)
    weights = pl.BlockSpec((block, span), at)
    small = pl.BlockSpec((block // CHUNK, span), at)
    return pl.pallas_call(
        scan_backward,
        grid=(seqs, blocks),
        in_specs=[
            rows, rows, rows, lanes, lanes, pl.BlockSpec((block, LANES), at), weights, weights,
            pl.BlockSpec((block * N, channels), at), pl.BlockSpec((N, channels), prior),
        ],
        out_specs=[rows, rows, small, small, small],
        out_shape=[jax.ShapeDtypeStruct((tokens, channels), F32)] * 2
        + [jax.ShapeDtypeStruct((tokens // CHUNK, span), F32)] * 3,
        scratch_shapes=[
            pltpu.VMEM((N, channels), F32),
            pltpu.VMEM((span, channels), BF),
            pltpu.VMEM((span, channels), BF),
        ],
        cost_estimate=pl.CostEstimate(
            flops=tokens * channels * N * 100, bytes_accessed=tokens * channels * 56, transcendentals=0
        ),
        compiler_params=pltpu.CompilerParams(vmem_limit_bytes=56 << 20),
        name="scan_backward",
    )(step, inj, dy, ksq_lanes, query_lanes, keep_lanes, wk, wk2, states, states)


def regroup(dp, seq):
    half = seq // 2
    forth = [
        (d * seq + s, (2 * (d // 2) + s % 2) * seq + half * (d % 2) + s // 2)
        for d in range(dp)
        for s in range(seq)
    ]
    return forth, [(b, a) for a, b in forth]


def local(
    hidden_in,
    doc_lengths,
    norm_gain,
    in_weight,
    conv_weight,
    conv_bias,
    x_weight,
    dt_weight,
    dt_bias,
    skip_gain,
    out_weight,
    out_cotangent,
):
    seqs, part_len, width = hidden_in.shape
    both = ("dp", "seq")
    dp, seq = lax.axis_size("dp"), lax.axis_size("seq")
    length = part_len * seq
    tokens = seqs * length
    forth, back = regroup(dp, seq)
    rows = out_weight.shape[0]
    channels = rows * dp
    lag_max = KCONV - 1

    small = jnp.concatenate(
        [x_weight, dt_weight, conv_weight.T, conv_bias[:, None], dt_bias[:, None], skip_gain[:, None]], axis=1
    )
    used = small.shape[1]
    padded_cols = -(-used // LANES) * LANES
    packed = jnp.concatenate([out_weight, jnp.pad(small, ((0, 0), (0, padded_cols - used)))], axis=1)

    hidden = lax.all_gather(hidden_in, "seq", axis=1, tiled=True).reshape(tokens, width)
    w_in = lax.all_gather(in_weight, "dp", axis=0, tiled=True)
    packed = lax.all_gather(lax.ppermute(packed, both, forth), "dp", axis=0, tiled=True)
    cot = lax.all_gather(out_cotangent, "seq", axis=1, tiled=True).reshape(tokens, width)

    w_out = packed[:, :width]
    tail = packed[:, width:]
    w_x = tail[:, : R + 2 * N]
    w_dt = tail[:, R + 2 * N : 2 * R + 2 * N]
    vectors = tail[:, 2 * R + 2 * N : used].astype(F32).T
    taps, conv_shift, rate_shift, skip = vectors[:KCONV], vectors[KCONV], vectors[KCONV + 1], vectors[KCONV + 2]

    begins, places = token_begins(doc_lengths, length)
    keep = (places[None, :] != begins).astype(F32).reshape(tokens, 1)
    valid = [(places[None, :] - (lag_max - w) >= begins)[:, :, None] for w in range(KCONV)]

    gain = norm_gain.astype(F32)
    x_full = hidden.astype(F32)
    inv_rms = lax.rsqrt(jnp.mean(x_full * x_full, axis=1, keepdims=True) + norm_eps)
    normed = (x_full * inv_rms * gain).astype(BF)
    pre = mm(normed, w_in, NT).astype(BF)
    x_inner = pre[:, :channels].reshape(seqs, length, channels)
    z_inner = pre[:, channels:].astype(F32)

    padded = jnp.pad(x_inner, ((0, 0), (lag_max, 0), (0, 0)))
    conv_sum = jnp.broadcast_to(conv_shift, (seqs, length, channels))
    for w in range(KCONV):
        window = padded[:, w : w + length, :].astype(F32)
        conv_sum = conv_sum + jnp.where(valid[w], window * taps[w], 0.0)
    conv_flat = conv_sum.reshape(tokens, channels)
    xc_low = jax.nn.silu(conv_flat).astype(BF)
    xc = xc_low.astype(F32)
    proj = lax.psum(mm(xc_low, w_x, NN), "seq")
    rate = proj[:, :R].astype(BF)
    key = proj[:, R : R + N]
    query = proj[:, R + N :]
    beta = jax.nn.sigmoid(mm(rate, w_dt, NT) + rate_shift)
    den = 1.0 + beta * jnp.sum(key * key, axis=1, keepdims=True)
    step = beta / den
    inj = step * xc

    def lanes(values):
        return jnp.broadcast_to(values[:, :, None], (tokens, N, LANES))

    ksq = keep * key * key
    key_lanes, ksq_lanes, query_lanes = lanes(key), lanes(ksq), lanes(query)
    keep_lanes = jnp.broadcast_to(keep, (tokens, LANES))
    eye = (jnp.arange(tokens)[:, None] % CHUNK == jnp.arange(CHUNK)[None, :]).astype(F32)

    def spread(values):
        return (values[:, None, :] * eye[:, :, None]).reshape(tokens, CHUNK * N).astype(BF)

    states, mixed = run_forward(seqs, length, step, inj, key_lanes, ksq_lanes, keep_lanes, spread(query))
    y_full = mixed + skip * xc

    d_gated = mm(cot, w_out, NT)
    z_gate = jax.nn.silu(z_inner)
    dy = d_gated * z_gate
    gated = (y_full * z_gate).astype(BF)
    branch = mm(gated, w_out, NN).astype(BF).reshape(seqs, length, width)
    branch = lax.psum_scatter(branch, "seq", scatter_dimension=1, tiled=True)
    output = (hidden_in.astype(F32) + branch.astype(F32)).astype(BF)

    d_inj, pull, dq, dk1, dk2 = run_backward(
        seqs, length, step, inj, dy, ksq_lanes, query_lanes, keep_lanes, spread(key), spread(ksq), states
    )
    dq, dk1, dk2 = dq.reshape(tokens, N), dk1.reshape(tokens, N), dk2.reshape(tokens, N)
    d_z = d_gated * y_full * silu_slope(z_inner)
    d_step = d_inj * xc - pull
    den_square = den * den
    d_norm = -jnp.sum(d_step * beta * beta / den_square, axis=1, keepdims=True)
    d_keys = dk1 - 2.0 * keep * key * dk2 + 2.0 * key * d_norm
    d_rate = (d_step / den_square * beta * (1.0 - beta)).astype(BF)
    d_proj = jnp.concatenate([mm(d_rate, w_dt, NN), d_keys, dq], axis=1)
    d_proj = lax.psum(d_proj, "seq").astype(BF)
    d_conv_out = mm(d_proj, w_x, NT) + step * d_inj + skip * dy
    d_conv = (d_conv_out * silu_slope(conv_flat)).reshape(seqs, length, channels)

    tap_grads = []
    d_x_inner = jnp.zeros((seqs, length, channels), F32)
    for w in range(KCONV):
        lag = lag_max - w
        window = padded[:, w : w + length, :].astype(F32)
        masked = jnp.where(valid[w], d_conv, 0.0)
        tap_grads.append(jnp.sum(masked * window, axis=(0, 1)))
        d_x_inner = d_x_inner + jnp.pad(masked, ((0, 0), (0, lag), (0, 0)))[:, lag:, :] * taps[w]
    d_pre = jnp.concatenate([d_x_inner.reshape(tokens, channels), d_z], axis=1).astype(BF)

    grad_w_out = mm(gated, cot, TN)
    vector_grads = jnp.stack(
        tap_grads
        + [
            jnp.sum(d_conv, axis=(0, 1)),
            jnp.sum(d_rate.astype(F32), axis=0),
            jnp.sum(dy * xc, axis=0),
        ],
        axis=1,
    )
    small_grads = jnp.concatenate([mm(xc_low, d_proj, TN), mm(d_rate, rate, TN), vector_grads], axis=1)
    packed_grads = jnp.concatenate([grad_w_out, jnp.pad(small_grads, ((0, 0), (0, padded_cols - used)))], axis=1)
    packed_grads = lax.psum_scatter(packed_grads.astype(BF), "dp", scatter_dimension=0, tiled=True)
    packed_grads = lax.ppermute(packed_grads, both, back).astype(F32)
    grad_out_weight = packed_grads[:, :width]
    tail = packed_grads[:, width:]

    grad_in_weight = lax.psum_scatter(mm(d_pre, normed, TN).astype(BF), "dp", scatter_dimension=0, tiled=True)
    grad_in_weight = grad_in_weight.astype(F32)
    d_normed = mm(d_pre, w_in, NN)
    gain_local = jnp.sum(d_normed * x_full * inv_rms, axis=0)
    grad_norm_gain = lax.psum(gain_local, both)
    d_normed = d_normed.astype(BF).reshape(seqs, length, width)
    d_normed = lax.psum_scatter(d_normed, "seq", scatter_dimension=1, tiled=True).astype(F32)
    own = hidden_in.astype(F32)
    own_rms = lax.rsqrt(jnp.mean(own * own, axis=2, keepdims=True) + norm_eps)
    scaled = d_normed * gain
    grad_in = (
        out_cotangent.astype(F32)
        + own_rms * scaled
        - own * (own_rms * own_rms * own_rms) * jnp.mean(own * scaled, axis=2, keepdims=True)
    ).astype(BF)

    base = 2 * R + 2 * N
    return (
        output,
        grad_in,
        grad_norm_gain,
        grad_in_weight,
        tail[:, base : base + KCONV].T,
        tail[:, base + KCONV],
        tail[:, : R + 2 * N],
        tail[:, R + 2 * N : base],
        tail[:, base + KCONV + 1],
        tail[:, base + KCONV + 2],
        grad_out_weight,
    )


def solution(mesh):
    both = ("dp", "seq")
    tokens = P("dp", "seq", None)
    matrix, vector = P(both, None), P(both)
    return jax.shard_map(
        local,
        mesh=mesh,
        in_specs=(
            tokens, P("dp", None), P(), matrix, P(None, both), vector,
            matrix, matrix, vector, vector, matrix, tokens,
        ),
        out_specs=(
            tokens, tokens, P(), matrix, P(None, both), vector,
            matrix, matrix, vector, vector, matrix,
        ),
        check_vma=False,
    )
```

time: 6740 us -> 827 us (0.12); the launches traced: 6650 us -> 818 us
  waiting for transfers between devices: 2600 us -> 407 us
  local copies, waits for them, and re-layouts: 2070 us -> 43.4 us
  other arithmetic: 1510 us -> 50.9 us
  blocking collectives: 293 us -> 89.4 us
  Pallas kernels: 0 us -> 112 us
    reduce_scatter x4, waiting for transfers between devices: 2400 us -> 180 us  [the longest x1 77 us: local(): branch = lax.psum_scatter(branch, 'seq', scatter_dimension=1, tiled=True)]
    dynamic_slice x2640 -> x0, local copies, waits for them, and re-layouts: 1500 us -> none  [the longest x768 518 us: run_block(): lax.scan(advance_one, state_in, (step_b, inject_b, key_b, query_b, keep_b))]
    reduce_sum x514 -> x4, other arithmetic: 605 us -> 19.1 us  [the longest x1 7.37 us: local(): jnp.sum(dy * xc, axis=0)]
    mul x1282 -> x2, other arithmetic: 428 us -> 0.01 us  [local(): d_keys = dk1 - 2.0 * keep * key * dk2 + 2.0 * key * d_norm]
    dynamic_update_slice x768 -> x0, other arithmetic: 425 us -> none  [the longest x256 417 us: local(): lax.scan(chain_block, (zero_state, unit_state), block_inputs)]
    dynamic_update_slice x1088 -> x0, local copies, waits for them, and re-layouts: 424 us -> none  [the longest x1024 369 us: run_block(): lax.scan(advance_one, state_in, (step_b, inject_b, key_b, query_b, keep_b))]
    all_gather x4 -> x0, blocking collectives: 251 us -> none  [the longest x1 69.4 us: local(): lax.all_gather(conv_bias, ('dp', 'seq'), axis=0, tiled=True)]
    pallas_call x0 -> x2, Pallas kernels: none -> 112 us  [the longest x1 75 us: run_backward(): pl.pallas_call(scan_backward, grid=(seqs, blocks), in_specs=[rows, rows,...]
where the time goes in v1:
time: 827 us; the launch traced here: 818 us
  waiting for transfers between devices  407 us (49%)
  Pallas kernels  112 us (14%)
  matrix products  92 us (11%)
  blocking collectives  89.4 us (11%)
  other arithmetic  50.9 us (6%)
  local copies, waits for them, and re-layouts  43.4 us (5%)
  between operations  14.7 us (2%)
  starting transfers between devices  8.62 us (1%)
    dot_general x12, matrix products, mm(): lax.dot_general(left, right, (dims, ((), ())), preferred_element_type=F32)  92 us
    reduce_scatter x1, waiting for transfers between devices, local(): branch = lax.psum_scatter(branch, 'seq', scatter_dimension=1, tiled=True)  77 us
    pallas_call x1, Pallas kernels, run_backward(): pl.pallas_call(scan_backward, grid=(seqs, blocks), in_specs=[rows, rows,...  75 us
    reduce_scatter x1, waiting for transfers between devices, local(): lax.psum_scatter(mm(d_pre, normed, TN).astype(BF), 'dp', scatter_dimensio...  71.9 us
    psum x1, blocking collectives, local(): grad_norm_gain = lax.psum(gain_local, both)  61.2 us
    all_gather x1, waiting for transfers between devices, local(): w_in = lax.all_gather(in_weight, 'dp', axis=0, tiled=True)  53.4 us
    all_gather x1, waiting for transfers between devices, local(): lax.all_gather(lax.ppermute(packed, both, forth), 'dp', axis=0, tiled=True)  41.8 us
    ppermute x1, waiting for transfers between devices, local(): lax.ppermute(packed, both, forth)  40.8 us
  transfers between devices with their start and end apart: 11, of which 10 were waited for; matrix products, arithmetic and copies ran while one was open for 12% of the time, Pallas kernels for 5%

profile of v1, /device:TPU:9, one launch (start us, length us, event | category | flops | bytes accessed | tf_op | source)
XLA Modules:
  0.0 818.1 jit_solution(1053843682400626039)
XLA Ops:
  17.2 40.8 %collective-permute-done = bf16[128,2432]{1,0:T(8,128)(2,1)S(1)} collective-permute-done((bf16[128,2432]{1,0:T(8,128)(2,1)S(1)}, bf16[128,2432]{1,0:T(8,128)(2,1)S(1)}, u32[]{:S(2)}, u32[]{:S(2)}) %collective-permute-start) | collective-permute-done | bytes 622624 | tf_op jit(solution)/shard_map/ppermute | solution.py:301
  60.0 38.7 %all-gather.7.cloned.1.call-done = bf16[1,1024,2048]{2,1,0:T(8,128)(2,1)} async-done(((bf16[1,256,2048]{2,1,0:T(8,128)(2,1)}), bf16[1,1024,2048]{2,1,0:T(8,128)(2,1)}) %all-gather.7.cloned.1.call-update) | async-done | bytes 4194320 | tf_op jit(solution)/shard_map/all_gather | solution.py:299
  101.8 41.8 %all-gather.5.cloned.1.call-done = bf16[1024,2432]{1,0:T(8,128)(2,1)} async-done(((bf16[128,2432]{1,0:T(8,128)(2,1)}), bf16[1024,2432]{1,0:T(8,128)(2,1)}) %all-gather.5.cloned.1.call-update) | async-done | bytes 4980752 | tf_op jit(solution)/shard_map/all_gather | solution.py:301
  146.5 53.4 %all-gather.9.cloned.1.call-done = bf16[2048,2048]{1,0:T(8,128)(2,1)} async-done(((bf16[256,2048]{1,0:T(8,128)(2,1)}), bf16[2048,2048]{1,0:T(8,128)(2,1)}) %all-gather.9.cloned.1.call-update) | async-done | bytes 8388624 | tf_op jit(solution)/shard_map/all_gather | solution.py:300
  199.9 12.6 %convolution_convert_fusion.1 = bf16[1024,2048]{1,0:T(8,128)(2,1)S(1)} fusion(bf16[2048,2048]{1,0:T(8,128)(2,1)} %all-gather.9.cloned.1.call-done, bf16[1,1024,2048]{2,1,0:T(8,128)(2,1)} %all-gather.7.cloned.1.call-done, f32[2048]{0:T(1024)S(1)} %convert_element_type.143, f32[1024]{0:T(1024)S(1)} %add_rsqrt_fusion), kind=kOutput, calls=%fused_computation.84 | convolution fusion | flops 8600420352 | bytes 16789504 | tf_op jit(solution)/shard_map/dot_general | solution.py:36
  222.8 38.0 %all-reduce.9.cloned.1.call-done = f32[1024,160]{0,1:T(8,128)} async-done(((f32[1024,160]{0,1:T(8,128)}), f32[1024,160]{0,1:T(8,128)}) %all-reduce.9.cloned.1.call-update) | async-done | bytes 655376 | tf_op jit(solution)/shard_map/psum | solution.py:331
  269.6 8.1 convert_multiply_fusion.6
  289.7 37.0 %scan_forward.1 = (bf16[16384,1024]{1,0:T(8,128)(2,1)}, f32[1024,1024]{1,0:T(8,128)S(1)}) custom-call(f32[1024,1024]{1,0:T(8,128)} %get-tuple-element.96.step_ref, f32[1024,1024]{1,0:T(8,128)} %get-tuple-element.95.inj_ref, f32[1024,16,128]{2,1,0:T(8,128)} %broadcast_in_dim.137.key_ref, f32[1024,16,128]{2,1,0:T(8,128)} %broadcast_in_dim.138.ksq_ref, ...), custom_call_target="tpu_custom_call" | custom-call | flops 671088640 | bytes 46137344 | tf_op jit(solution)/shard_map/scan_forward/pallas_call | solution.py:187
  328.8 12.3 %all-gather.11.cloned.1.call-done = bf16[1,1024,2048]{2,1,0:T(8,128)(2,1)} async-done(((bf16[1,256,2048]{2,1,0:T(8,128)(2,1)}), bf16[1,1024,2048]{2,1,0:T(8,128)(2,1)}) %all-gather.11.cloned.1.call-update) | async-done | bytes 4194320 | tf_op jit(solution)/shard_map/all_gather | solution.py:302
  341.1 13.0 %fusion.34 = (bf16[1024,1024]{1,0:T(8,128)(2,1)}, bf16[1024,1024]{1,0:T(8,128)(2,1)}, f32[1024,1024]{1,0:T(8,128)}) fusion(f32[1024,1024]{1,0:T(8,128)} %copy-done.1, bf16[1024,1024]{1,0:T(8,128)(2,1)S(1)} %get-tuple-element.97, f32[1024]{0:T(1024)S(1)} %get-tuple-element.81, bf16[1024,2048]{1,0:T(8,128)(2,1)} %copy-done.13, ...), kind=kOutput, calls=%fused_computation.58 | convolution fusion | flops 4313841664 | bytes 25169920 | tf_op jit(solution)/shard_map/dot_general | solution.py:36
  359.9 75.0 %scan_backward.1 = (f32[1024,1024]{1,0:T(8,128)}, f32[1024,1024]{1,0:T(8,128)}, f32[64,256]{1,0:T(8,128)}, f32[64,256]{1,0:T(8,128)}, f32[64,256]{1,0:T(8,128)}) custom-call(f32[1024,1024]{1,0:T(8,128)} %get-tuple-element.96.step_ref, f32[1024,1024]{1,0:T(8,128)} %get-tuple-element.95.inj_ref, f32[1024,1024]{1,0:T(8,128)} %get-tuple-element.103.dy_ref, ...), custom_call_target="tpu_custom_call" | custom-call | flops 1677721600 | bytes 58720256 | tf_op jit(solution)/shard_map/scan_backward/pallas_call | solution.py:235
  435.0 7.4 fusion.38
  452.0 28.2 %all-reduce.10 = bf16[1024,160]{0,1:T(8,128)(2,1)S(1)} all-reduce(f32[1024,160]{0,1:T(8,128)S(1)} %pad_maximum_fusion.3), channel_id=1, replica_groups=mesh['dp'=8,'seq'=4] {'seq'}, use_global_device_ids=true, to_apply=%region_8.9 | all-reduce | flops 163840 | bytes 983040 | tf_op jit(solution)/shard_map/psum | solution.py:373
  480.8 8.3 %fusion.78 = (bf16[1024]{0:T(1024)(128)(2,1)S(1)}, bf16[1024]{0:T(1024)(128)(2,1)S(1)}, f32[1024,1024]{1,0:T(8,128)S(1)}) fusion(bf16[1024,2048]{1,0:T(8,128)(2,1)} %copy-done.13, pred[1024]{0:T(1024)(128)(4,1)S(1)} %get-tuple-element.114, f32[1024,1024]{1,0:T(8,128)} %get-tuple-element.98, f32[1024,1024]{1,0:T(8,128)} %get-tuple-element.103.dy_ref, ...), kind=kOutput, calls=%fused_computation.160 | convolution fusion | flops 353368064 | bytes 23929856 | tf_op jit(solution)/shard_map/dot_general | solution.py:36
  496.5 7.4 fusion.44
  506.7 7.6 fusion.57
  514.4 12.8 %fusion.5 = (f32[2048]{0:T(1024)S(1)}, bf16[1,1024,2048]{2,1,0:T(8,128)(2,1)}) fusion(bf16[1,1024,2048]{2,1,0:T(8,128)(2,1)S(1)} %copy-done.12, f32[1024]{0:T(1024)S(1)} %add_rsqrt_fusion, bf16[2048,2048]{1,0:T(8,128)(2,1)} %all-gather.9.cloned.1.call-done, bf16[1024,1024]{1,0:T(8,128)(2,1)S(1)} %copy-done.24, bf16[1024,1024]{1,0:T(8,128)(2,1)S(1)} %fusion.57), kind=kOutput, calls=%fused_computation.9 | convolution fusion | flops 8608806912 | bytes 20983808 | tf_op jit(solution)/shard_map/dot_general | solution.py:36
  527.3 9.4 %convert_bitcast_fusion.1 = bf16[1,1024,2048]{2,1,0:T(8,128)(2,1)} fusion(bf16[1024,1024]{1,0:T(8,128)(2,1)} %get-tuple-element.100, bf16[1024,2432]{1,0:T(8,128)(2,1)} %all-gather.5.cloned.1.call-done), kind=kOutput, calls=%fused_computation.76 | convolution fusion | flops 4297064448 | bytes 10485760 | tf_op jit(solution)/shard_map/dot_general | solution.py:36
  536.8 14.1 %convolution_convert_fusion = bf16[2048,2048]{1,0:T(8,128)(2,1)} fusion(bf16[1024,1024]{1,0:T(8,128)(2,1)} %get-tuple-element.99, bf16[1024,1024]{1,0:T(8,128)(2,1)S(1)} %fusion.57, bf16[1,1024,2048]{2,1,0:T(8,128)(2,1)} %all-gather.7.cloned.1.call-done, f32[2048]{0:T(1024)S(1)} %convert_element_type.143, f32[1024]{0:T(1024)S(1)} %add_rsqrt_fusion), kind=kOutput, calls=%fused_computation.10 | convolution fusion | flops 8610906112 | bytes 16789504 | tf_op jit(solution)/shard_map/dot_general | solution.py:36
  551.0 14.9 %reduce-scatter.11.cloned.1.call-done = bf16[128,2432]{1,0:T(8,128)(2,1)} async-done(((bf16[1024,2432]{1,0:T(8,128)(2,1)}), bf16[128,2432]{1,0:T(8,128)(2,1)}) %reduce-scatter.11.cloned.1.call-update) | async-done | bytes 622608 | tf_op jit(solution)/shard_map/reduce_scatter | solution.py:399
  570.4 61.2 %psum.23 = f32[2048]{0:T(1024)} all-reduce(f32[2048]{0:T(1024)S(1)} %get-tuple-element.101), channel_id=1, replica_groups=mesh['dp'=8,'seq'=4] {'dp','seq'}, use_global_device_ids=true, to_apply=%region_12.13 | all-reduce | flops 2048 | bytes 16384 | tf_op jit(solution)/shard_map/psum | solution.py:408
  637.8 16.3 %reduce-scatter.7.cloned.1.call-done = bf16[1,256,2048]{2,1,0:T(8,128)(2,1)} async-done(((bf16[1,1024,2048]{2,1,0:T(8,128)(2,1)}), bf16[1,256,2048]{2,1,0:T(8,128)(2,1)}) %reduce-scatter.7.cloned.1.call-update) | async-done | bytes 1048592 | tf_op jit(solution)/shard_map/reduce_scatter | solution.py:410
  655.9 77.0 %reduce-scatter.5.cloned.1.call-done = bf16[1,256,2048]{2,1,0:T(8,128)(2,1)} async-done(((bf16[1,1024,2048]{2,1,0:T(8,128)(2,1)}), bf16[1,256,2048]{2,1,0:T(8,128)(2,1)}) %reduce-scatter.5.cloned.1.call-update) | async-done | bytes 1048592 | tf_op jit(solution)/shard_map/reduce_scatter | solution.py:359
  736.6 71.9 %reduce-scatter.9.cloned.1.call-done = bf16[256,2048]{1,0:T(8,128)(2,1)} async-done(((bf16[2048,2048]{1,0:T(8,128)(2,1)}), bf16[256,2048]{1,0:T(8,128)(2,1)}) %reduce-scatter.9.cloned.1.call-update) | async-done | bytes 1048592 | tf_op jit(solution)/shard_map/reduce_scatter | solution.py:404
  (142 shorter events, 96.2 us)
Async XLA Ops:
  7.2 52.5 %copy-start.22 = (bf16[2048]{0:T(1024)(128)(2,1)S(1)}, bf16[2048]{0:T(1024)(128)(2,1)}, u32[]{:S(2)}) copy-start(bf16[2048]{0:T(1024)(128)(2,1)} %param.14) | copy-start | bytes 12292
  7.2 52.5 %copy-start.23 = (s32[1,3]{1,0:T(1,128)S(1)}, s32[1,3]{1,0:T(1,128)}, u32[]{:S(2)}) copy-start(s32[1,3]{1,0:T(1,128)} %param.13) | copy-start | bytes 40
  7.2 91.5 %all-gather.7.cloned.1.call-start = ((), (), s32[]{:S(2)}) async-start(), calls=%async_computation.5 | async-start | bytes 5242880 | tf_op jit(solution)/shard_map/all_gather | solution.py:299
  7.9 135.7 %all-gather.5.cloned.1.call-start = ((), (), s32[]{:S(2)}) async-start(), calls=%async_computation.4 | async-start | bytes 5603328 | tf_op jit(solution)/shard_map/all_gather | solution.py:301
  14.0 44.0 %collective-permute-start = (bf16[128,2432]{1,0:T(8,128)(2,1)S(1)}, bf16[128,2432]{1,0:T(8,128)(2,1)S(1)}, u32[]{:S(2)}, u32[]{:S(2)}) collective-permute-start(bf16[128,2432]{1,0:T(8,128)(2,1)S(1)} %fusion.61), channel_id=1, source_target_pairs={{0,0},{1,4},{2,1},{3,5},{4,2},{5,6},{6,3},{7,7},{8,8},{9,12},{10,9... | collective-permute-start | bytes 1867784 | tf_op jit(solution)/shard_map/ppermute | solution.py:301
  58.9 141.1 %all-gather.9.cloned.1.call-start = ((), (), s32[]{:S(2)}) async-start(), calls=%async_computation.6 | async-start | bytes 9437184 | tf_op jit(solution)/shard_map/all_gather | solution.py:300
  59.6 201.3 %all-reduce.9.cloned.1.call-start = ((), (), s32[]{:S(2)}) async-start(), calls=%async_computation.7 | async-start | bytes 1310720 | tf_op jit(solution)/shard_map/psum | solution.py:331
  221.7 119.4 %all-gather.11.cloned.1.call-start = ((), (), s32[]{:S(2)}) async-start(), calls=%async_computation.9 | async-start | bytes 5242880 | tf_op jit(solution)/shard_map/all_gather | solution.py:302
  222.3 343.6 %reduce-scatter.11.cloned.1.call-start = ((), (), s32[]{:S(2)}) async-start(), calls=%async_computation.12 | async-start | bytes 5603328 | tf_op jit(solution)/shard_map/reduce_scatter | solution.py:399
  269.6 8.3 %copy-start.15 = (f32[1024,16]{1,0:T(8,128)S(1)}, f32[1024,16]{1,0:T(8,128)}, u32[]{:S(2)}) copy-start(f32[1024,16]{1,0:T(8,128)} %copy.97) | copy-start | bytes 196612
  278.0 11.8 %copy-start = (f32[1024,128]{1,0:T(8,128)}, f32[1024,128]{1,0:T(8,128)S(1)}, u32[]{:S(2)}) copy-start(f32[1024,128]{1,0:T(8,128)S(1)} %broadcast_in_dim.139.keep_ref) | copy-start | bytes 1572868
  359.9 75.0 %copy-start.5 = (f32[1024,1024]{1,0:T(8,128)S(1)}, f32[1024,1024]{1,0:T(8,128)}, u32[]{:S(2)}) copy-start(f32[1024,1024]{1,0:T(8,128)} %get-tuple-element.103.dy_ref) | copy-start | bytes 12582916
  434.9 7.4 copy-start.6
  434.9 7.4 copy-start.7
  435.0 8.3 %copy-start.8 = (f32[1024,1024]{1,0:T(8,128)S(1)}, f32[1024,1024]{1,0:T(8,128)}, u32[]{:S(2)}) copy-start(f32[1024,1024]{1,0:T(8,128)} %get-tuple-element.21) | copy-start | bytes 12582916
  480.8 8.4 %copy-start.3 = (bf16[1,1024,1024]{2,1,0:T(8,128)(2,1)S(1)}, bf16[1,1024,1024]{2,1,0:T(8,128)(2,1)}, u32[]{:S(2)}) copy-start(bf16[1,1024,1024]{2,1,0:T(8,128)(2,1)} %copy-done.2) | copy-start | bytes 6291460
  506.6 147.4 %reduce-scatter.7.cloned.1.call-start = ((), (), s32[]{:S(2)}) async-start(), calls=%async_computation.10 | async-start | bytes 5242880 | tf_op jit(solution)/shard_map/reduce_scatter | solution.py:410
  506.7 7.6 copy-start.12
  506.7 7.7 copy-start.24
  527.3 205.6 %reduce-scatter.5.cloned.1.call-start = ((), (), s32[]{:S(2)}) async-start(), calls=%async_computation.8 | async-start | bytes 5242880 | tf_op jit(solution)/shard_map/reduce_scatter | solution.py:359
  536.7 271.8 %reduce-scatter.9.cloned.1.call-start = ((), (), s32[]{:S(2)}) async-start(), calls=%async_computation.11 | async-start | bytes 9437184 | tf_op jit(solution)/shard_map/reduce_scatter | solution.py:404
  550.9 103.1 %copy-start.10 = (bf16[1,256,2048]{2,1,0:T(8,128)(2,1)S(1)}, bf16[1,256,2048]{2,1,0:T(8,128)(2,1)}, u32[]{:S(2)}) copy-start(bf16[1,256,2048]{2,1,0:T(8,128)(2,1)} %param.12) | copy-start | bytes 3145732
  551.0 181.9 %copy-start.11 = (bf16[1,256,2048]{2,1,0:T(8,128)(2,1)S(1)}, bf16[1,256,2048]{2,1,0:T(8,128)(2,1)}, u32[]{:S(2)}) copy-start(bf16[1,256,2048]{2,1,0:T(8,128)(2,1)} %param.23) | copy-start | bytes 3145732
  565.8 65.8 %collective-permute-start.1 = (bf16[128,2432]{1,0:T(8,128)(2,1)}, bf16[128,2432]{1,0:T(8,128)(2,1)S(1)}, u32[]{:S(2)}, u32[]{:S(2)}) collective-permute-start(bf16[128,2432]{1,0:T(8,128)(2,1)} %reduce-scatter.11.cloned.1.call-done), channel_id=1, source_target_pairs={{0,0},{4,1},{1,2},{5,3},{2,4},{6,5},{3,6},{7,7},{8,8},{12,9},{9,10... | collective-permute-start | bytes 1867784 | tf_op jit(solution)/shard_map/ppermute | solution.py:400
  (12 other events, 54.5 us)
Sparse Core Ops, SparseCore 0:
  9.6 89.0 all-gather.6
  101.2 42.3 all-gather.4
  145.5 54.3 all-gather.8
  221.8 39.0 all-reduce.8
  262.3 78.8 all-gather.10
  506.7 59.0 reduce-scatter.10
  568.2 85.7 reduce-scatter.6
  656.4 76.4 reduce-scatter.4
  736.7 71.7 reduce-scatter.8

commit v2 on v1

--- a/solution.py
+++ b/solution.py
@@ -255,6 +255,184 @@
     )(step, inj, dy, ksq_lanes, query_lanes, keep_lanes, wk, wk2, states, states)
 
 
+MESH = pl.DeviceIdType.MESH
+
+
+def any_specs(count):
+    return [pl.BlockSpec(memory_space=pl.ANY)] * count
+
+
+def place():
+    return lax.axis_index("dp"), lax.axis_index("seq")
+
+
+def mate(d):
+    return d + 1 - 2 * lax.rem(d, 2)
+
+
+def remote(src, dst, send, recv, device):
+    return pltpu.make_async_remote_copy(
+        src_ref=src, dst_ref=dst, send_sem=send, recv_sem=recv, device_id=device, device_id_type=MESH
+    )
+
+
+def greet(device, here=True):
+    barrier = pltpu.get_barrier_semaphore()
+
+    def tell():
+        pl.semaphore_signal(barrier, inc=1, device_id=device, device_id_type=MESH)
+
+    if here is True:
+        tell()
+    else:
+        pl.when(here)(tell)
+
+
+def gather_kernel(
+    dp, seq, hid_ref, w_ref, pk_ref, hid_out, w_out, pk_out,
+    z_send, z_recv, w_send, w_recv, f_send, f_recv, p_send, p_recv, q_send, q_recv, t_sem, own_sem,
+):
+    d, s = place()
+    part = hid_ref.shape[1]
+    w_rows, p_rows = w_ref.shape[0], pk_ref.shape[0]
+    pieces = z_send.shape[2]
+    piece = part // pieces
+    half = seq // 2
+    pairs = dp // 2
+    to_d, to_s = 2 * (d // 2) + lax.rem(s, 2), half * lax.rem(d, 2) + s // 2
+    from_d, from_s = 2 * (d // 2) + s // half, 2 * lax.rem(s, half) + lax.rem(d, 2)
+    moves = jnp.logical_or(to_d != d, to_s != s)
+
+    greet((d, s - 1), s > 0)
+    greet((d, s + 1), s < seq - 1)
+    for k in range(1, pairs):
+        greet((lax.rem(d + 2 * k, dp), s))
+    greet((mate(d), s))
+    greet((to_d, to_s), moves)
+    greet((from_d, from_s), moves)
+    count = pairs + jnp.where(s > 0, 1, 0) + jnp.where(s < seq - 1, 1, 0) + jnp.where(moves, 2, 0)
+    pl.semaphore_wait(pltpu.get_barrier_semaphore(), count)
+
+    def shard(which, q):
+        return hid_out.at[:, pl.ds(which * part + q * piece, piece), :]
+
+    def hop(way, k, q):
+        which = s - k if way == 0 else s + k
+        src = hid_ref.at[:, pl.ds(q * piece, piece), :] if k == 0 else shard(which, q)
+        near = s + 1 if way == 0 else s - 1
+        return remote(src, shard(which, q), z_send.at[way, k, q], z_recv.at[way, k, q], (d, near))
+
+    def can_send(way, k):
+        if way == 0:
+            return jnp.logical_and(s - k >= 0, s < seq - 1)
+        return jnp.logical_and(s + k < seq, s > 0)
+
+    def w_slot(which):
+        return w_out.at[pl.ds(which * w_rows, w_rows)]
+
+    def p_slot(which):
+        return pk_out.at[pl.ds(which * p_rows, p_rows)]
+
+    def spread(slot, own, send, recv, k):
+        return remote(own, slot(d), send.at[k], recv.at[k], (lax.rem(d + 2 * k, dp), s))
+
+    def source(k):
+        return lax.rem(d - 2 * k + dp, dp)
+
+    def across(slot, send, recv, k, own=None):
+        return remote(own if k == 0 else slot(source(k)), slot(source(k)), send.at[k], recv.at[k], (mate(d), s))
+
+    for q in range(pieces):
+        for way in range(2):
+            pl.when(can_send(way, 0))(hop(way, 0, q).start)
+    transfer = remote(pk_ref, p_slot(to_d), t_sem.at[0], t_sem.at[1], (to_d, to_s))
+    stay = pltpu.make_async_copy(pk_ref, p_slot(d), own_sem.at[2])
+    pl.when(moves)(transfer.start)
+    pl.when(jnp.logical_not(moves))(stay.start)
+    for k in range(1, pairs):
+        spread(w_slot, w_ref, w_send, w_recv, k).start()
+    across(w_slot, f_send, f_recv, 0, w_ref).start()
+    own_w = pltpu.make_async_copy(w_ref, w_slot(d), own_sem.at[0])
+    own_h = pltpu.make_async_copy(hid_ref, hid_out.at[:, pl.ds(s * part, part), :], own_sem.at[1])
+    own_w.start()
+    own_h.start()
+
+    pl.when(moves)(remote(pk_ref, p_slot(d), t_sem.at[0], t_sem.at[1], (to_d, to_s)).wait_recv)
+    pl.when(jnp.logical_not(moves))(stay.wait)
+    for k in range(1, pairs):
+        spread(p_slot, p_slot(d), p_send, p_recv, k).start()
+    across(p_slot, q_send, q_recv, 0, p_slot(d)).start()
+
+    def arrive(k):
+        for q in range(pieces):
+            for way in range(2):
+                got = s - k >= 0 if way == 0 else s + k < seq
+
+                @pl.when(got)
+                def _():
+                    which = s - k if way == 0 else s + k
+                    remote(
+                        shard(which, q), shard(which, q), z_send.at[way, k - 1, q], z_recv.at[way, k - 1, q], (d, s)
+                    ).wait_recv()
+
+                if k < seq - 1:
+                    pl.when(can_send(way, k))(hop(way, k, q).start)
+
+    for k in range(1, seq - 1):
+        arrive(k)
+    for slot, own, send, recv, over_send, over_recv in (
+        (w_slot, w_ref, w_send, w_recv, f_send, f_recv),
+        (p_slot, None, p_send, p_recv, q_send, q_recv),
+    ):
+        for k in range(1, pairs):
+            remote(slot(source(k)), slot(source(k)), send.at[k], recv.at[k], (d, s)).wait_recv()
+            across(slot, over_send, over_recv, k).start()
+    arrive(seq - 1)
+
+    def other(k):
+        return lax.rem(mate(d) - 2 * k + dp, dp)
+
+    for slot, own, over_send, over_recv in ((w_slot, w_ref, f_send, f_recv), (p_slot, p_slot(d), q_send, q_recv)):
+        for k in range(pairs):
+            remote(slot(other(k)), slot(other(k)), over_send.at[k], over_recv.at[k], (d, s)).wait_recv()
+            across(slot, over_send, over_recv, k, own).wait_send()
+    for k in range(1, pairs):
+        spread(w_slot, w_ref, w_send, w_recv, k).wait_send()
+        spread(p_slot, p_slot(d), p_send, p_recv, k).wait_send()
+    for k in range(seq - 1):
+        for q in range(pieces):
+            for way in range(2):
+                pl.when(can_send(way, k))(hop(way, k, q).wait_send)
+    pl.when(moves)(transfer.wait_send)
+    own_w.wait()
+    own_h.wait()
+
+
+def gather(hidden, weight, packed, collective_id=0):
+    dp, seq = lax.axis_size("dp"), lax.axis_size("seq")
+    seqs, part, width = hidden.shape
+    pieces = 4 if part % 64 == 0 else 1
+    dma = pltpu.SemaphoreType.DMA
+    return pl.pallas_call(
+        functools.partial(gather_kernel, dp, seq),
+        in_specs=any_specs(3),
+        out_specs=any_specs(3),
+        out_shape=[
+            jax.ShapeDtypeStruct((seqs, part * seq, width), hidden.dtype),
+            jax.ShapeDtypeStruct((weight.shape[0] * dp, weight.shape[1]), weight.dtype),
+            jax.ShapeDtypeStruct((packed.shape[0] * dp, packed.shape[1]), packed.dtype),
+        ],
+        scratch_shapes=[
+            dma((2, seq, pieces)), dma((2, seq, pieces)),
+            dma((dp // 2,)), dma((dp // 2,)), dma((dp // 2,)), dma((dp // 2,)),
+            dma((dp // 2,)), dma((dp // 2,)), dma((dp // 2,)), dma((dp // 2,)),
+            dma((2,)), dma((3,)),
+        ],
+        compiler_params=pltpu.CompilerParams(collective_id=collective_id, has_side_effects=True),
+        name="gather_in",
+    )(hidden, weight, packed)
+
+
 def regroup(dp, seq):
     half = seq // 2
     forth = [
@@ -296,9 +474,8 @@
     padded_cols = -(-used // LANES) * LANES
     packed = jnp.concatenate([out_weight, jnp.pad(small, ((0, 0), (0, padded_cols - used)))], axis=1)
 
-    hidden = lax.all_gather(hidden_in, "seq", axis=1, tiled=True).reshape(tokens, width)
-    w_in = lax.all_gather(in_weight, "dp", axis=0, tiled=True)
-    packed = lax.all_gather(lax.ppermute(packed, both, forth), "dp", axis=0, tiled=True)
+    hidden, w_in, packed = gather(hidden_in, in_weight, packed)
+    hidden = hidden.reshape(tokens, width)
     cot = lax.all_gather(out_cotangent, "seq", axis=1, tiled=True).reshape(tokens, width)
 
     w_out = packed[:, :width]

time: 827 us -> 735 us (0.89)
  waiting for transfers between devices: 407 us -> 236 us
  Pallas kernels: 112 us -> 193 us
    all_gather x3 -> x0, waiting for transfers between devices: 134 us -> none  [the longest x1 53.4 us: local(): w_in = lax.all_gather(in_weight, 'dp', axis=0, tiled=True)]
    pallas_call x0 -> x1, Pallas kernels: none -> 80.7 us  [gather(): pl.pallas_call(functools.partial(gather_kernel, dp, seq), in_specs=any_sp...]
    ppermute x1 -> x0, waiting for transfers between devices: 40.8 us -> none  [local(): lax.ppermute(packed, both, forth)]
  transfers between devices with their start and end apart: 11 -> 7, of which waited for: 10 -> 6; matrix products, arithmetic and copies ran while one was open for 12% -> 11% of each run, Pallas kernels for 5% -> 5%
where the time goes in v2:
time: 735 us; the launch traced here: 726 us
  waiting for transfers between devices  236 us (32%)
  Pallas kernels  193 us (26%)
  matrix products  90.2 us (12%)
  blocking collectives  89.5 us (12%)
  other arithmetic  52.8 us (7%)
  local copies, waits for them, and re-layouts  43.8 us (6%)
  between operations  14.9 us (2%)
    dot_general x12, matrix products, mm(): lax.dot_general(left, right, (dims, ((), ())), preferred_element_type=F32)  90.2 us
    pallas_call x1, Pallas kernels, gather(): pl.pallas_call(functools.partial(gather_kernel, dp, seq), in_specs=any_sp...  80.7 us
    reduce_scatter x1, waiting for transfers between devices, local(): branch = lax.psum_scatter(branch, 'seq', scatter_dimension=1, tiled=True)  76.9 us
    pallas_call x1, Pallas kernels, run_backward(): pl.pallas_call(scan_backward, grid=(seqs, blocks), in_specs=[rows, rows,...  75 us
    reduce_scatter x1, waiting for transfers between devices, local(): lax.psum_scatter(mm(d_pre, normed, TN).astype(BF), 'dp', scatter_dimensio...  71.8 us
    psum x1, blocking collectives, local(): grad_norm_gain = lax.psum(gain_local, both)  61.3 us
    psum x1, waiting for transfers between devices, local(): proj = lax.psum(mm(xc_low, w_x, NN), 'seq')  43.2 us
    pallas_call x1, Pallas kernels, run_forward(): pl.pallas_call(scan_forward, grid=(seqs, blocks), in_specs=[pl.BlockSpec(...  37 us
  transfers between devices with their start and end apart: 7, of which 6 were waited for; matrix products, arithmetic and copies ran while one was open for 11% of the time, Pallas kernels for 5%

profile of v2, /device:TPU:9, one launch (start us, length us, event | category | flops | bytes accessed | tf_op | source)
XLA Modules:
  0.0 725.5 jit_solution(12086345734638682607)
XLA Ops:
  16.4 80.7 %gather_in.1 = (bf16[1,1024,2048]{2,1,0:T(8,128)(2,1)}, bf16[2048,2048]{1,0:T(8,128)(2,1)}, bf16[1024,2432]{1,0:T(8,128)(2,1)}) custom-call(bf16[1,256,2048]{2,1,0:T(8,128)(2,1)} %hid_ref.1, bf16[256,2048]{1,0:T(8,128)(2,1)} %w_ref.1, bf16[128,2432]{1,0:T(8,128)(2,1)} %fusion.61.pk_ref), custom_call_target="tpu_custom_call" | custom-call | tf_op jit(solution)/shard_map/gather_in/pallas_call | solution.py:416
  103.3 11.3 %convolution_convert_fusion.1 = bf16[1024,2048]{1,0:T(8,128)(2,1)S(1)} fusion(bf16[2048,2048]{1,0:T(8,128)(2,1)} %get-tuple-element.23, bf16[1,1024,2048]{2,1,0:T(8,128)(2,1)S(1)} %copy-done.13, f32[2048]{0:T(1024)S(1)} %convert_element_type.143, f32[1024]{0:T(1024)S(1)} %add_rsqrt_fusion), kind=kOutput, calls=%fused_computation.84 | convolution fusion | flops 8600420352 | bytes 16789504 | tf_op jit(solution)/shard_map/dot_general | solution.py:36
  114.9 6.2 multiply_convert_fusion.2
  125.1 43.2 %all-reduce.9.cloned.1.call-done = f32[1024,160]{0,1:T(8,128)} async-done(((f32[1024,160]{0,1:T(8,128)}), f32[1024,160]{0,1:T(8,128)}) %all-reduce.9.cloned.1.call-update) | async-done | bytes 655376 | tf_op jit(solution)/shard_map/psum | solution.py:508
  177.2 8.1 %convert_multiply_fusion.6 = (f32[1024,1024]{1,0:T(8,128)}, f32[1024,1024]{1,0:T(8,128)}, f32[1024,1024]{1,0:T(8,128)}) fusion(bf16[1024,1024]{1,0:T(8,128)(2,1)S(1)} %get-tuple-element.103, f32[1024]{0:T(1024)S(1)} %get-tuple-element.113, f32[1024]{0:T(1024)S(1)} %get-tuple-element.88, bf16[1024,2432]{1,0:T(8,128)(2,1)} %get-tuple-element.21, ...), kind=kOutput, calls=%fused_computation.14 | convolution fusion | flops 278921216 | bytes 15212544 | tf_op jit(solution)/shard_map/dot_general | solution.py:36
  185.5 5.9 broadcast_in_dim.138.ksq_ref
  191.4 5.8 broadcast_in_dim.137.key_ref
  197.3 37.0 %scan_forward.1 = (bf16[16384,1024]{1,0:T(8,128)(2,1)}, f32[1024,1024]{1,0:T(8,128)S(1)}) custom-call(f32[1024,1024]{1,0:T(8,128)} %get-tuple-element.102.step_ref, f32[1024,1024]{1,0:T(8,128)} %get-tuple-element.101.inj_ref, f32[1024,16,128]{2,1,0:T(8,128)} %broadcast_in_dim.137.key_ref, f32[1024,16,128]{2,1,0:T(8,128)} %broadcast_in_dim.138.ksq_ref, ...), custom_call_target="tpu_custom_call" | custom-call | flops 671088640 | bytes 46137344 | tf_op jit(solution)/shard_map/scan_forward/pallas_call | solution.py:187
  236.3 12.5 %all-gather.2.cloned.1.call-done = bf16[1,1024,2048]{2,1,0:T(8,128)(2,1)} async-done(((bf16[1,256,2048]{2,1,0:T(8,128)(2,1)}), bf16[1,1024,2048]{2,1,0:T(8,128)(2,1)}) %all-gather.2.cloned.1.call-update) | async-done | bytes 4194320 | tf_op jit(solution)/shard_map/all_gather | solution.py:479
  248.8 13.0 %fusion.34 = (bf16[1024,1024]{1,0:T(8,128)(2,1)}, bf16[1024,1024]{1,0:T(8,128)(2,1)}, f32[1024,1024]{1,0:T(8,128)}) fusion(f32[1024,1024]{1,0:T(8,128)} %copy-done.1, bf16[1024,1024]{1,0:T(8,128)(2,1)S(1)} %get-tuple-element.103, f32[1024]{0:T(1024)S(1)} %get-tuple-element.87, bf16[1024,2048]{1,0:T(8,128)(2,1)} %copy-done.15, ...), kind=kOutput, calls=%fused_computation.58 | convolution fusion | flops 4313841664 | bytes 25169920 | tf_op jit(solution)/shard_map/dot_general | solution.py:36
  267.6 75.0 %scan_backward.1 = (f32[1024,1024]{1,0:T(8,128)}, f32[1024,1024]{1,0:T(8,128)}, f32[64,256]{1,0:T(8,128)}, f32[64,256]{1,0:T(8,128)}, f32[64,256]{1,0:T(8,128)}) custom-call(f32[1024,1024]{1,0:T(8,128)} %get-tuple-element.102.step_ref, f32[1024,1024]{1,0:T(8,128)} %get-tuple-element.101.inj_ref, f32[1024,1024]{1,0:T(8,128)} %get-tuple-element.109.dy_ref, ...), custom_call_target="tpu_custom_call" | custom-call | flops 1677721600 | bytes 58720256 | tf_op jit(solution)/shard_map/scan_backward/pallas_call | solution.py:235
  342.7 7.4 %fusion.38 = (bf16[1024]{0:T(1024)(128)(2,1)S(1)}, f32[1024]{0:T(1024)S(1)}) fusion(f32[1024,1024]{1,0:T(8,128)S(1)} %copy-done.6, bf16[1024,1024]{1,0:T(8,128)(2,1)S(1)} %get-tuple-element.103, f32[1024]{0:T(1024)S(1)} %get-tuple-element.113, f32[1024,1024]{1,0:T(8,128)} %get-tuple-element.125, f32[1024]{0:T(1024)S(1)} %get-tuple-element.88, ...), kind=kLoop, calls=%fused_computation.62 | loop fusion | flops 16775168 | bytes 18888704 | tf_op jit(solution)/shard_map/reduce_sum | solution.py:570
  359.4 28.2 %all-reduce.10 = bf16[1024,160]{0,1:T(8,128)(2,1)S(1)} all-reduce(f32[1024,160]{0,1:T(8,128)S(1)} %pad_maximum_fusion.3), channel_id=1, replica_groups=mesh['dp'=8,'seq'=4] {'seq'}, use_global_device_ids=true, to_apply=%region_8.9 | all-reduce | flops 163840 | bytes 983040 | tf_op jit(solution)/shard_map/psum | solution.py:550
  388.1 8.3 %fusion.78 = (bf16[1024]{0:T(1024)(128)(2,1)S(1)}, bf16[1024]{0:T(1024)(128)(2,1)S(1)}, f32[1024,1024]{1,0:T(8,128)S(1)}) fusion(bf16[1024,2048]{1,0:T(8,128)(2,1)} %copy-done.15, pred[1024]{0:T(1024)(128)(4,1)S(1)} %get-tuple-element.120, f32[1024,1024]{1,0:T(8,128)} %get-tuple-element.104, f32[1024,1024]{1,0:T(8,128)} %get-tuple-element.109.dy_ref, ...), kind=kOutput, calls=%fused_computation.160 | convolution fusion | flops 353368064 | bytes 23929856 | tf_op jit(solution)/shard_map/dot_general | solution.py:36
  403.8 7.4 %fusion.44 = bf16[1024,2048]{1,0:T(8,128)(2,1)S(1)} fusion(bf16[1024,1024]{1,0:T(8,128)(2,1)} %get-tuple-element.106, bf16[1,1024,2048]{2,1,0:T(8,128)(2,1)} %all-gather.2.cloned.1.call-done), kind=kOutput, calls=%fused_computation.85 | convolution fusion | flops 4297064448 | bytes 10485760 | tf_op jit(solution)/shard_map/dot_general | solution.py:36
  414.0 7.6 %fusion.57 = bf16[1024,1024]{1,0:T(8,128)(2,1)S(1)} fusion(f32[1024]{0:T(1024)S(1)} %get-tuple-element.89, f32[1024,1024]{1,0:T(8,128)} %copy-done.10, pred[1024]{0:T(1024)(128)(4,1)S(1)} %get-tuple-element.120, f32[1024]{0:T(1024)S(1)} %get-tuple-element.90, f32[1,1024,1024]{2,1,0:T(8,128)} %get-tuple-element.98, f32[1024]{0:T(1024)S(1)} %get-tuple-element.91, ...), kind=kLoop, calls=%fused_computation.101 | loop fusion | flops 9437184 | bytes 18891776 | tf_op jit(solution)/shard_map/reshape | solution.py:562
  421.7 12.8 %fusion.5 = (f32[2048]{0:T(1024)S(1)}, bf16[1,1024,2048]{2,1,0:T(8,128)(2,1)}) fusion(bf16[1,1024,2048]{2,1,0:T(8,128)(2,1)S(1)} %copy-done.14, f32[1024]{0:T(1024)S(1)} %add_rsqrt_fusion, bf16[2048,2048]{1,0:T(8,128)(2,1)} %get-tuple-element.23, bf16[1024,1024]{1,0:T(8,128)(2,1)S(1)} %copy-done.23, bf16[1024,1024]{1,0:T(8,128)(2,1)S(1)} %fusion.57), kind=kOutput, calls=%fused_computation.9 | convolution fusion | flops 8608806912 | bytes 20983808 | tf_op jit(solution)/shard_map/dot_general | solution.py:36
  434.6 9.4 %convert_bitcast_fusion.1 = bf16[1,1024,2048]{2,1,0:T(8,128)(2,1)} fusion(bf16[1024,1024]{1,0:T(8,128)(2,1)} %get-tuple-element.106, bf16[1024,2432]{1,0:T(8,128)(2,1)} %get-tuple-element.21), kind=kOutput, calls=%fused_computation.76 | convolution fusion | flops 4297064448 | bytes 10485760 | tf_op jit(solution)/shard_map/dot_general | solution.py:36
  444.1 14.1 %convolution_convert_fusion = bf16[2048,2048]{1,0:T(8,128)(2,1)} fusion(bf16[1024,1024]{1,0:T(8,128)(2,1)} %get-tuple-element.105, bf16[1024,1024]{1,0:T(8,128)(2,1)S(1)} %fusion.57, bf16[1,1024,2048]{2,1,0:T(8,128)(2,1)} %get-tuple-element.22, f32[2048]{0:T(1024)S(1)} %convert_element_type.143, f32[1024]{0:T(1024)S(1)} %add_rsqrt_fusion), kind=kOutput, calls=%fused_computation.10 | convolution fusion | flops 8610906112 | bytes 16789504 | tf_op jit(solution)/shard_map/dot_general | solution.py:36
  458.3 14.9 %reduce-scatter.11.cloned.1.call-done = bf16[128,2432]{1,0:T(8,128)(2,1)} async-done(((bf16[1024,2432]{1,0:T(8,128)(2,1)}), bf16[128,2432]{1,0:T(8,128)(2,1)}) %reduce-scatter.11.cloned.1.call-update) | async-done | bytes 622608 | tf_op jit(solution)/shard_map/reduce_scatter | solution.py:576
  477.8 61.3 %psum.23 = f32[2048]{0:T(1024)} all-reduce(f32[2048]{0:T(1024)S(1)} %get-tuple-element.107), channel_id=1, replica_groups=mesh['dp'=8,'seq'=4] {'dp','seq'}, use_global_device_ids=true, to_apply=%region_12.13 | all-reduce | flops 2048 | bytes 16384 | tf_op jit(solution)/shard_map/psum | solution.py:585
  545.3 16.2 %reduce-scatter.7.cloned.1.call-done = bf16[1,256,2048]{2,1,0:T(8,128)(2,1)} async-done(((bf16[1,1024,2048]{2,1,0:T(8,128)(2,1)}), bf16[1,256,2048]{2,1,0:T(8,128)(2,1)}) %reduce-scatter.7.cloned.1.call-update) | async-done | bytes 1048592 | tf_op jit(solution)/shard_map/reduce_scatter | solution.py:587
  563.2 76.9 %reduce-scatter.5.cloned.1.call-done = bf16[1,256,2048]{2,1,0:T(8,128)(2,1)} async-done(((bf16[1,1024,2048]{2,1,0:T(8,128)(2,1)}), bf16[1,256,2048]{2,1,0:T(8,128)(2,1)}) %reduce-scatter.5.cloned.1.call-update) | async-done | bytes 1048592 | tf_op jit(solution)/shard_map/reduce_scatter | solution.py:536
  643.9 71.8 %reduce-scatter.9.cloned.1.call-done = bf16[256,2048]{1,0:T(8,128)(2,1)} async-done(((bf16[2048,2048]{1,0:T(8,128)(2,1)}), bf16[256,2048]{1,0:T(8,128)(2,1)}) %reduce-scatter.9.cloned.1.call-update) | async-done | bytes 1048592 | tf_op jit(solution)/shard_map/reduce_scatter | solution.py:581
  (130 shorter events, 75.5 us)
Async XLA Ops:
  7.2 161.2 %all-reduce.9.cloned.1.call-start = ((), (), s32[]{:S(2)}) async-start(), calls=%async_computation.4 | async-start | bytes 1310720 | tf_op jit(solution)/shard_map/psum | solution.py:508
  97.1 6.2 copy-start.13
  114.6 6.4 copy-start.15
  114.9 6.2 copy-start.2
  123.8 125.0 %all-gather.2.cloned.1.call-start = ((), (), s32[]{:S(2)}) async-start(), calls=%async_computation.6 | async-start | bytes 5242880 | tf_op jit(solution)/shard_map/all_gather | solution.py:479
  124.6 348.7 %reduce-scatter.11.cloned.1.call-start = ((), (), s32[]{:S(2)}) async-start(), calls=%async_computation.9 | async-start | bytes 5603328 | tf_op jit(solution)/shard_map/reduce_scatter | solution.py:576
  177.1 8.4 %copy-start.17 = (f32[1024,16]{1,0:T(8,128)S(1)}, f32[1024,16]{1,0:T(8,128)}, u32[]{:S(2)}) copy-start(f32[1024,16]{1,0:T(8,128)} %copy.97) | copy-start | bytes 196612
  185.5 11.8 %copy-start = (f32[1024,128]{1,0:T(8,128)}, f32[1024,128]{1,0:T(8,128)S(1)}, u32[]{:S(2)}) copy-start(f32[1024,128]{1,0:T(8,128)S(1)} %broadcast_in_dim.139.keep_ref) | copy-start | bytes 1572868
  267.6 75.0 %copy-start.6 = (f32[1024,1024]{1,0:T(8,128)S(1)}, f32[1024,1024]{1,0:T(8,128)}, u32[]{:S(2)}) copy-start(f32[1024,1024]{1,0:T(8,128)} %get-tuple-element.109.dy_ref) | copy-start | bytes 12582916
  342.6 7.4 %copy-start.7 = (f32[1024,1024]{1,0:T(8,128)S(1)}, f32[1024,1024]{1,0:T(8,128)}, u32[]{:S(2)}) copy-start(f32[1024,1024]{1,0:T(8,128)} %get-tuple-element.26) | copy-start | bytes 12582916
  342.6 7.4 %copy-start.8 = (f32[1024,1024]{1,0:T(8,128)S(1)}, f32[1024,1024]{1,0:T(8,128)}, u32[]{:S(2)}) copy-start(f32[1024,1024]{1,0:T(8,128)} %get-tuple-element.125) | copy-start | bytes 12582916
  342.6 8.3 %copy-start.9 = (f32[1024,1024]{1,0:T(8,128)S(1)}, f32[1024,1024]{1,0:T(8,128)}, u32[]{:S(2)}) copy-start(f32[1024,1024]{1,0:T(8,128)} %get-tuple-element.27) | copy-start | bytes 12582916
  350.9 6.4 copy-start.22
  350.9 6.7 copy-start.21
  388.1 8.4 %copy-start.3 = (bf16[1,1024,1024]{2,1,0:T(8,128)(2,1)S(1)}, bf16[1,1024,1024]{2,1,0:T(8,128)(2,1)}, u32[]{:S(2)}) copy-start(bf16[1,1024,1024]{2,1,0:T(8,128)(2,1)} %copy-done.2) | copy-start | bytes 6291460
  396.4 6.2 copy-start.10
  413.9 147.5 %reduce-scatter.7.cloned.1.call-start = ((), (), s32[]{:S(2)}) async-start(), calls=%async_computation.7 | async-start | bytes 5242880 | tf_op jit(solution)/shard_map/reduce_scatter | solution.py:587
  414.0 7.6 %copy-start.14 = (bf16[1,1024,2048]{2,1,0:T(8,128)(2,1)S(1)}, bf16[1,1024,2048]{2,1,0:T(8,128)(2,1)}, u32[]{:S(2)}) copy-start(bf16[1,1024,2048]{2,1,0:T(8,128)(2,1)} %get-tuple-element.22) | copy-start | bytes 12582916
  414.0 7.7 %copy-start.23 = (bf16[1024,1024]{1,0:T(8,128)(2,1)S(1)}, bf16[1024,1024]{1,0:T(8,128)(2,1)}, u32[]{:S(2)}) copy-start(bf16[1024,1024]{1,0:T(8,128)(2,1)} %get-tuple-element.105) | copy-start | bytes 6291460
  434.6 205.5 %reduce-scatter.5.cloned.1.call-start = ((), (), s32[]{:S(2)}) async-start(), calls=%async_computation.5 | async-start | bytes 5242880 | tf_op jit(solution)/shard_map/reduce_scatter | solution.py:536
  444.1 271.6 %reduce-scatter.9.cloned.1.call-start = ((), (), s32[]{:S(2)}) async-start(), calls=%async_computation.8 | async-start | bytes 9437184 | tf_op jit(solution)/shard_map/reduce_scatter | solution.py:581
  458.3 103.2 %copy-start.11 = (bf16[1,256,2048]{2,1,0:T(8,128)(2,1)S(1)}, bf16[1,256,2048]{2,1,0:T(8,128)(2,1)}, u32[]{:S(2)}) copy-start(bf16[1,256,2048]{2,1,0:T(8,128)(2,1)} %hid_ref.1) | copy-start | bytes 3145732
  458.3 181.9 %copy-start.12 = (bf16[1,256,2048]{2,1,0:T(8,128)(2,1)S(1)}, bf16[1,256,2048]{2,1,0:T(8,128)(2,1)}, u32[]{:S(2)}) copy-start(bf16[1,256,2048]{2,1,0:T(8,128)(2,1)} %param.23) | copy-start | bytes 3145732
  473.2 65.9 %collective-permute-start = (bf16[128,2432]{1,0:T(8,128)(2,1)}, bf16[128,2432]{1,0:T(8,128)(2,1)S(1)}, u32[]{:S(2)}, u32[]{:S(2)}) collective-permute-start(bf16[128,2432]{1,0:T(8,128)(2,1)} %reduce-scatter.11.cloned.1.call-done), channel_id=1, source_target_pairs={{0,0},{4,1},{1,2},{5,3},{2,4},{6,5},{3,6},{7,7},{8,8},{12,9},{9,10... | collective-permute-start | bytes 1867784 | tf_op jit(solution)/shard_map/ppermute | solution.py:577
  (7 other events, 26.7 us)
Sparse Core Ops, SparseCore 0:
  123.9 44.3 all-reduce.8
  170.0 78.8 all-gather.1
  414.1 59.1 reduce-scatter.10
  475.5 85.9 reduce-scatter.6
  563.6 76.5 reduce-scatter.4
  643.8 71.7 reduce-scatter.8

commit v3 on v2

--- a/solution.py
+++ b/solution.py
@@ -433,14 +433,221 @@
     )(hidden, weight, packed)
 
 
-def regroup(dp, seq):
+def added(ref, *others):
+    total = ref[...].astype(F32)
+    for other in others:
+        total = total + other[...].astype(F32)
+    return total
+
+
+def scatter_kernel(
+    dp, seq, dn_ref, gw_ref, pk_ref, gain_ref, hid_ref, cot_ref, scale_ref,
+    out_ref, gw_out, pk_out, gain_out,
+    own, come, gw_own, gw_x, gw_r, pk_own, pk_x, pk_r, pk_fin, g_x, g_r, g_z, g_a, g_b,
+    load, z_send, z_recv, w_load, wx_send, wx_recv, w_send, w_recv,
+    p_load, px_send, px_recv, p_send, p_recv, t_sem, gx_sem, g_send, g_recv, gz_send, gz_recv,
+):
+    d, s = place()
+    seqs, part, width = out_ref.shape
+    pieces = z_send.shape[1]
+    piece = part // pieces
     half = seq // 2
-    forth = [
-        (d * seq + s, (2 * (d // 2) + s % 2) * seq + half * (d % 2) + s // 2)
-        for d in range(dp)
-        for s in range(seq)
-    ]
-    return forth, [(b, a) for a, b in forth]
+    pairs = dp // 2
+    mine, odd = d // 2, lax.rem(d, 2)
+    to_d, to_s = 2 * (d // 2) + s // half, 2 * lax.rem(s, half) + lax.rem(d, 2)
+    from_d, from_s = 2 * (d // 2) + lax.rem(s, 2), half * lax.rem(d, 2) + s // 2
+    moves = jnp.logical_or(to_d != d, to_s != s)
+
+    for k in range(1, seq):
+        greet((d, lax.rem(s + k, seq)))
+    for k in range(1, pairs):
+        greet((lax.rem(d + 2 * k, dp), s))
+    greet((mate(d), s))
+    greet((to_d, to_s), moves)
+    greet((from_d, from_s), moves)
+    pl.semaphore_wait(pltpu.get_barrier_semaphore(), seq - 1 + pairs + jnp.where(moves, 2, 0))
+
+    def swap(src_ref, dst, send, recv, j):
+        rows = dst.shape[1]
+        other = 2 * j + 1 - odd
+        return remote(src_ref.at[pl.ds(other * rows, rows)], dst.at[j], send.at[j], recv.at[j], (mate(d), s))
+
+    def fetch(src_ref, dst, sem, j):
+        rows = dst.shape[1]
+        return pltpu.make_async_copy(src_ref.at[pl.ds((2 * j + odd) * rows, rows)], dst.at[j], sem.at[j])
+
+    def chunk(r):
+        return pltpu.make_async_copy(dn_ref.at[:, pl.ds(r * part, part), :], own.at[r], load.at[r])
+
+    gain_swap = remote(gain_ref, g_x, gx_sem.at[0], gx_sem.at[1], (mate(d), s))
+    gain_swap.start()
+    for j in range(pairs):
+        swap(pk_ref, pk_x, px_send, px_recv, j).start()
+    ends = []
+    for i in range(seq):
+        ends.append(seq - 1 - i // 2 if i % 2 == 0 else i // 2)
+    for r in ends:
+        chunk(r).start()
+    for j in range(pairs):
+        fetch(pk_ref, pk_own, p_load, j).start()
+    for j in range(pairs):
+        swap(gw_ref, gw_x, wx_send, wx_recv, j).start()
+        fetch(gw_ref, gw_own, w_load, j).start()
+    for r in ends:
+        chunk(r).wait()
+
+    def give(way, r, q):
+        rows = pl.ds(q * piece, piece)
+        slot = r if way == 0 else jnp.where(s - 1 == r, seq, r)
+        near = s + 1 if way == 0 else s - 1
+        return remote(own.at[r, :, rows, :], come.at[slot, :, rows, :], z_send.at[r, q], z_recv.at[slot, q], (d, near))
+
+    def landed(slot, q):
+        rows = pl.ds(q * piece, piece)
+        here = come.at[slot, :, rows, :]
+        remote(here, here, z_send.at[0, q], z_recv.at[slot, q], (d, s)).wait_recv()
+
+    def pass_on(way, r):
+        first = s == 0 if way == 0 else s == seq - 1
+        sends = s < r if way == 0 else s > r
+        for q in range(pieces):
+            @pl.when(jnp.logical_and(sends, jnp.logical_not(first)))
+            def _():
+                rows = pl.ds(q * piece, piece)
+                landed(r, q)
+                own[r, :, rows, :] = added(own.at[r, :, rows, :], come.at[r, :, rows, :]).astype(BF)
+
+            pl.when(sends)(give(way, r, q).start)
+
+    def round_of(i):
+        pass_on(0, seq - 1 - i)
+        pass_on(1, i)
+
+    def onward(part_own, part_r, send, recv, k):
+        j = lax.rem(mine + k, pairs)
+        return remote(part_own.at[j], part_r.at[k - 1], send.at[k], recv.at[k], (lax.rem(d + 2 * k, dp), s))
+
+    def join(src_ref, part_own, part_x, part_r, sem, xs, xr, send, recv):
+        for k in range(1, pairs + 1):
+            j = lax.rem(mine + k, pairs)
+            fetch(src_ref, part_own, sem, j).wait()
+            swap(src_ref, part_x, xs, xr, j).wait_recv()
+            if k < pairs:
+                part_own[j] = added(part_own.at[j], part_x.at[j]).astype(BF)
+                onward(part_own, part_r, send, recv, k).start()
+
+    def finish(part_own, part_x, part_r, send, recv):
+        for k in range(1, pairs):
+            onward(part_own, part_r, send, recv, k).wait_recv()
+        return added(part_own.at[mine], part_x.at[mine], *[part_r.at[k] for k in range(pairs - 1)])
+
+    round_of(0) if seq == 2 else None
+    gain_swap.wait_recv()
+    g_a[...] = gain_ref[...] + g_x[...]
+
+    def gain_near(k):
+        return remote(g_a, g_r.at[k - 1], g_send.at[k], g_recv.at[k], (lax.rem(d + 2 * k, dp), s))
+
+    def gain_far(k):
+        return remote(g_b, g_z.at[k - 1], gz_send.at[k], gz_recv.at[k], (d, lax.rem(s + k, seq)))
+
+    for k in range(1, pairs):
+        gain_near(k).start()
+    join(pk_ref, pk_own, pk_x, pk_r, p_load, px_send, px_recv, p_send, p_recv)
+    if seq > 2:
+        round_of(0)
+    join(gw_ref, gw_own, gw_x, gw_r, w_load, wx_send, wx_recv, w_send, w_recv)
+    for k in range(1, pairs):
+        gain_near(k).wait_recv()
+    g_b[...] = added(g_a, *[g_r.at[k] for k in range(pairs - 1)])
+    for k in range(1, seq):
+        gain_far(k).start()
+    for i in range(1, seq - 2):
+        round_of(i)
+    pk_fin[...] = finish(pk_own, pk_x, pk_r, p_send, p_recv).astype(BF)
+    back = remote(pk_fin, pk_out, t_sem.at[0], t_sem.at[1], (to_d, to_s))
+    stay = pltpu.make_async_copy(pk_fin, pk_out, t_sem.at[2])
+    pl.when(moves)(back.start)
+    pl.when(jnp.logical_not(moves))(stay.start)
+    if seq > 2:
+        round_of(seq - 2)
+    gw_out[...] = finish(gw_own, gw_x, gw_r, w_send, w_recv)
+    for k in range(1, seq):
+        gain_far(k).wait_recv()
+    gain_out[...] = added(g_b, *[g_z.at[k] for k in range(seq - 1)])
+
+    for q in range(pieces):
+        pl.when(s > 0)(functools.partial(landed, s, q))
+        pl.when(s < seq - 1)(functools.partial(landed, seq, q))
+        rows = pl.ds(q * piece, piece)
+        from_left = jnp.where(s > 0, come[s, :, rows, :].astype(F32), 0.0)
+        from_right = jnp.where(s < seq - 1, come[seq, :, rows, :].astype(F32), 0.0)
+        total = own[s, :, rows, :].astype(F32) + from_left + from_right
+        x = hid_ref[:, rows, :].astype(F32)
+        inv = lax.rsqrt(jnp.mean(x * x, axis=2, keepdims=True) + norm_eps)
+        scaled = total * scale_ref[...].astype(F32)[None]
+        out_ref[:, rows, :] = (
+            cot_ref[:, rows, :].astype(F32)
+            + inv * scaled
+            - x * (inv * inv * inv) * jnp.mean(x * scaled, axis=2, keepdims=True)
+        ).astype(BF)
+
+    for q in range(pieces):
+        for r in range(1, seq):
+            pl.when(s < r)(give(0, r, q).wait_send)
+        for r in range(seq - 1):
+            pl.when(s > r)(give(1, r, q).wait_send)
+    gain_swap.wait_send()
+    for j in range(pairs):
+        swap(pk_ref, pk_x, px_send, px_recv, j).wait_send()
+        swap(gw_ref, gw_x, wx_send, wx_recv, j).wait_send()
+    for k in range(1, pairs):
+        onward(pk_own, pk_r, p_send, p_recv, k).wait_send()
+        onward(gw_own, gw_r, w_send, w_recv, k).wait_send()
+        gain_near(k).wait_send()
+    for k in range(1, seq):
+        gain_far(k).wait_send()
+    pl.when(moves)(back.wait_send)
+    pl.when(moves)(remote(pk_fin, pk_out, t_sem.at[0], t_sem.at[1], (to_d, to_s)).wait_recv)
+    pl.when(jnp.logical_not(moves))(stay.wait)
+
+
+def scatter(d_normed, grad_in_w, packed_grads, gain, hidden_in, cotangent, norm_gain, collective_id=1):
+    dp, seq = lax.axis_size("dp"), lax.axis_size("seq")
+    seqs, part, width = hidden_in.shape
+    w_rows, p_rows = grad_in_w.shape[0] // dp, packed_grads.shape[0] // dp
+    cols = packed_grads.shape[1]
+    pieces = 4 if part % 64 == 0 else 1
+    pairs = dp // 2
+    dma, vmem = pltpu.SemaphoreType.DMA, pltpu.VMEM
+    here = pl.BlockSpec(memory_space=pltpu.VMEM)
+    return pl.pallas_call(
+        functools.partial(scatter_kernel, dp, seq),
+        in_specs=any_specs(3) + [here] * 4,
+        out_specs=[here] * 4,
+        out_shape=[
+            jax.ShapeDtypeStruct((seqs, part, width), BF),
+            jax.ShapeDtypeStruct((w_rows, width), F32),
+            jax.ShapeDtypeStruct((p_rows, cols), BF),
+            jax.ShapeDtypeStruct(gain.shape, F32),
+        ],
+        scratch_shapes=[
+            vmem((seq, seqs, part, width), BF), vmem((seq + 1, seqs, part, width), BF),
+            vmem((pairs, w_rows, width), BF), vmem((pairs, w_rows, width), BF), vmem((pairs - 1, w_rows, width), BF),
+            vmem((pairs, p_rows, cols), BF), vmem((pairs, p_rows, cols), BF), vmem((pairs - 1, p_rows, cols), BF),
+            vmem((p_rows, cols), BF),
+            vmem(gain.shape, F32), vmem((pairs - 1,) + gain.shape, F32), vmem((seq - 1,) + gain.shape, F32),
+            vmem(gain.shape, F32), vmem(gain.shape, F32),
+            dma((seq,)), dma((seq, pieces)), dma((seq + 1, pieces)),
+            dma((pairs,)), dma((pairs,)), dma((pairs,)), dma((pairs,)), dma((pairs,)),
+            dma((pairs,)), dma((pairs,)), dma((pairs,)), dma((pairs,)), dma((pairs,)),
+            dma((3,)), dma((2,)), dma((pairs,)), dma((pairs,)), dma((seq,)), dma((seq,)),
+        ],
+        compiler_params=pltpu.CompilerParams(
+            collective_id=collective_id, has_side_effects=True, vmem_limit_bytes=60 << 20
+        ),
+        name="scatter_out",
+    )(d_normed, grad_in_w, packed_grads, gain, hidden_in, cotangent, norm_gain)
 
 
 def local(
@@ -458,11 +665,9 @@
     out_cotangent,
 ):
     seqs, part_len, width = hidden_in.shape
-    both = ("dp", "seq")
     dp, seq = lax.axis_size("dp"), lax.axis_size("seq")
     length = part_len * seq
     tokens = seqs * length
-    forth, back = regroup(dp, seq)
     rows = out_weight.shape[0]
     channels = rows * dp
     lag_max = KCONV - 1
@@ -573,26 +778,21 @@
     )
     small_grads = jnp.concatenate([mm(xc_low, d_proj, TN), mm(d_rate, rate, TN), vector_grads], axis=1)
     packed_grads = jnp.concatenate([grad_w_out, jnp.pad(small_grads, ((0, 0), (0, padded_cols - used)))], axis=1)
-    packed_grads = lax.psum_scatter(packed_grads.astype(BF), "dp", scatter_dimension=0, tiled=True)
-    packed_grads = lax.ppermute(packed_grads, both, back).astype(F32)
+    d_normed = mm(d_pre, w_in, NN)
+    gain_local = jnp.sum(d_normed * x_full * inv_rms, axis=0)
+    grad_in, grad_in_weight, packed_grads, grad_norm_gain = scatter(
+        d_normed.astype(BF).reshape(seqs, length, width),
+        mm(d_pre, normed, TN).astype(BF),
+        packed_grads.astype(BF),
+        gain_local.reshape(8, width // 8),
+        hidden_in,
+        out_cotangent,
+        norm_gain.reshape(1, width),
+    )
+    grad_norm_gain = grad_norm_gain.reshape(width)
+    packed_grads = packed_grads.astype(F32)
     grad_out_weight = packed_grads[:, :width]
     tail = packed_grads[:, width:]
-
-    grad_in_weight = lax.psum_scatter(mm(d_pre, normed, TN).astype(BF), "dp", scatter_dimension=0, tiled=True)
-    grad_in_weight = grad_in_weight.astype(F32)
-    d_normed = mm(d_pre, w_in, NN)
-    gain_local = jnp.sum(d_normed * x_full * inv_rms, axis=0)
-    grad_norm_gain = lax.psum(gain_local, both)
-    d_normed = d_normed.astype(BF).reshape(seqs, length, width)
-    d_normed = lax.psum_scatter(d_normed, "seq", scatter_dimension=1, tiled=True).astype(F32)
-    own = hidden_in.astype(F32)
-    own_rms = lax.rsqrt(jnp.mean(own * own, axis=2, keepdims=True) + norm_eps)
-    scaled = d_normed * gain
-    grad_in = (
-        out_cotangent.astype(F32)
-        + own_rms * scaled
-        - own * (own_rms * own_rms * own_rms) * jnp.mean(own * scaled, axis=2, keepdims=True)
-    ).astype(BF)
 
     base = 2 * R + 2 * N
     return (

time: 735 us -> 618 us (0.84)
  waiting for transfers between devices: 236 us -> 44.9 us
  Pallas kernels: 193 us -> 317 us
  blocking collectives: 89.5 us -> 28.2 us
  local copies, waits for them, and re-layouts: 43.8 us -> 63.8 us
  other arithmetic: 52.8 us -> 40.9 us
    pallas_call x0 -> x1, Pallas kernels: none -> 124 us  [scatter(): pl.pallas_call(functools.partial(scatter_kernel, dp, seq), in_specs=any_s...]
    reduce_scatter x3 -> x0, waiting for transfers between devices: 103 us -> none  [the longest x1 71.8 us: local(): lax.psum_scatter(mm(d_pre, normed, TN).astype(BF), 'dp', scatter_dimensio...]
    reduce_scatter x1, waiting for transfers between devices: 76.9 us -> 0.01 us  [local(): branch = lax.psum_scatter(branch, 'seq', scatter_dimension=1, tiled=True)]
    psum x1 -> x0, blocking collectives: 61.3 us -> none  [local(): grad_norm_gain = lax.psum(gain_local, both)]
    psum x1, waiting for transfers between devices: 43.2 us -> 32.6 us  [local(): proj = lax.psum(mm(xc_low, w_x, NN), 'seq')]
    reduce_scatter x1, starting transfers between devices: 0.04 us -> 10.6 us  [local(): branch = lax.psum_scatter(branch, 'seq', scatter_dimension=1, tiled=True)]
  transfers between devices with their start and end apart: 7 -> 3, of which waited for: 6 -> 2; matrix products, arithmetic and copies ran while one was open for 11% -> 17% of each run, Pallas kernels for 5% -> 26%
where the time goes in v3:
time: 618 us; the launch traced here: 610 us
  Pallas kernels  317 us (51%)
  matrix products  90.6 us (15%)
  local copies, waits for them, and re-layouts  63.8 us (10%)
  waiting for transfers between devices  44.9 us (7%)
  other arithmetic  40.9 us (7%)
  blocking collectives  28.2 us (5%)
  between operations  14.5 us (2%)
  starting transfers between devices  10.6 us (2%)
    pallas_call x1, Pallas kernels, scatter(): pl.pallas_call(functools.partial(scatter_kernel, dp, seq), in_specs=any_s...  124 us
    dot_general x12, matrix products, mm(): lax.dot_general(left, right, (dims, ((), ())), preferred_element_type=F32)  90.6 us
    pallas_call x1, Pallas kernels, gather(): pl.pallas_call(functools.partial(gather_kernel, dp, seq), in_specs=any_sp...  80.7 us
    pallas_call x1, Pallas kernels, run_backward(): pl.pallas_call(scan_backward, grid=(seqs, blocks), in_specs=[rows, rows,...  75 us
    pallas_call x1, Pallas kernels, run_forward(): pl.pallas_call(scan_forward, grid=(seqs, blocks), in_specs=[pl.BlockSpec(...  37.2 us
    psum x1, waiting for transfers between devices, local(): proj = lax.psum(mm(xc_low, w_x, NN), 'seq')  32.6 us
    psum x1, blocking collectives, local(): d_proj = lax.psum(d_proj, 'seq').astype(BF)  28.2 us
    broadcast_in_dim x3, local copies, waits for them, and re-layouts, lanes(): return jnp.broadcast_to(values[:, :, None], (tokens, N, LANES))  17.6 us
  transfers between devices with their start and end apart: 3, of which 2 were waited for; matrix products, arithmetic and copies ran while one was open for 17% of the time, Pallas kernels for 26%

profile of v3, /device:TPU:9, one launch (start us, length us, event | category | flops | bytes accessed | tf_op | source)
XLA Modules:
  0.0 610.1 jit_solution(5447983844163879031)
XLA Ops:
  14.1 80.7 %gather_in.1 = (bf16[1,1024,2048]{2,1,0:T(8,128)(2,1)}, bf16[2048,2048]{1,0:T(8,128)(2,1)}, bf16[1024,2432]{1,0:T(8,128)(2,1)}) custom-call(bf16[1,256,2048]{2,1,0:T(8,128)(2,1)} %hid_ref.3, bf16[256,2048]{1,0:T(8,128)(2,1)} %w_ref.1, bf16[128,2432]{1,0:T(8,128)(2,1)} %fusion.55.pk_ref), custom_call_target="tpu_custom_call" | custom-call | tf_op jit(solution)/shard_map/gather_in/pallas_call | solution.py:416
  94.8 3.2 fusion.1
  98.3 11.3 %convolution_convert_fusion.1 = bf16[1024,2048]{1,0:T(8,128)(2,1)S(1)} fusion(bf16[2048,2048]{1,0:T(8,128)(2,1)} %get-tuple-element.27, bf16[1,1024,2048]{2,1,0:T(8,128)(2,1)S(1)} %copy-done.10, f32[2048]{0:T(1024)S(1)} %convert_element_type.130, f32[1024]{0:T(1024)S(1)} %add_rsqrt_fusion), kind=kOutput, calls=%fused_computation.84 | convolution fusion | flops 8600420352 | bytes 16789504 | tf_op jit(solution)/shard_map/dot_general | solution.py:36
  115.6 9.8 %multiply_convert_fusion.2 = (bf16[1024,1024]{1,0:T(8,128)(2,1)S(1)}, f32[1024,1024]{1,0:T(8,128)}) fusion(f32[1024]{0:T(1024)S(1)} %get-tuple-element.95, bf16[1024,2048]{1,0:T(8,128)(2,1)} %copy-done.13, pred[1024]{0:T(1024)(128)(4,1)S(1)} %get-tuple-element.124, f32[1024]{0:T(1024)S(1)} %get-tuple-element.96, pred[1024]{0:T(1024)(128)(4,1)S(1)} %get-tuple-element.125, ...), kind=kLoop, calls=%fused_computation.81 | loop fusion | flops 22020096 | bytes 10510336 | tf_op jit(solution)/shard_map/convert_element_type | solution.py:711
  128.9 10.6 %reduce-scatter.2.cloned.1.call-start = ((), (), s32[]{:S(2)}) async-start(), calls=%async_computation.2 | async-start | bytes 5242880 | tf_op jit(solution)/shard_map/reduce_scatter | solution.py:741
  140.1 32.6 %all-reduce.9.cloned.1.call-done = f32[1024,160]{0,1:T(8,128)} async-done(((f32[1024,160]{0,1:T(8,128)}), f32[1024,160]{0,1:T(8,128)}) %all-reduce.9.cloned.1.call-update) | async-done | bytes 655376 | tf_op jit(solution)/shard_map/psum | solution.py:713
  182.4 8.1 %convert_multiply_fusion.6 = (f32[1024,1024]{1,0:T(8,128)}, f32[1024,1024]{1,0:T(8,128)}, f32[1024,1024]{1,0:T(8,128)}) fusion(bf16[1024,1024]{1,0:T(8,128)(2,1)S(1)} %get-tuple-element.109, f32[1024]{0:T(1024)S(1)} %get-tuple-element.117, f32[1024]{0:T(1024)S(1)} %get-tuple-element.94, bf16[1024,2432]{1,0:T(8,128)(2,1)} %get-tuple-element.25, ...), kind=kOutput, calls=%fused_computation.14 | convolution fusion | flops 278921216 | bytes 15212544 | tf_op jit(solution)/shard_map/dot_general | solution.py:36
  190.5 5.9 broadcast_in_dim.135.ksq_ref
  196.4 5.8 broadcast_in_dim.134.key_ref
  202.4 37.2 %scan_forward.1 = (bf16[16384,1024]{1,0:T(8,128)(2,1)}, f32[1024,1024]{1,0:T(8,128)S(1)}) custom-call(f32[1024,1024]{1,0:T(8,128)} %get-tuple-element.108.step_ref, f32[1024,1024]{1,0:T(8,128)} %get-tuple-element.107.inj_ref, f32[1024,16,128]{2,1,0:T(8,128)} %broadcast_in_dim.134.key_ref, f32[1024,16,128]{2,1,0:T(8,128)} %broadcast_in_dim.135.ksq_ref, ...), custom_call_target="tpu_custom_call" | custom-call | flops 671088640 | bytes 46137344 | tf_op jit(solution)/shard_map/scan_forward/pallas_call | solution.py:187
  241.7 11.5 %all-gather.2.cloned.1.call-done = bf16[1,1024,2048]{2,1,0:T(8,128)(2,1)} async-done(((bf16[1,256,2048]{2,1,0:T(8,128)(2,1)}), bf16[1,1024,2048]{2,1,0:T(8,128)(2,1)}) %all-gather.2.cloned.1.call-update) | async-done | bytes 4194320 | tf_op jit(solution)/shard_map/all_gather | solution.py:684
  253.2 13.2 %fusion.34 = (bf16[1024,1024]{1,0:T(8,128)(2,1)}, bf16[1024,1024]{1,0:T(8,128)(2,1)}, f32[1024,1024]{1,0:T(8,128)}) fusion(f32[1024,1024]{1,0:T(8,128)} %copy-done.1, bf16[1024,1024]{1,0:T(8,128)(2,1)S(1)} %get-tuple-element.109, f32[1024]{0:T(1024)S(1)} %get-tuple-element.93, bf16[1024,2048]{1,0:T(8,128)(2,1)} %copy-done.13, ...), kind=kOutput, calls=%fused_computation.58 | convolution fusion | flops 4313841664 | bytes 25169920 | tf_op jit(solution)/shard_map/dot_general | solution.py:36
  266.3 5.9 broadcast_in_dim.138.query_ref
  272.2 75.0 %scan_backward.1 = (f32[1024,1024]{1,0:T(8,128)}, f32[1024,1024]{1,0:T(8,128)}, f32[64,256]{1,0:T(8,128)}, f32[64,256]{1,0:T(8,128)}, f32[64,256]{1,0:T(8,128)}) custom-call(f32[1024,1024]{1,0:T(8,128)} %get-tuple-element.108.step_ref, f32[1024,1024]{1,0:T(8,128)} %get-tuple-element.107.inj_ref, f32[1024,1024]{1,0:T(8,128)} %get-tuple-element.115.dy_ref, ...), custom_call_target="tpu_custom_call" | custom-call | flops 1677721600 | bytes 58720256 | tf_op jit(solution)/shard_map/scan_backward/pallas_call | solution.py:235
  347.2 5.3 fusion.73
  354.3 3.5 fusion.38
  361.9 28.2 %all-reduce.10 = bf16[1024,160]{0,1:T(8,128)(2,1)S(1)} all-reduce(f32[1024,160]{0,1:T(8,128)S(1)} %pad_maximum_fusion.3), channel_id=1, replica_groups=mesh['dp'=8,'seq'=4] {'seq'}, use_global_device_ids=true, to_apply=%region_7.8 | all-reduce | flops 163840 | bytes 983040 | tf_op jit(solution)/shard_map/psum | solution.py:755
  390.9 9.2 %convert_bitcast_fusion.1 = bf16[1,1024,2048]{2,1,0:T(8,128)(2,1)} fusion(bf16[1024,1024]{1,0:T(8,128)(2,1)} %get-tuple-element.112, bf16[1024,2432]{1,0:T(8,128)(2,1)} %get-tuple-element.25), kind=kOutput, calls=%fused_computation.76 | convolution fusion | flops 4297064448 | bytes 10485760 | tf_op jit(solution)/shard_map/dot_general | solution.py:36
  400.1 8.3 %fusion.72 = (bf16[1024]{0:T(1024)(128)(2,1)S(1)}, bf16[1024]{0:T(1024)(128)(2,1)S(1)}, f32[1024,1024]{1,0:T(8,128)S(1)}) fusion(bf16[1024,2048]{1,0:T(8,128)(2,1)} %copy-done.13, pred[1024]{0:T(1024)(128)(4,1)S(1)} %get-tuple-element.124, f32[1024,1024]{1,0:T(8,128)} %get-tuple-element.110, f32[1024,1024]{1,0:T(8,128)} %get-tuple-element.115.dy_ref, ...), kind=kOutput, calls=%fused_computation.147 | convolution fusion | flops 353368064 | bytes 23929856 | tf_op jit(solution)/shard_map/dot_general | solution.py:36
  419.2 14.2 %fusion.5 = (f32[2048]{0:T(1024)S(1)}, bf16[1,1024,2048]{2,1,0:T(8,128)(2,1)}) fusion(bf16[1,1024,2048]{2,1,0:T(8,128)(2,1)S(1)} %copy-done.11, f32[1024]{0:T(1024)S(1)} %add_rsqrt_fusion, bf16[2048,2048]{1,0:T(8,128)(2,1)} %get-tuple-element.27, bf16[1024,1024]{1,0:T(8,128)(2,1)S(1)} %copy-done.26, bf16[1024,1024]{1,0:T(8,128)(2,1)S(1)} %fusion.51), kind=kOutput, calls=%fused_computation.9 | convolution fusion | flops 8608806912 | bytes 20983808 | tf_op jit(solution)/shard_map/dot_general | solution.py:36
  438.6 7.5 %fusion.44 = bf16[1024,2048]{1,0:T(8,128)(2,1)S(1)} fusion(bf16[1024,1024]{1,0:T(8,128)(2,1)} %get-tuple-element.112, bf16[1,1024,2048]{2,1,0:T(8,128)(2,1)} %all-gather.2.cloned.1.call-done), kind=kOutput, calls=%fused_computation.85 | convolution fusion | flops 4297064448 | bytes 10485760 | tf_op jit(solution)/shard_map/dot_general | solution.py:36
  446.1 3.0 fusion.6.pk_ref
  451.4 11.9 %convolution_convert_fusion.gw_ref = bf16[2048,2048]{1,0:T(8,128)(2,1)} fusion(bf16[1024,1024]{1,0:T(8,128)(2,1)S(1)} %copy-done.27, bf16[1024,1024]{1,0:T(8,128)(2,1)S(1)} %copy-done.18, bf16[1,1024,2048]{2,1,0:T(8,128)(2,1)S(1)} %copy-done.12, f32[2048]{0:T(1024)S(1)} %convert_element_type.130, f32[1024]{0:T(1024)S(1)} %add_rsqrt_fusion), kind=kOutput, calls=%fused_computation.10 | convolution fusion | flops 8610906112 | bytes 16789504 | tf_op jit(solution)/shard_map/dot_general | solution.py:36
  463.3 123.7 %scatter_out.1 = (bf16[1,256,2048]{2,1,0:T(8,128)(2,1)}, f32[256,2048]{1,0:T(8,128)}, bf16[128,2432]{1,0:T(8,128)(2,1)}, f32[8,256]{1,0:T(8,128)}) custom-call(bf16[1,1024,2048]{2,1,0:T(8,128)(2,1)} %get-tuple-element.114.dn_ref, bf16[2048,2048]{1,0:T(8,128)(2,1)} %convolution_convert_fusion.gw_ref, bf16[1024,2432]{1,0:T(8,128)(2,1)} %fusion.6.pk_ref, ...), custom_call_target="tpu_custom_call" | custom-call | tf_op jit(solution)/shard_map/scatter_out/pallas_call | solution.py:624
  (129 shorter events, 70.0 us)
Async XLA Ops:
  7.2 165.6 %all-reduce.9.cloned.1.call-start = ((), (), s32[]{:S(2)}) async-start(), calls=%async_computation.1 | async-start | bytes 1310720 | tf_op jit(solution)/shard_map/psum | solution.py:713
  11.3 86.8 %copy-start.23 = (bf16[2048]{0:T(1024)(128)(2,1)S(1)}, bf16[2048]{0:T(1024)(128)(2,1)}, u32[]{:S(2)}) copy-start(bf16[2048]{0:T(1024)(128)(2,1)} %param.14) | copy-start | bytes 12292
  109.6 5.7 copy-start.25
  128.1 125.0 %all-gather.2.cloned.1.call-start = ((), (), s32[]{:S(2)}) async-start(), calls=%async_computation.3 | async-start | bytes 5242880 | tf_op jit(solution)/shard_map/all_gather | solution.py:684
  128.9 468.2 %reduce-scatter.2.cloned.1.call-start = ((), (), s32[]{:S(2)}) async-start(), calls=%async_computation.2 | async-start | bytes 5242880 | tf_op jit(solution)/shard_map/reduce_scatter | solution.py:741
  182.4 8.1 %copy-start.15 = (f32[1024,16]{1,0:T(8,128)S(1)}, f32[1024,16]{1,0:T(8,128)}, u32[]{:S(2)}) copy-start(f32[1024,16]{1,0:T(8,128)} %copy.97) | copy-start | bytes 196612
  202.4 37.2 %copy-start = (f32[1024,128]{1,0:T(8,128)}, f32[1024,128]{1,0:T(8,128)S(1)}, u32[]{:S(2)}) copy-start(f32[1024,128]{1,0:T(8,128)S(1)} %broadcast_in_dim.136.keep_ref) | copy-start | bytes 1572868
  253.2 13.2 %copy-start.14 = (f32[1024,16]{1,0:T(8,128)S(1)}, f32[1024,16]{1,0:T(8,128)}, u32[]{:S(2)}) copy-start(f32[1024,16]{1,0:T(8,128)} %copy.99) | copy-start | bytes 196612
  272.2 75.0 %copy-start.7 = (f32[1024,1024]{1,0:T(8,128)S(1)}, f32[1024,1024]{1,0:T(8,128)}, u32[]{:S(2)}) copy-start(f32[1024,1024]{1,0:T(8,128)} %get-tuple-element.127) | copy-start | bytes 12582916
  347.2 5.3 copy-start.5
  347.2 5.9 copy-start.6
  347.2 7.1 %copy-start.8 = (f32[1024,1024]{1,0:T(8,128)S(1)}, f32[1024,1024]{1,0:T(8,128)}, u32[]{:S(2)}) copy-start(f32[1024,1024]{1,0:T(8,128)} %get-tuple-element.31) | copy-start | bytes 12582916
  354.3 5.6 copy-start.22
  354.3 5.9 copy-start.21
  400.1 8.3 %copy-start.4 = (bf16[1,1024,1024]{2,1,0:T(8,128)(2,1)S(1)}, bf16[1,1024,1024]{2,1,0:T(8,128)(2,1)}, u32[]{:S(2)}) copy-start(bf16[1,1024,1024]{2,1,0:T(8,128)(2,1)} %slice_bitcast_fusion) | copy-start | bytes 6291460
  419.2 14.2 %copy-start.17 = (bf16[1024,1024]{1,0:T(8,128)(2,1)}, bf16[1024,1024]{1,0:T(8,128)(2,1)S(1)}, u32[]{:S(2)}) copy-start(bf16[1024,1024]{1,0:T(8,128)(2,1)S(1)} %fusion.51) | copy-start | bytes 6291460
  419.2 14.8 %copy-start.3 = (bf16[1024,1024]{1,0:T(8,128)(2,1)S(1)}, bf16[1024,1024]{1,0:T(8,128)(2,1)}, u32[]{:S(2)}) copy-start(bf16[1024,1024]{1,0:T(8,128)(2,1)} %copy-done.2) | copy-start | bytes 6291460
  446.1 4.0 copy-start.12
  446.1 4.7 copy-start.18
  446.1 5.3 copy-start.27
  587.0 7.8 %copy-start.24 = (f32[8,256]{1,0:T(8,128)S(1)}, f32[8,256]{1,0:T(8,128)}, u32[]{:S(2)}) copy-start(f32[8,256]{1,0:T(8,128)} %get-tuple-element.36) | copy-start | bytes 24580
  587.0 10.1 %copy-start.9 = (bf16[1,256,2048]{2,1,0:T(8,128)(2,1)S(1)}, bf16[1,256,2048]{2,1,0:T(8,128)(2,1)}, u32[]{:S(2)}) copy-start(bf16[1,256,2048]{2,1,0:T(8,128)(2,1)} %hid_ref.3) | copy-start | bytes 3145732
  588.3 5.0 copy-start.19
  588.3 13.7 %copy-start.16 = (f32[256,2048]{1,0:T(8,128)S(1)}, f32[256,2048]{1,0:T(8,128)}, u32[]{:S(2)}) copy-start(f32[256,2048]{1,0:T(8,128)} %get-tuple-element.143) | copy-start | bytes 6291460
  (7 other events, 20.4 us)
Sparse Core Ops, SparseCore 0:
  128.3 44.4 all-reduce.8
  174.3 78.8 all-gather.1
  400.3 80.7 reduce-scatter.1

commit v4 on v3

--- a/solution.py
+++ b/solution.py
@@ -13,6 +13,8 @@
 KCONV = 4
 CHUNK = 16
 LANES = 128
+GROUP = 1024
+BLOCK = 128
 
 norm_eps = 1e-05
 BF = jnp.bfloat16
@@ -45,214 +47,345 @@
     return jnp.broadcast_to(ref[i : i + 1, pl.ds(lane, LANES)], (8, LANES))
 
 
+def wide(ref, rows, count):
+    value = ref[rows, :]
+    return jnp.concatenate([value] * (count // LANES), axis=1)
+
+
+def merge(even, odd, stride):
+    low = lax.broadcasted_iota(jnp.int32, (8, LANES), 0) % (2 * stride) < stride
+    if stride == 4:
+        return jnp.where(low, even, odd) + pltpu.roll(jnp.where(low, odd, even), 4, 0)
+    return jnp.where(low, even + pltpu.roll(even, 8 - stride, 0), odd + pltpu.roll(odd, stride, 0))
+
+
+def collect(stack, value, descending):
+    level = 0
+    while stack and stack[-1][0] == level:
+        other = stack.pop()[1]
+        value = merge(value, other, 1 << level) if descending else merge(other, value, 1 << level)
+        level += 1
+    stack.append((level, value))
+
+
+def each_chunk(tokens, channels, body):
+    group = math.gcd(channels, 512)
+
+    def run(k, carried):
+        rows = pl.ds(pl.multiple_of(k * CHUNK, CHUNK), CHUNK)
+        for first in range(0, channels, group):
+            body(rows, pl.ds(first, group), first)
+        return carried
+
+    lax.fori_loop(0, tokens // CHUNK, run, 0)
+
+
+def load_carry(carry, tiles):
+    out = []
+    for lane in tiles:
+        out += [carry[0:8, pl.ds(lane, LANES)], carry[8:16, pl.ds(lane, LANES)]]
+    return tuple(out)
+
+
+def store_carry(carry, tiles, values):
+    for j, lane in enumerate(tiles):
+        carry[0:8, pl.ds(lane, LANES)] = values[2 * j]
+        carry[8:16, pl.ds(lane, LANES)] = values[2 * j + 1]
+
+
+def halves(value):
+    return [value[0:8], value[8:16]]
+
+
+def token(keys, queries, keeps, i):
+    return row(keeps, i, 0), halves(keys[i].astype(F32)), halves(queries[i].astype(F32))
+
+
 def lane_groups(channels):
-    group = math.gcd(channels, 512)
-    return [(g, group) for g in range(0, channels, group)]
-
-
-def scan_forward(step_ref, inj_ref, key_ref, ksq_ref, keep_ref, wq_ref, s_ref, y_ref, carry):
-    @pl.when(pl.program_id(1) == 0)
-    def _():
-        carry[...] = jnp.zeros_like(carry)
-
-    tokens, channels = step_ref.shape
-    for first, group in lane_groups(channels):
-        tiles = list(range(first, first + group, LANES))
-
-        def chunk(k, state):
-            base = pl.multiple_of(k * CHUNK, CHUNK)
-            state = list(state)
-            steps, injs, keeps = (r.at[pl.ds(base, CHUNK)] for r in (step_ref, inj_ref, keep_ref))
-            for i in range(CHUNK):
-                at = base + i
-                keep = row(keeps, i, 0)
-                key = [key_ref[at, 0:8, :], key_ref[at, 8:16, :]]
-                ksq = [ksq_ref[at, 0:8, :], ksq_ref[at, 8:16, :]]
-                for j, lane in enumerate(tiles):
-                    step = row(steps, i, lane)
-                    inj = row(injs, i, lane)
-                    for h in range(2):
-                        state[2 * j + h] = (keep - step * ksq[h]) * state[2 * j + h] + inj * key[h]
-                    both = jnp.concatenate([state[2 * j], state[2 * j + 1]], axis=0)
-                    s_ref[pl.ds(pl.multiple_of(at * N, N), N), pl.ds(lane, LANES)] = both.astype(BF)
-            rows = pl.ds(pl.multiple_of(k * CHUNK * N, CHUNK * N), CHUNK * N)
-            y_ref[pl.ds(base, CHUNK), pl.ds(first, group)] = mm(
-                wq_ref[pl.ds(base, CHUNK), :], s_ref[rows, pl.ds(first, group)], NN
-            )
-            return tuple(state)
-
-        start = []
-        for lane in tiles:
-            start += [carry[0:8, pl.ds(lane, LANES)], carry[8:16, pl.ds(lane, LANES)]]
-        end = lax.fori_loop(0, tokens // CHUNK, chunk, tuple(start))
-        for j, lane in enumerate(tiles):
-            carry[0:8, pl.ds(lane, LANES)] = end[2 * j]
-            carry[8:16, pl.ds(lane, LANES)] = end[2 * j + 1]
-
-
-def scan_backward(
-    step_ref, inj_ref, dy_ref, ksq_ref, query_ref, keep_ref, wk_ref, wk2_ref, s_ref, before_ref,
-    dinj_ref, pull_ref, dq_ref, dk1_ref, dk2_ref, carry, g_buf, sg_buf,
+    group = math.gcd(channels, GROUP)
+    return [list(range(first, first + group, LANES)) for first in range(0, channels, group)]
+
+
+def forward_kernel(
+    xc_ref, z_ref, rate_ref, key_ref, query_ref, keep_ref, ksum_ref, wdt_ref, vec_ref,
+    s_ref, y_ref, gated_ref, step, inj, carry,
 ):
     @pl.when(pl.program_id(1) == 0)
     def _():
         carry[...] = jnp.zeros_like(carry)
 
-    tokens, channels = step_ref.shape
+    tokens, channels = xc_ref.shape
+    step[...] = mm(rate_ref[...], wdt_ref[...], NT)
+
+    def prepare(rows, cols, first):
+        beta = jax.nn.sigmoid(step[rows, cols] + vec_ref[0:1, cols])
+        eps = beta / (1.0 + beta * wide(ksum_ref, rows, cols.size))
+        step[rows, cols] = eps
+        inj[rows, cols] = eps * xc_ref[rows, cols].astype(F32)
+
+    each_chunk(tokens, channels, prepare)
+    for tiles in lane_groups(channels):
+
+        def chunk(k, state):
+            state = list(state)
+            base = pl.multiple_of(k * CHUNK, CHUNK)
+            steps, injs, keeps, keys, queries = (
+                r.at[pl.ds(base, CHUNK)] for r in (step, inj, keep_ref, key_ref, query_ref)
+            )
+            saved = s_ref.at[pl.ds(pl.multiple_of(k * CHUNK * N, CHUNK * N), CHUNK * N)]
+            stacks = [[] for _ in tiles]
+            for i in range(CHUNK):
+                keep, key, query = token(keys, queries, keeps, i)
+                ksq = [keep * key[h] * key[h] for h in range(2)]
+                for j, lane in enumerate(tiles):
+                    eps, push = row(steps, i, lane), row(injs, i, lane)
+                    for h in range(2):
+                        state[2 * j + h] = (keep - eps * ksq[h]) * state[2 * j + h] + push * key[h]
+                    both = jnp.concatenate([state[2 * j], state[2 * j + 1]], axis=0)
+                    saved[i * N : (i + 1) * N, pl.ds(lane, LANES)] = both.astype(BF)
+                    collect(stacks[j], state[2 * j] * query[0] + state[2 * j + 1] * query[1], False)
+                    if i % 8 == 7:
+                        y_ref[pl.ds(pl.multiple_of(base + i - 7, 8), 8), pl.ds(lane, LANES)] = stacks[j].pop()[1]
+            return tuple(state)
+
+        store_carry(carry, tiles, lax.fori_loop(0, tokens // CHUNK, chunk, load_carry(carry, tiles)))
+
+    def emit(rows, cols, first):
+        y_full = y_ref[rows, cols] + vec_ref[1:2, cols] * xc_ref[rows, cols].astype(F32)
+        y_ref[rows, cols] = y_full
+        z = z_ref[rows, cols].astype(F32)
+        gated_ref[rows, cols] = (y_full * (z * jax.nn.sigmoid(z))).astype(BF)
+
+    each_chunk(tokens, channels, emit)
+
+
+def backward_kernel(
+    dg_ref, y_ref, xc_ref, z_ref, rate_ref, key_ref, query_ref, keep_ref, ksum_ref, wdt_ref, vec_ref, s_ref, before_ref,
+    dz_ref, rest_ref, dq_ref, dk_ref, dnorm_ref, drow_ref, gdt_ref, sums_ref,
+    step, inj, dy, mix, pull, beta, drate, carry, acc_q, acc_k,
+):
+    turn = pl.program_id(1)
+    tokens, channels = xc_ref.shape
     chunks = tokens // CHUNK
-    span = CHUNK * N
-    pick = lax.broadcasted_iota(jnp.int32, (CHUNK, span), 0) == (
-        lax.broadcasted_iota(jnp.int32, (CHUNK, span), 1) // N
+
+    @pl.when(jnp.logical_and(pl.program_id(0) == 0, turn == 0))
+    def _():
+        gdt_ref[...] = jnp.zeros_like(gdt_ref)
+        sums_ref[...] = jnp.zeros_like(sums_ref)
+
+    @pl.when(turn == 0)
+    def _():
+        carry[...] = jnp.zeros_like(carry)
+
+    beta[...] = mm(rate_ref[...], wdt_ref[...], NT)
+
+    def prepare(rows, cols, first):
+        rate_beta = jax.nn.sigmoid(beta[rows, cols] + vec_ref[0:1, cols])
+        eps = rate_beta / (1.0 + rate_beta * wide(ksum_ref, rows, cols.size))
+        beta[rows, cols] = rate_beta
+        step[rows, cols] = eps
+        xc = xc_ref[rows, cols].astype(F32)
+        inj[rows, cols] = eps * xc
+        z = z_ref[rows, cols].astype(F32)
+        sig = jax.nn.sigmoid(z)
+        d_gated = dg_ref[rows, cols]
+        d_y = d_gated * (z * sig)
+        dy[rows, cols] = d_y
+        dz_ref[rows, cols] = (d_gated * y_ref[rows, cols] * (sig * (1.0 + z * (1.0 - sig)))).astype(BF)
+        weighted = d_y * xc
+        sums_ref[8:16, cols] += weighted[0:8] + weighted[8:16]
+
+    each_chunk(tokens, channels, prepare)
+    for tiles in lane_groups(channels):
+        start = tiles[0] == 0
+
+        def chunk(back, carried):
+            k = chunks - 1 - back
+            pulled, now = list(carried[0]), list(carried[1])
+            base = pl.multiple_of(k * CHUNK, CHUNK)
+            steps, injs, dys, keeps, keys, queries = (
+                r.at[pl.ds(base, CHUNK)] for r in (step, inj, dy, keep_ref, key_ref, query_ref)
+            )
+            stacks = [([], []) for _ in tiles]
+            for i in reversed(range(CHUNK)):
+                keep, key, query = token(keys, queries, keeps, i)
+                kept = [keep * key[h] for h in range(2)]
+                ksq = [kept[h] * key[h] for h in range(2)]
+                if i > 0:
+                    before = pl.ds(pl.multiple_of((base + i) * N - N, N), N)
+                else:
+                    before = pl.ds(pl.multiple_of(jnp.maximum(base * N - N, 0), N), N)
+                seen, plain, scaled = [0.0, 0.0], [0.0, 0.0], [0.0, 0.0]
+                for j, lane in enumerate(tiles):
+                    eps, push, d_y = row(steps, i, lane), row(injs, i, lane), row(dys, i, lane)
+                    prior = s_ref[before, pl.ds(lane, LANES)]
+                    if i == 0:
+                        prior = jnp.where(k > 0, prior, before_ref[:, pl.ds(lane, LANES)])
+                    prior = halves(prior.astype(F32))
+                    by_key, by_square = [], []
+                    for h in range(2):
+                        at = 2 * j + h
+                        grad = pulled[at] + d_y * query[h]
+                        pulled[at] = (keep - eps * ksq[h]) * grad
+                        keyed = eps * (grad * key[h])
+                        prod = keyed * prior[h]
+                        seen[h] += now[at] * d_y
+                        plain[h] += grad * push
+                        scaled[h] += prod
+                        by_key.append(keyed)
+                        by_square.append(prod * kept[h])
+                        now[at] = prior[h]
+                    collect(stacks[j][0], by_key[0] + by_key[1], True)
+                    collect(stacks[j][1], by_square[0] + by_square[1], True)
+                    if i % 8 == 0:
+                        rows = pl.ds(pl.multiple_of(base + i, 8), 8)
+                        mix[rows, pl.ds(lane, LANES)] = stacks[j][0].pop()[1]
+                        pull[rows, pl.ds(lane, LANES)] = stacks[j][1].pop()[1]
+                for ref, parts in ((acc_q, seen), (acc_k, [plain[h] - 2.0 * keep * scaled[h] for h in range(2)])):
+                    for h in range(2):
+                        rows = pl.ds(pl.multiple_of((base + i) * N + 8 * h, 8), 8)
+                        if start:
+                            ref[rows, :] = parts[h]
+                        else:
+                            ref[rows, :] += parts[h]
+            return (tuple(pulled), tuple(now))
+
+        now = []
+        for lane in tiles:
+            now += halves(s_ref[tokens * N - N : tokens * N, pl.ds(lane, LANES)].astype(F32))
+        pulled, now = lax.fori_loop(0, chunks, chunk, (load_carry(carry, tiles), tuple(now)))
+        store_carry(carry, tiles, pulled)
+
+    ones = jnp.ones((LANES, LANES), BF)
+    diagonal = lax.broadcasted_iota(jnp.int32, (LANES, LANES), 0) == (
+        lax.broadcasted_iota(jnp.int32, (LANES, LANES), 1)
     )
-
-    def diagonal(left, right):
-        return jnp.sum(jnp.where(pick, mm(left.astype(BF), right, NT), 0.0), axis=0, keepdims=True)
-
-    for first, group in lane_groups(channels):
-        tiles = list(range(first, first + group, LANES))
-        cols = pl.ds(first, group)
-
-        def chunk(turn, pulled):
-            k = chunks - 1 - turn
-            base = pl.multiple_of(k * CHUNK, CHUNK)
-            pulled = list(pulled)
-            steps, dys, keeps = (r.at[pl.ds(base, CHUNK)] for r in (step_ref, dy_ref, keep_ref))
-            for i in reversed(range(CHUNK)):
-                at = base + i
-                keep = row(keeps, i, 0)
-                ksq = [ksq_ref[at, 0:8, :], ksq_ref[at, 8:16, :]]
-                query = [query_ref[at, 0:8, :], query_ref[at, 8:16, :]]
-                for j, lane in enumerate(tiles):
-                    step = row(steps, i, lane)
-                    dy = row(dys, i, lane)
-                    here = []
-                    for h in range(2):
-                        grad = pulled[2 * j + h] + dy * query[h]
-                        pulled[2 * j + h] = (keep - step * ksq[h]) * grad
-                        here.append(grad)
-                    g_buf[i * N : (i + 1) * N, pl.ds(lane, LANES)] = jnp.concatenate(here, axis=0).astype(BF)
-            low = pl.multiple_of(k * span, span)
-            now = s_ref[pl.ds(low, span), cols]
-            grads = g_buf[:, cols]
-            sg_buf[N:span, cols] = g_buf[N:span, cols] * s_ref[pl.ds(low, span - N), cols]
-
-            @pl.when(k == 0)
-            def _():
-                sg_buf[0:N, cols] = g_buf[0:N, cols] * before_ref[:, cols]
-
-            @pl.when(k > 0)
-            def _():
-                prior = s_ref[pl.ds(pl.multiple_of(jnp.maximum(low - N, 0), N), N), cols]
-                sg_buf[0:N, cols] = g_buf[0:N, cols] * prior
-
-            prods = sg_buf[:, cols]
-            here = pl.ds(base, CHUNK)
-            dinj_ref[here, cols] = mm(wk_ref[here, :], grads, NN)
-            pull_ref[here, cols] = mm(wk2_ref[here, :], prods, NN)
-            dq = diagonal(dy_ref[here, cols], now)
-            dk1 = diagonal(inj_ref[here, cols], grads)
-            dk2 = diagonal(step_ref[here, cols], prods)
-            one = pl.ds(k, 1)
-            if first == 0:
-                dq_ref[one, :] = dq
-                dk1_ref[one, :] = dk1
-                dk2_ref[one, :] = dk2
-            else:
-                dq_ref[one, :] += dq
-                dk1_ref[one, :] += dk1
-                dk2_ref[one, :] += dk2
-            return tuple(pulled)
-
-        start = []
-        for lane in tiles:
-            start += [carry[0:8, pl.ds(lane, LANES)], carry[8:16, pl.ds(lane, LANES)]]
-        end = lax.fori_loop(0, chunks, chunk, tuple(start))
-        for j, lane in enumerate(tiles):
-            carry[0:8, pl.ds(lane, LANES)] = end[2 * j]
-            carry[8:16, pl.ds(lane, LANES)] = end[2 * j + 1]
-
-
-def run_forward(seqs, length, step, inj, key_lanes, ksq_lanes, keep_lanes, wq):
-    channels = step.shape[1]
-    block = math.gcd(length, 128)
-    blocks = length // block
+    for out, ref in ((dq_ref, acc_q), (dk_ref, acc_k)):
+        for first in range(0, tokens * N, LANES):
+            sums = mm(ref[first : first + LANES, :].astype(BF), ones, NN)
+            at = first // LANES
+            out[at : at + 1, :] = jnp.sum(jnp.where(diagonal, sums, 0.0), axis=0, keepdims=True)
+
+    def settle(rows, cols, first):
+        rate_beta, eps = beta[rows, cols], step[rows, cols]
+        through = mix[rows, cols]
+        change = through * xc_ref[rows, cols].astype(F32) - pull[rows, cols]
+        inverse = 1.0 / (1.0 + rate_beta * wide(ksum_ref, rows, cols.size))
+        low = (change * inverse * (1.0 - rate_beta)).astype(BF)
+        drate[rows, cols] = low
+        lowered = low.astype(F32)
+        sums_ref[0:8, cols] += lowered[0:8] + lowered[8:16]
+        rest_ref[rows, cols] = through + vec_ref[1:2, cols] * dy[rows, cols]
+        square = change * eps
+        total = square[:, 0:LANES]
+        for lane in range(LANES, cols.size, LANES):
+            total = total + square[:, lane : lane + LANES]
+        if first == 0:
+            dnorm_ref[rows, :] = total
+        else:
+            dnorm_ref[rows, :] += total
+
+    each_chunk(tokens, channels, settle)
+    drow_ref[...] = mm(drate[...], wdt_ref[...], NN)
+    gdt_ref[...] += mm(drate[...], rate_ref[...], TN)
+
+
+def scan_blocks(length):
+    block = math.gcd(length, BLOCK)
+    return block, length // block
+
+
+def row_spec(rows, cols, when, col=0):
+    return pl.BlockSpec((rows, cols), lambda b, t: (when(b, t), col))
+
+
+def spread_spec(block, when):
+    return pl.BlockSpec((block, N, LANES), lambda b, t: (when(b, t), 0, 0))
+
+
+def whole(array):
+    return pl.BlockSpec(array.shape, lambda b, t: (0, 0), pipeline_mode=pl.Buffered(1))
+
+
+def scan_forward(seqs, length, xc, pre, rate, key_lanes, query_lanes, keep_lanes, ksum_lanes, w_dt, vectors):
+    tokens, channels = xc.shape
+    block, blocks = scan_blocks(length)
 
     def at(b, t):
-        return (b * blocks + t, 0)
-
-    def at3(b, t):
-        return (b * blocks + t, 0, 0)
-
-    tokens = seqs * length
+        return b * blocks + t
+
+    rows = row_spec(block, channels, at)
+    lanes = row_spec(block, LANES, at)
+    vmem = pltpu.VMEM
     return pl.pallas_call(
-        scan_forward,
+        forward_kernel,
         grid=(seqs, blocks),
         in_specs=[
-            pl.BlockSpec((block, channels), at),
-            pl.BlockSpec((block, channels), at),
-            pl.BlockSpec((block, N, LANES), at3),
-            pl.BlockSpec((block, N, LANES), at3),
-            pl.BlockSpec((block, LANES), at),
-            pl.BlockSpec((block, CHUNK * N), at),
-        ],
-        out_specs=[
-            pl.BlockSpec((block * N, channels), at),
-            pl.BlockSpec((block, channels), at),
-        ],
+            rows, row_spec(block, channels, at, 1), row_spec(block, R, at),
+            spread_spec(block, at), spread_spec(block, at), lanes, lanes, whole(w_dt), whole(vectors),
+        ],
+        out_specs=[row_spec(block * N, channels, at), rows, rows],
         out_shape=[
             jax.ShapeDtypeStruct((tokens * N, channels), BF),
             jax.ShapeDtypeStruct((tokens, channels), F32),
-        ],
-        scratch_shapes=[pltpu.VMEM((N, channels), F32)],
+            jax.ShapeDtypeStruct((tokens, channels), BF),
+        ],
+        scratch_shapes=[vmem((block, channels), F32), vmem((block, channels), F32), vmem((N, channels), F32)],
         cost_estimate=pl.CostEstimate(
-            flops=tokens * channels * N * 40, bytes_accessed=tokens * channels * 44, transcendentals=0
+            flops=tokens * channels * N * 60, bytes_accessed=tokens * channels * 44, transcendentals=0
         ),
-        compiler_params=pltpu.CompilerParams(vmem_limit_bytes=48 << 20),
+        compiler_params=pltpu.CompilerParams(vmem_limit_bytes=40 << 20),
         name="scan_forward",
-    )(step, inj, key_lanes, ksq_lanes, keep_lanes, wq)
-
-
-def run_backward(seqs, length, step, inj, dy, ksq_lanes, query_lanes, keep_lanes, wk, wk2, states):
-    channels = step.shape[1]
-    block = math.gcd(length, 128)
-    blocks = length // block
+    )(xc, pre, rate, key_lanes, query_lanes, keep_lanes, ksum_lanes, w_dt, vectors)
+
+
+def scan_backward(seqs, length, d_gated, y, xc, pre, rate, key_lanes, query_lanes, keep_lanes, ksum_lanes, w_dt, vectors, states):
+    tokens, channels = xc.shape
+    block, blocks = scan_blocks(length)
 
     def at(b, t):
-        return (b * blocks + blocks - 1 - t, 0)
-
-    def at3(b, t):
-        return (b * blocks + blocks - 1 - t, 0, 0)
+        return b * blocks + blocks - 1 - t
 
     def prior(b, t):
-        return (jnp.maximum((b * blocks + blocks - 1 - t) * block - 1, 0), 0)
-
-    tokens = seqs * length
-    span = CHUNK * N
-    rows = pl.BlockSpec((block, channels), at)
-    lanes = pl.BlockSpec((block, N, LANES), at3)
-    weights = pl.BlockSpec((block, span), at)
-    small = pl.BlockSpec((block // CHUNK, span), at)
+        return (jnp.maximum(at(b, t) * block - 1, 0), 0)
+
+    rows = row_spec(block, channels, at)
+    lanes = row_spec(block, LANES, at)
+    flat = row_spec(block * N // LANES, LANES, at)
+    vmem = pltpu.VMEM
+    wide_f32 = vmem((block, channels), F32)
     return pl.pallas_call(
-        scan_backward,
+        backward_kernel,
         grid=(seqs, blocks),
         in_specs=[
-            rows, rows, rows, lanes, lanes, pl.BlockSpec((block, LANES), at), weights, weights,
-            pl.BlockSpec((block * N, channels), at), pl.BlockSpec((N, channels), prior),
-        ],
-        out_specs=[rows, rows, small, small, small],
-        out_shape=[jax.ShapeDtypeStruct((tokens, channels), F32)] * 2
-        + [jax.ShapeDtypeStruct((tokens // CHUNK, span), F32)] * 3,
+            rows, rows, rows, row_spec(block, channels, at, 1), row_spec(block, R, at),
+            spread_spec(block, at), spread_spec(block, at), lanes, lanes, whole(w_dt), whole(vectors),
+            row_spec(block * N, channels, at), pl.BlockSpec((N, channels), prior),
+        ],
+        out_specs=[
+            rows, rows, flat, flat, lanes, row_spec(block, R, at),
+            pl.BlockSpec((channels, R), lambda b, t: (0, 0)), pl.BlockSpec((16, channels), lambda b, t: (0, 0)),
+        ],
+        out_shape=[
+            jax.ShapeDtypeStruct((tokens, channels), BF),
+            jax.ShapeDtypeStruct((tokens, channels), F32),
+            jax.ShapeDtypeStruct((tokens * N // LANES, LANES), F32),
+            jax.ShapeDtypeStruct((tokens * N // LANES, LANES), F32),
+            jax.ShapeDtypeStruct((tokens, LANES), F32),
+            jax.ShapeDtypeStruct((tokens, R), F32),
+            jax.ShapeDtypeStruct((channels, R), F32),
+            jax.ShapeDtypeStruct((16, channels), F32),
+        ],
         scratch_shapes=[
-            pltpu.VMEM((N, channels), F32),
-            pltpu.VMEM((span, channels), BF),
-            pltpu.VMEM((span, channels), BF),
+            wide_f32, wide_f32, wide_f32, wide_f32, wide_f32, wide_f32, vmem((block, channels), BF),
+            vmem((N, channels), F32), vmem((block * N, LANES), F32), vmem((block * N, LANES), F32),
         ],
         cost_estimate=pl.CostEstimate(
             flops=tokens * channels * N * 100, bytes_accessed=tokens * channels * 56, transcendentals=0
         ),
-        compiler_params=pltpu.CompilerParams(vmem_limit_bytes=56 << 20),
+        compiler_params=pltpu.CompilerParams(vmem_limit_bytes=48 << 20),
         name="scan_backward",
-    )(step, inj, dy, ksq_lanes, query_lanes, keep_lanes, wk, wk2, states, states)
+    )(d_gated, y, xc, pre, rate, key_lanes, query_lanes, keep_lanes, ksum_lanes, w_dt, vectors, states, states)
 
 
 MESH = pl.DeviceIdType.MESH
@@ -650,6 +783,92 @@
     )(d_normed, grad_in_w, packed_grads, gain, hidden_in, cotangent, norm_gain)
 
 
+def reduce_kernel(
+    seq, wide_ref, thin_ref, wide_out, thin_out, wide_x, thin_x, wide_s, thin_s,
+    xw_send, xw_recv, xt_send, xt_recv, sw_send, sw_recv, st_send, st_recv,
+):
+    d, s = place()
+    rows = wide_ref.shape[0] // seq
+    for k in range(1, seq):
+        greet((d, lax.rem(s + k, seq)))
+    pl.semaphore_wait(pltpu.get_barrier_semaphore(), seq - 1)
+
+    def piece(ref, which):
+        return ref.at[pl.ds(pl.multiple_of(which * rows, rows), rows)]
+
+    def ask(k):
+        to = lax.rem(s + k, seq)
+        return (
+            remote(piece(wide_ref, to), wide_x.at[k - 1], xw_send.at[k - 1], xw_recv.at[k - 1], (d, to)),
+            remote(thin_ref.at[to], thin_x.at[k - 1], xt_send.at[k - 1], xt_recv.at[k - 1], (d, to)),
+        )
+
+    def tell(k):
+        to = lax.rem(s + k, seq)
+        return (
+            remote(wide_s, piece(wide_out, s), sw_send.at[k - 1], sw_recv.at[k - 1], (d, to)),
+            remote(thin_s, thin_out.at[s], st_send.at[k - 1], st_recv.at[k - 1], (d, to)),
+        )
+
+    def told(k):
+        source = lax.rem(s - k + seq, seq)
+        return (
+            remote(wide_s, piece(wide_out, source), sw_send.at[k - 1], sw_recv.at[k - 1], (d, s)),
+            remote(thin_s, thin_out.at[source], st_send.at[k - 1], st_recv.at[k - 1], (d, s)),
+        )
+
+    order = sorted(range(1, seq), key=lambda k: -min(k, seq - k))
+    for k in order:
+        for copy in ask(k):
+            copy.start()
+    for k in order:
+        for copy in ask(k):
+            copy.wait_recv()
+    start = pl.ds(pl.multiple_of(s * rows, rows), rows)
+    total = wide_ref[start, :].astype(F32)
+    thin = thin_ref[s]
+    for k in range(seq - 1):
+        total = total + wide_x[k].astype(F32)
+        thin = thin + thin_x[k]
+    wide_s[...] = total.astype(BF)
+    thin_s[...] = thin
+    for k in order:
+        for copy in tell(k):
+            copy.start()
+    wide_out[start, :] = total.astype(BF)
+    thin_out[s] = thin
+    for k in order:
+        for copy in told(k):
+            copy.wait_recv()
+    for k in order:
+        for copy in ask(k) + tell(k):
+            copy.wait_send()
+
+
+def reduce_over_seq(wide_part, thin_part, collective_id):
+    seq = lax.axis_size("seq")
+    tokens, cols = wide_part.shape
+    thin_part = jnp.swapaxes(thin_part.reshape(-1, seq, tokens // seq), 0, 1)
+    dma, vmem = pltpu.SemaphoreType.DMA, pltpu.VMEM
+    here = pl.BlockSpec(memory_space=pltpu.VMEM)
+    rows, few = tokens // seq, thin_part.shape[1:]
+    wide_sum, thin_sum = pl.pallas_call(
+        functools.partial(reduce_kernel, seq),
+        in_specs=[here] * 2,
+        out_specs=[here] * 2,
+        out_shape=[
+            jax.ShapeDtypeStruct((tokens, cols), BF),
+            jax.ShapeDtypeStruct(thin_part.shape, F32),
+        ],
+        scratch_shapes=[
+            vmem((seq - 1, rows, cols), BF), vmem((seq - 1,) + few, F32), vmem((rows, cols), BF), vmem(few, F32),
+        ] + [dma((seq - 1,))] * 8,
+        compiler_params=pltpu.CompilerParams(collective_id=collective_id, has_side_effects=True),
+        name="reduce_seq",
+    )(wide_part.astype(BF), thin_part)
+    return wide_sum, jnp.swapaxes(thin_sum, 0, 1).reshape(-1, tokens)
+
+
 def local(
     hidden_in,
     doc_lengths,
@@ -681,7 +900,8 @@
 
     hidden, w_in, packed = gather(hidden_in, in_weight, packed)
     hidden = hidden.reshape(tokens, width)
-    cot = lax.all_gather(out_cotangent, "seq", axis=1, tiled=True).reshape(tokens, width)
+    cot, hidden = lax.optimization_barrier((out_cotangent, hidden))
+    cot = lax.all_gather(cot, "seq", axis=1, tiled=True).reshape(tokens, width)
 
     w_out = packed[:, :width]
     tail = packed[:, width:]
@@ -700,7 +920,6 @@
     normed = (x_full * inv_rms * gain).astype(BF)
     pre = mm(normed, w_in, NT).astype(BF)
     x_inner = pre[:, :channels].reshape(seqs, length, channels)
-    z_inner = pre[:, channels:].astype(F32)
 
     padded = jnp.pad(x_inner, ((0, 0), (lag_max, 0), (0, 0)))
     conv_sum = jnp.broadcast_to(conv_shift, (seqs, length, channels))
@@ -709,51 +928,31 @@
         conv_sum = conv_sum + jnp.where(valid[w], window * taps[w], 0.0)
     conv_flat = conv_sum.reshape(tokens, channels)
     xc_low = jax.nn.silu(conv_flat).astype(BF)
-    xc = xc_low.astype(F32)
-    proj = lax.psum(mm(xc_low, w_x, NN), "seq")
-    rate = proj[:, :R].astype(BF)
-    key = proj[:, R : R + N]
-    query = proj[:, R + N :]
-    beta = jax.nn.sigmoid(mm(rate, w_dt, NT) + rate_shift)
-    den = 1.0 + beta * jnp.sum(key * key, axis=1, keepdims=True)
-    step = beta / den
-    inj = step * xc
-
-    def lanes(values):
-        return jnp.broadcast_to(values[:, :, None], (tokens, N, LANES))
-
-    ksq = keep * key * key
-    key_lanes, ksq_lanes, query_lanes = lanes(key), lanes(ksq), lanes(query)
+    rate, thin = reduce_over_seq(mm(xc_low, w_x[:, :R], NN), mm(w_x[:, R:], xc_low, ((0,), (1,))), 2)
+    key, query = thin[:N].T, thin[N:].T
+    key_lanes, query_lanes = (
+        jnp.broadcast_to(part.astype(BF)[:, :, None], (tokens, N, LANES)) for part in (key, query)
+    )
+    ksum = jnp.sum(key * key, axis=1, keepdims=True)
     keep_lanes = jnp.broadcast_to(keep, (tokens, LANES))
-    eye = (jnp.arange(tokens)[:, None] % CHUNK == jnp.arange(CHUNK)[None, :]).astype(F32)
-
-    def spread(values):
-        return (values[:, None, :] * eye[:, :, None]).reshape(tokens, CHUNK * N).astype(BF)
-
-    states, mixed = run_forward(seqs, length, step, inj, key_lanes, ksq_lanes, keep_lanes, spread(query))
-    y_full = mixed + skip * xc
-
-    d_gated = mm(cot, w_out, NT)
-    z_gate = jax.nn.silu(z_inner)
-    dy = d_gated * z_gate
-    gated = (y_full * z_gate).astype(BF)
+    ksum_lanes = jnp.broadcast_to(ksum, (tokens, LANES))
+    vectors = jnp.pad(jnp.stack([rate_shift, skip]), ((0, 6), (0, 0)))
+    states, y_full, gated = scan_forward(
+        seqs, length, xc_low, pre, rate, key_lanes, query_lanes, keep_lanes, ksum_lanes, w_dt, vectors
+    )
     branch = mm(gated, w_out, NN).astype(BF).reshape(seqs, length, width)
     branch = lax.psum_scatter(branch, "seq", scatter_dimension=1, tiled=True)
     output = (hidden_in.astype(F32) + branch.astype(F32)).astype(BF)
 
-    d_inj, pull, dq, dk1, dk2 = run_backward(
-        seqs, length, step, inj, dy, ksq_lanes, query_lanes, keep_lanes, spread(key), spread(ksq), states
+    d_z, rest, dq, dk, d_norm, d_row, grad_dt, sums = scan_backward(
+        seqs, length, mm(cot, w_out, NT), y_full, xc_low, pre, rate, key_lanes, query_lanes, keep_lanes, ksum_lanes, w_dt, vectors, states
     )
-    dq, dk1, dk2 = dq.reshape(tokens, N), dk1.reshape(tokens, N), dk2.reshape(tokens, N)
-    d_z = d_gated * y_full * silu_slope(z_inner)
-    d_step = d_inj * xc - pull
-    den_square = den * den
-    d_norm = -jnp.sum(d_step * beta * beta / den_square, axis=1, keepdims=True)
-    d_keys = dk1 - 2.0 * keep * key * dk2 + 2.0 * key * d_norm
-    d_rate = (d_step / den_square * beta * (1.0 - beta)).astype(BF)
-    d_proj = jnp.concatenate([mm(d_rate, w_dt, NN), d_keys, dq], axis=1)
-    d_proj = lax.psum(d_proj, "seq").astype(BF)
-    d_conv_out = mm(d_proj, w_x, NT) + step * d_inj + skip * dy
+    dq, dk = dq.reshape(tokens, N), dk.reshape(tokens, N)
+    d_norm = -jnp.sum(d_norm, axis=1, keepdims=True)
+    d_keys = dk + 2.0 * key * d_norm
+    d_row, thin = reduce_over_seq(d_row, jnp.concatenate([d_keys.T, dq.T], axis=0), 3)
+    d_proj = jnp.concatenate([d_row, thin.T.astype(BF)], axis=1)
+    d_conv_out = mm(d_proj, w_x, NT) + rest
     d_conv = (d_conv_out * silu_slope(conv_flat)).reshape(seqs, length, channels)
 
     tap_grads = []
@@ -764,19 +963,19 @@
         masked = jnp.where(valid[w], d_conv, 0.0)
         tap_grads.append(jnp.sum(masked * window, axis=(0, 1)))
         d_x_inner = d_x_inner + jnp.pad(masked, ((0, 0), (0, lag), (0, 0)))[:, lag:, :] * taps[w]
-    d_pre = jnp.concatenate([d_x_inner.reshape(tokens, channels), d_z], axis=1).astype(BF)
+    d_pre = jnp.concatenate([d_x_inner.reshape(tokens, channels).astype(BF), d_z], axis=1)
 
     grad_w_out = mm(gated, cot, TN)
     vector_grads = jnp.stack(
         tap_grads
         + [
             jnp.sum(d_conv, axis=(0, 1)),
-            jnp.sum(d_rate.astype(F32), axis=0),
-            jnp.sum(dy * xc, axis=0),
+            jnp.sum(sums[:8], axis=0),
+            jnp.sum(sums[8:], axis=0),
         ],
         axis=1,
     )
-    small_grads = jnp.concatenate([mm(xc_low, d_proj, TN), mm(d_rate, rate, TN), vector_grads], axis=1)
+    small_grads = jnp.concatenate([mm(xc_low, d_proj, TN), grad_dt, vector_grads], axis=1)
     packed_grads = jnp.concatenate([grad_w_out, jnp.pad(small_grads, ((0, 0), (0, padded_cols - used)))], axis=1)
     d_normed = mm(d_pre, w_in, NN)
     gain_local = jnp.sum(d_normed * x_full * inv_rms, axis=0)

time: 618 us -> 561 us (0.908)
  Pallas kernels: 317 us -> 372 us
  waiting for transfers between devices: 44.9 us -> 0.04 us
  blocking collectives: 28.2 us -> 0 us
  matrix products: 90.6 us -> 75.9 us
  other arithmetic: 40.9 us -> 29.8 us
  starting transfers between devices: 10.6 us -> 0.08 us
    pallas_call x2 -> x4, Pallas kernels: 112 us -> 177 us  [the longest x2 77 us: reduce_over_seq(): pl.pallas_call(functools.partial(reduce_kernel, seq), in_specs=[here] * 2...]
    psum x1 -> x0, waiting for transfers between devices: 32.6 us -> none  [local(): proj = lax.psum(mm(xc_low, w_x, NN), 'seq')]
    psum x1 -> x0, blocking collectives: 28.2 us -> none  [local(): d_proj = lax.psum(d_proj, 'seq').astype(BF)]
    dot_general x12 -> x10, matrix products: 90.6 us -> 75.9 us  [mm(): lax.dot_general(left, right, (dims, ((), ())), preferred_element_type=F32)]
    all_gather x1, waiting for transfers between devices: 11.5 us -> 0.01 us  [local(): cot = lax.all_gather(cot, 'seq', axis=1, tiled=True).reshape(tokens, width)]
    reduce_scatter x1, starting transfers between devices: 10.6 us -> 0.04 us  [local(): branch = lax.psum_scatter(branch, 'seq', scatter_dimension=1, tiled=True)]
    broadcast_in_dim x3, local copies, waits for them, and re-layouts: 17.6 us -> 7.93 us  [the longest x2 7.74 us: local(): jnp.broadcast_to(part.astype(BF)[:, :, None], (tokens, N, LANES))]
    pallas_call x1, Pallas kernels: 124 us -> 115 us  [scatter(): pl.pallas_call(functools.partial(scatter_kernel, dp, seq), in_specs=any_s...]
  transfers between devices with their start and end apart: 3 -> 2, of which waited for: 2 -> 0; matrix products, arithmetic and copies ran while one was open for 17% -> 26% of each run, Pallas kernels for 26% -> 53%
where the time goes in v4:
time: 561 us; the launch traced here: 551 us
  Pallas kernels  372 us (66%)
  matrix products  75.9 us (14%)
  local copies, waits for them, and re-layouts  58.1 us (10%)
  other arithmetic  29.8 us (5%)
  between operations  14.8 us (3%)
    pallas_call x1, Pallas kernels, scatter(): pl.pallas_call(functools.partial(scatter_kernel, dp, seq), in_specs=any_s...  115 us
    pallas_call x1, Pallas kernels, gather(): pl.pallas_call(functools.partial(gather_kernel, dp, seq), in_specs=any_sp...  80.7 us
    pallas_call x2, Pallas kernels, reduce_over_seq(): pl.pallas_call(functools.partial(reduce_kernel, seq), in_specs=[here] * 2...  77 us
    dot_general x10, matrix products, mm(): lax.dot_general(left, right, (dims, ((), ())), preferred_element_type=F32)  75.9 us
    pallas_call x1, Pallas kernels, scan_backward(): pl.pallas_call(backward_kernel, grid=(seqs, blocks), in_specs=[rows, rows...  67.2 us
    pallas_call x1, Pallas kernels, scan_forward(): pl.pallas_call(forward_kernel, grid=(seqs, blocks), in_specs=[rows, row_s...  32.5 us
    unnamed x73, local copies, waits for them, and re-layouts  18.3 us
  transfers between devices with their start and end apart: 2, of which 0 were waited for; matrix products, arithmetic and copies ran while one was open for 26% of the time, Pallas kernels for 53%

profile of v4, /device:TPU:9, one launch (start us, length us, event | category | flops | bytes accessed | tf_op | source)
XLA Modules:
  0.0 550.9 jit_solution(17218019539565680924)
XLA Ops:
  14.1 80.7 %gather_in.1 = (bf16[1,1024,2048]{2,1,0:T(8,128)(2,1)}, bf16[2048,2048]{1,0:T(8,128)(2,1)}, bf16[1024,2432]{1,0:T(8,128)(2,1)}) custom-call(bf16[1,256,2048]{2,1,0:T(8,128)(2,1)} %hid_ref.3, bf16[256,2048]{1,0:T(8,128)(2,1)} %w_ref.1, bf16[128,2432]{1,0:T(8,128)(2,1)} %fusion.50.pk_ref), custom_call_target="tpu_custom_call" | custom-call | tf_op jit(solution)/shard_map/gather_in/pallas_call | solution.py:549
  94.9 7.6 %copy.90 = bf16[1024,2432]{0,1:T(8,128)(2,1)} copy(bf16[1024,2432]{1,0:T(8,128)(2,1)} %get-tuple-element.35) | data formatting | bytes 9961472 | tf_op jit(solution)/shard_map/gather_in/pallas_call | solution.py:549
  104.5 3.1 fusion.1
  107.9 13.2 %convolution_convert_fusion.1.z_ref = bf16[1024,2048]{1,0:T(8,128)(2,1)S(1)} fusion(bf16[2048,2048]{1,0:T(8,128)(2,1)} %get-tuple-element.38, bf16[1024,2048]{1,0:T(8,128)(2,1)} %bitcast.118, f32[2048]{0:T(1024)S(1)} %convert_element_type.119, f32[1024]{0:T(1024)S(1)} %add_rsqrt_fusion), kind=kOutput, calls=%fused_computation.64 | convolution fusion | flops 8600420352 | bytes 16789504 | tf_op jit(solution)/shard_map/dot_general | solution.py:38
  121.4 4.9 fusion.34
  126.4 2.7 convolution_convert_fusion.3.wide_ref
  129.0 2.8 fusion.49.thin_ref
  131.9 53.0 %reduce_seq.2 = (bf16[1024,128]{1,0:T(8,128)(2,1)}, f32[4,32,256]{2,1,0:T(8,128)}) custom-call(bf16[1024,128]{1,0:T(8,128)(2,1)} %convolution_convert_fusion.3.wide_ref, f32[4,32,256]{2,1,0:T(8,128)} %fusion.49.thin_ref), custom_call_target="tpu_custom_call" | custom-call | tf_op jit(solution)/shard_map/reduce_seq/pallas_call | solution.py:855
  187.0 3.9 broadcast_in_dim.125.key_ref
  190.9 3.9 broadcast_in_dim.126.query_ref
  195.2 32.5 %scan_forward.1 = (bf16[16384,1024]{1,0:T(8,128)(2,1)}, f32[1024,1024]{1,0:T(8,128)S(1)}, bf16[1024,1024]{1,0:T(8,128)(2,1)S(1)}) custom-call(bf16[1024,1024]{1,0:T(8,128)(2,1)S(1)} %get-tuple-element.116.xc_ref, bf16[1024,2048]{1,0:T(8,128)(2,1)S(1)} %copy-done.1, bf16[1024,128]{1,0:T(8,128)(2,1)S(1)} %copy-done.5, ...), custom_call_target="tpu_custom_call" | custom-call | flops 1006632960 | bytes 46137344 | tf_op jit(solution)/shard_map/scan_forward/pallas_call | solution.py:320
  230.9 6.2 %convert_bitcast_fusion.1 = bf16[1,1024,2048]{2,1,0:T(8,128)(2,1)} fusion(bf16[1024,1024]{1,0:T(8,128)(2,1)S(1)} %get-tuple-element.41, bf16[1024,2432]{1,0:T(8,128)(2,1)S(1)} %bitcast.116), kind=kOutput, calls=%fused_computation.62 | convolution fusion | flops 4297064448 | bytes 10485760 | tf_op jit(solution)/shard_map/dot_general | solution.py:38
  237.8 10.0 %fusion.29.dg_ref = f32[1024,1024]{1,0:T(8,128)} fusion(bf16[1,1024,2048]{2,1,0:T(8,128)(2,1)} %all-gather.2.cloned.1.call-done, bf16[1024,2432]{1,0:T(8,128)(2,1)} %get-tuple-element.35), kind=kOutput, calls=%fused_computation.46 | convolution fusion | flops 4294967296 | bytes 12582912 | tf_op jit(solution)/shard_map/dot_general | solution.py:38
  247.8 67.2 %scan_backward.1 = (bf16[1024,1024]{1,0:T(8,128)(2,1)S(1)}, f32[1024,1024]{1,0:T(8,128)}, f32[128,128]{1,0:T(8,128)S(1)}, f32[128,128]{1,0:T(8,128)S(1)}, f32[10...) custom-call(f32[1024,1024]{1,0:T(8,128)} %fusion.29.dg_ref, ...), custom_call_target="tpu_custom_call" | custom-call | flops 1677721600 | bytes 58720256 | tf_op jit(solution)/shard_map/scan_backward/pallas_call | solution.py:357
  323.4 24.1 %reduce_seq.3 = (bf16[1024,128]{1,0:T(8,128)(2,1)}, f32[4,32,256]{2,1,0:T(8,128)}) custom-call(bf16[1024,128]{1,0:T(8,128)(2,1)} %convert_element_type.137.wide_ref, f32[4,32,256]{2,1,0:T(8,128)} %bitcast.124), custom_call_target="tpu_custom_call" | custom-call | tf_op jit(solution)/shard_map/reduce_seq/pallas_call | solution.py:855
  350.3 6.8 %fusion.64 = (bf16[1024]{0:T(1024)(128)(2,1)S(1)}, bf16[1024]{0:T(1024)(128)(2,1)S(1)}, f32[1024,1024]{1,0:T(8,128)S(1)}) fusion(bf16[1024,2048]{1,0:T(8,128)(2,1)} %copy-done, pred[1024]{0:T(1024)(128)(4,1)S(1)} %get-tuple-element.128, f32[1,1024,1024]{2,1,0:T(8,128)} %copy-done.21, f32[1024,1024]{1,0:T(8,128)} %get-tuple-element.51, ...), kind=kOutput, calls=%fused_computation.117 | convolution fusion | flops 350877696 | bytes 15537152 | tf_op jit(solution)/shard_map/dot_general | solution.py:38
  357.2 3.3 fusion.23
  367.6 3.9 fusion.44
  371.5 13.6 %fusion.5 = (f32[2048]{0:T(1024)S(1)}, bf16[1,1024,2048]{2,1,0:T(8,128)(2,1)}) fusion(bf16[1024,2048]{1,0:T(8,128)(2,1)S(1)} %bitcast.119, f32[1024]{0:T(1024)S(1)} %copy-done.28, bf16[2048,2048]{1,0:T(8,128)(2,1)} %get-tuple-element.38, bf16[1024,1024]{1,0:T(8,128)(2,1)S(1)} %copy-done.14, bf16[1024,1024]{1,0:T(8,128)(2,1)} %fusion.44), kind=kOutput, calls=%fused_computation.9 | convolution fusion | flops 8608806912 | bytes 20983808 | tf_op jit(solution)/shard_map/dot_general | solution.py:38
  385.7 2.9 concatenate.28
  388.6 7.0 %fusion.38 = bf16[1024,2048]{1,0:T(8,128)(2,1)S(1)} fusion(bf16[1024,1024]{1,0:T(8,128)(2,1)S(1)} %copy-done.12, bf16[1,1024,2048]{2,1,0:T(8,128)(2,1)} %all-gather.2.cloned.1.call-done), kind=kOutput, calls=%fused_computation.65 | convolution fusion | flops 4297064448 | bytes 10485760 | tf_op jit(solution)/shard_map/dot_general | solution.py:38
  395.7 3.0 fusion.6.pk_ref
  400.9 12.0 %convolution_convert_fusion.gw_ref = bf16[2048,2048]{1,0:T(8,128)(2,1)} fusion(bf16[1024,1024]{1,0:T(8,128)(2,1)S(1)} %copy-done.15, bf16[1024,1024]{1,0:T(8,128)(2,1)S(1)} %copy-done.23, bf16[1024,2048]{1,0:T(8,128)(2,1)S(1)} %bitcast.120, f32[2048]{0:T(1024)S(1)} %convert_element_type.119, f32[1024]{0:T(1024)S(1)} %copy-done.28), kind=kOutput, calls=%fused_computation.10 | convolution fusion | flops 8610906112 | bytes 16789504 | tf_op jit(solution)/shard_map/dot_general | solution.py:38
  412.9 114.6 %scatter_out.1 = (bf16[1,256,2048]{2,1,0:T(8,128)(2,1)}, f32[256,2048]{1,0:T(8,128)}, bf16[128,2432]{1,0:T(8,128)(2,1)}, f32[8,256]{1,0:T(8,128)}) custom-call(bf16[1,1024,2048]{2,1,0:T(8,128)(2,1)} %get-tuple-element.119.dn_ref, bf16[2048,2048]{1,0:T(8,128)(2,1)} %convolution_convert_fusion.gw_ref, bf16[1024,2432]{1,0:T(8,128)(2,1)} %fusion.6.pk_ref, ...), custom_call_target="tpu_custom_call" | custom-call | tf_op jit(solution)/shard_map/scatter_out/pallas_call | solution.py:757
  (136 shorter events, 53.2 us)
Async XLA Ops:
  7.2 230.6 %all-gather.2.cloned.1.call-start = ((), (), s32[]{:S(2)}) async-start(), calls=%async_computation.2 | async-start | bytes 5242880 | tf_op jit(solution)/shard_map/all_gather | solution.py:904
  94.8 442.8 %reduce-scatter.2.cloned.1.call-start = ((), (), s32[]{:S(2)}) async-start(), calls=%async_computation.1 | async-start | bytes 5242880 | tf_op jit(solution)/shard_map/reduce_scatter | solution.py:944
  102.5 5.0 copy-start.25
  102.5 5.1 copy-start.29
  107.9 13.2 %copy-start.27 = (f32[1024]{0:T(1024)}, f32[1024]{0:T(1024)S(1)}, u32[]{:S(2)}) copy-start(f32[1024]{0:T(1024)S(1)} %add_rsqrt_fusion) | copy-start | bytes 12292
  121.1 5.2 copy-start
  121.4 4.9 copy-start.16
  126.3 68.8 %copy-start.2 = (bf16[1024,1024]{1,0:T(8,128)(2,1)}, bf16[1024,1024]{1,0:T(8,128)(2,1)S(1)}, u32[]{:S(2)}) copy-start(bf16[1024,1024]{1,0:T(8,128)(2,1)S(1)} %get-tuple-element.116.xc_ref) | copy-start | bytes 6291460
  187.0 8.2 %copy-start.1 = (bf16[1024,2048]{1,0:T(8,128)(2,1)S(1)}, bf16[1024,2048]{1,0:T(8,128)(2,1)}, u32[]{:S(2)}) copy-start(bf16[1024,2048]{1,0:T(8,128)(2,1)} %copy-done) | copy-start | bytes 12582916
  187.0 8.2 %copy-start.5 = (bf16[1024,128]{1,0:T(8,128)(2,1)S(1)}, bf16[1024,128]{1,0:T(8,128)(2,1)}, u32[]{:S(2)}) copy-start(bf16[1024,128]{1,0:T(8,128)(2,1)} %get-tuple-element.39.rate_ref) | copy-start | bytes 786436
  190.9 40.1 %slice-start = ((s8[4980736]{0:T(1024)(128)(4,1)}), s8[4194304]{0:T(1024)(128)(4,1)S(1)}, s32[]{:S(2)}) async-start(s8[4980736]{0:T(1024)(128)(4,1)} %bitcast.115), calls=%async_computation.3 | async-start | bytes 8388608
  195.2 35.8 %slice-start.1 = ((s8[4980736]{0:T(1024)(128)(4,1)}), s8[786432]{0:T(1024)(128)(4,1)S(1)}, s32[]{:S(2)}) async-start(s8[4980736]{0:T(1024)(128)(4,1)} %bitcast.115), calls=%async_computation.4 | async-start | bytes 1572864
  237.8 10.0 %copy-start.6 = (bf16[1024,128]{1,0:T(8,128)(2,1)S(1)}, bf16[1024,128]{1,0:T(8,128)(2,1)}, u32[]{:S(2)}) copy-start(bf16[1024,128]{1,0:T(8,128)(2,1)} %get-tuple-element.39.rate_ref) | copy-start | bytes 786436
  318.8 29.8 %copy-start.3 = (bf16[1024,1024]{1,0:T(8,128)(2,1)S(1)}, bf16[1024,1024]{1,0:T(8,128)(2,1)}, u32[]{:S(2)}) copy-start(bf16[1024,1024]{1,0:T(8,128)(2,1)} %copy-done.2) | copy-start | bytes 6291460
  350.3 6.8 %copy-start.17 = (bf16[1,1024,1024]{2,1,0:T(8,128)(2,1)S(1)}, bf16[1,1024,1024]{2,1,0:T(8,128)(2,1)}, u32[]{:S(2)}) copy-start(bf16[1,1024,1024]{2,1,0:T(8,128)(2,1)} %copy-done.16) | copy-start | bytes 6291460
  357.2 9.7 %copy-start.8 = (f32[1024,128]{1,0:T(8,128)S(1)}, f32[1024,128]{1,0:T(8,128)}, u32[]{:S(2)}) copy-start(f32[1024,128]{1,0:T(8,128)} %copy-done.7) | copy-start | bytes 1572868
  367.6 3.9 copy-start.28
  371.5 17.1 %copy-start.12 = (bf16[1024,1024]{1,0:T(8,128)(2,1)S(1)}, bf16[1024,1024]{1,0:T(8,128)(2,1)}, u32[]{:S(2)}) copy-start(bf16[1024,1024]{1,0:T(8,128)(2,1)} %copy-done.11) | copy-start | bytes 6291460
  395.7 4.6 copy-start.20
  395.7 5.2 copy-start.23
  527.5 7.8 %copy-start.26 = (f32[8,256]{1,0:T(8,128)S(1)}, f32[8,256]{1,0:T(8,128)}, u32[]{:S(2)}) copy-start(f32[8,256]{1,0:T(8,128)} %get-tuple-element.56) | copy-start | bytes 24580
  527.5 10.1 %copy-start.18 = (bf16[1,256,2048]{2,1,0:T(8,128)(2,1)S(1)}, bf16[1,256,2048]{2,1,0:T(8,128)(2,1)}, u32[]{:S(2)}) copy-start(bf16[1,256,2048]{2,1,0:T(8,128)(2,1)} %hid_ref.3) | copy-start | bytes 3145732
  528.8 5.0 copy-start.24
  528.8 13.7 %copy-start.22 = (f32[256,2048]{1,0:T(8,128)S(1)}, f32[256,2048]{1,0:T(8,128)}, u32[]{:S(2)}) copy-start(f32[256,2048]{1,0:T(8,128)} %get-tuple-element.147) | copy-start | bytes 6291460
  (10 other events, 20.5 us)
Sparse Core Ops, SparseCore 0:
  95.0 98.6 all-gather.1
  237.3 77.3 reduce-scatter.1

commit v5 on v4

--- a/solution.py
+++ b/solution.py
@@ -403,6 +403,14 @@
     return d + 1 - 2 * lax.rem(d, 2)
 
 
+def forward_home(d, s, seq):
+    return 2 * (d // 2) + lax.rem(s, 2), (seq // 2) * lax.rem(d, 2) + s // 2
+
+
+def backward_home(d, s, seq):
+    return 2 * (d // 2) + s // (seq // 2), 2 * lax.rem(s, seq // 2) + lax.rem(d, 2)
+
+
 def remote(src, dst, send, recv, device):
     return pltpu.make_async_remote_copy(
         src_ref=src, dst_ref=dst, send_sem=send, recv_sem=recv, device_id=device, device_id_type=MESH
@@ -421,19 +429,31 @@
         pl.when(here)(tell)
 
 
-def gather_kernel(
-    dp, seq, hid_ref, w_ref, pk_ref, hid_out, w_out, pk_out,
-    z_send, z_recv, w_send, w_recv, f_send, f_recv, p_send, p_recv, q_send, q_recv, t_sem, own_sem,
-):
+PARTS = 4
+
+
+def gather_kernel(dp, seq, fused, *refs):
+    refs = list(refs)
+
+    def take(count):
+        out = refs[:count]
+        del refs[:count]
+        return out
+
+    hid_ref, w_ref = take(2)
+    parts = take(PARTS)
+    gain_ref = take(1)[0] if fused else None
+    hid_out, w_out = take(2)
+    slots = take(PARTS)
+    normed_out, pre_out = take(2) if fused else (None, None)
+    z_send, z_recv, w_send, w_recv, f_send, f_recv, p_send, p_recv, q_send, q_recv, t_send, t_recv, own_sem = take(13)
     d, s = place()
     part = hid_ref.shape[1]
-    w_rows, p_rows = w_ref.shape[0], pk_ref.shape[0]
     pieces = z_send.shape[2]
     piece = part // pieces
-    half = seq // 2
     pairs = dp // 2
-    to_d, to_s = 2 * (d // 2) + lax.rem(s, 2), half * lax.rem(d, 2) + s // 2
-    from_d, from_s = 2 * (d // 2) + s // half, 2 * lax.rem(s, half) + lax.rem(d, 2)
+    to_d, to_s = forward_home(d, s, seq)
+    from_d, from_s = backward_home(d, s, seq)
     moves = jnp.logical_or(to_d != d, to_s != s)
 
     greet((d, s - 1), s > 0)
@@ -460,110 +480,172 @@
             return jnp.logical_and(s - k >= 0, s < seq - 1)
         return jnp.logical_and(s + k < seq, s > 0)
 
-    def w_slot(which):
-        return w_out.at[pl.ds(which * w_rows, w_rows)]
-
-    def p_slot(which):
-        return pk_out.at[pl.ds(which * p_rows, p_rows)]
-
-    def spread(slot, own, send, recv, k):
-        return remote(own, slot(d), send.at[k], recv.at[k], (lax.rem(d + 2 * k, dp), s))
+    def landed(way, k, q):
+        which = jnp.where(way == 0, s - k, s + k)
+        here = shard(which, q)
+        remote(here, here, z_send.at[way, k - 1, q], z_recv.at[way, k - 1, q], (d, s)).wait_recv()
+
+    def spread(out, own, send, recv, k):
+        return remote(own, out.at[d], send.at[k], recv.at[k], (lax.rem(d + 2 * k, dp), s))
 
     def source(k):
         return lax.rem(d - 2 * k + dp, dp)
 
-    def across(slot, send, recv, k, own=None):
-        return remote(own if k == 0 else slot(source(k)), slot(source(k)), send.at[k], recv.at[k], (mate(d), s))
+    def across(out, send, recv, k, own=None):
+        return remote(own if k == 0 else out.at[source(k)], out.at[source(k)], send.at[k], recv.at[k], (mate(d), s))
 
     for q in range(pieces):
         for way in range(2):
             pl.when(can_send(way, 0))(hop(way, 0, q).start)
-    transfer = remote(pk_ref, p_slot(to_d), t_sem.at[0], t_sem.at[1], (to_d, to_s))
-    stay = pltpu.make_async_copy(pk_ref, p_slot(d), own_sem.at[2])
-    pl.when(moves)(transfer.start)
-    pl.when(jnp.logical_not(moves))(stay.start)
+    transfers = [remote(parts[m], slots[m].at[to_d], t_send.at[m], t_recv.at[m], (to_d, to_s)) for m in range(PARTS)]
+    stays = [pltpu.make_async_copy(parts[m], slots[m].at[d], own_sem.at[2 + m]) for m in range(PARTS)]
+    for m in range(PARTS):
+        pl.when(moves)(transfers[m].start)
+        pl.when(jnp.logical_not(moves))(stays[m].start)
     for k in range(1, pairs):
-        spread(w_slot, w_ref, w_send, w_recv, k).start()
-    across(w_slot, f_send, f_recv, 0, w_ref).start()
-    own_w = pltpu.make_async_copy(w_ref, w_slot(d), own_sem.at[0])
+        spread(w_out, w_ref, w_send, w_recv, k).start()
+    across(w_out, f_send, f_recv, 0, w_ref).start()
+    own_w = pltpu.make_async_copy(w_ref, w_out.at[d], own_sem.at[0])
     own_h = pltpu.make_async_copy(hid_ref, hid_out.at[:, pl.ds(s * part, part), :], own_sem.at[1])
     own_w.start()
     own_h.start()
 
-    pl.when(moves)(remote(pk_ref, p_slot(d), t_sem.at[0], t_sem.at[1], (to_d, to_s)).wait_recv)
-    pl.when(jnp.logical_not(moves))(stay.wait)
-    for k in range(1, pairs):
-        spread(p_slot, p_slot(d), p_send, p_recv, k).start()
-    across(p_slot, q_send, q_recv, 0, p_slot(d)).start()
-
-    def arrive(k):
+    for m in range(PARTS):
+        slot = slots[m].at[d]
+        pl.when(moves)(remote(parts[m], slot, t_send.at[m], t_recv.at[m], (to_d, to_s)).wait_recv)
+        pl.when(jnp.logical_not(moves))(stays[m].wait)
+        for k in range(1, pairs):
+            spread(slots[m], slot, p_send.at[m], p_recv.at[m], k).start()
+        across(slots[m], q_send.at[m], q_recv.at[m], 0, slot).start()
+
+    for k in range(1, seq - 1):
         for q in range(pieces):
             for way in range(2):
-                got = s - k >= 0 if way == 0 else s + k < seq
-
-                @pl.when(got)
-                def _():
-                    which = s - k if way == 0 else s + k
-                    remote(
-                        shard(which, q), shard(which, q), z_send.at[way, k - 1, q], z_recv.at[way, k - 1, q], (d, s)
-                    ).wait_recv()
-
-                if k < seq - 1:
-                    pl.when(can_send(way, k))(hop(way, k, q).start)
-
-    for k in range(1, seq - 1):
-        arrive(k)
-    for slot, own, send, recv, over_send, over_recv in (
-        (w_slot, w_ref, w_send, w_recv, f_send, f_recv),
-        (p_slot, None, p_send, p_recv, q_send, q_recv),
-    ):
+                pl.when(s - k >= 0 if way == 0 else s + k < seq)(functools.partial(landed, way, k, q))
+                pl.when(can_send(way, k))(hop(way, k, q).start)
+    own_w.wait()
+    own_h.wait()
+    flows = [(w_out, w_ref, w_send, w_recv, f_send, f_recv)]
+    flows += [
+        (slots[m], slots[m].at[d], p_send.at[m], p_recv.at[m], q_send.at[m], q_recv.at[m]) for m in range(PARTS)
+    ]
+    for out, own, send, recv, over_send, over_recv in flows:
         for k in range(1, pairs):
-            remote(slot(source(k)), slot(source(k)), send.at[k], recv.at[k], (d, s)).wait_recv()
-            across(slot, over_send, over_recv, k).start()
-    arrive(seq - 1)
-
-    def other(k):
-        return lax.rem(mate(d) - 2 * k + dp, dp)
-
-    for slot, own, over_send, over_recv in ((w_slot, w_ref, f_send, f_recv), (p_slot, p_slot(d), q_send, q_recv)):
+            here = out.at[source(k)]
+            remote(here, here, send.at[k], recv.at[k], (d, s)).wait_recv()
+            across(out, over_send, over_recv, k).start()
+    for out, own, send, recv, over_send, over_recv in flows:
         for k in range(pairs):
-            remote(slot(other(k)), slot(other(k)), over_send.at[k], over_recv.at[k], (d, s)).wait_recv()
-            across(slot, over_send, over_recv, k, own).wait_send()
-    for k in range(1, pairs):
-        spread(w_slot, w_ref, w_send, w_recv, k).wait_send()
-        spread(p_slot, p_slot(d), p_send, p_recv, k).wait_send()
+            here = out.at[lax.rem(mate(d) - 2 * k + dp, dp)]
+            remote(here, here, over_send.at[k], over_recv.at[k], (d, s)).wait_recv()
+
+    last = seq - 1
+    if fused:
+        w_all, x_buf, w_sem, x_sem = take(4)
+        width, columns = x_buf.shape[1], pre_out.shape[1]
+        cut = math.gcd(columns, 512)
+        fetch_w = pltpu.make_async_copy(w_out, w_all, w_sem)
+        fetch_w.start()
+        fetch_w.wait()
+
+        def project(which, k, way):
+            here = pl.multiple_of(which * part, part)
+            for q in range(pieces):
+                pl.when(k == last)(functools.partial(landed, way, last, q))
+                fetch = pltpu.make_async_copy(
+                    hid_out.at[0, pl.ds(which * part + q * piece, piece)], x_buf.at[pl.ds(q * piece, piece)], x_sem
+                )
+                fetch.start()
+                fetch.wait()
+                x = x_buf[pl.ds(q * piece, piece), :].astype(F32)
+                inv = lax.rsqrt(jnp.mean(x * x, axis=1, keepdims=True) + norm_eps)
+                rows = pl.ds(pl.multiple_of(here + q * piece, piece), piece)
+                normed_out[rows, :] = (x * inv * gain_ref[...].astype(F32)).astype(BF)
+
+            def matmul(at, carried):
+                cols = pl.ds(pl.multiple_of(at * cut, cut), cut)
+                w_rows = w_all.shape[1]
+                block = w_all[pl.ds(at * (cut // w_rows), cut // w_rows)].reshape(cut, width)
+                pre_out[pl.ds(here, part), cols] = mm(normed_out[pl.ds(here, part), :], block, NT).astype(BF)
+                return carried
+
+            lax.fori_loop(0, columns // cut, matmul, 0)
+
+        def visit(m, carried):
+            k = (m + 1) // 2
+            way = lax.rem(m, 2)
+            which = jnp.where(way == 0, s - k, s + k)
+
+            @pl.when(jnp.logical_and(which >= 0, which < seq))
+            def _():
+                project(which, k, way)
+
+            return carried
+
+        lax.fori_loop(0, 2 * seq - 1, visit, 0)
+    else:
+        for q in range(pieces):
+            for way in range(2):
+                pl.when(s - last >= 0 if way == 0 else s + last < seq)(functools.partial(landed, way, last, q))
+
+    for out, own, send, recv, over_send, over_recv in flows:
+        for k in range(pairs):
+            across(out, over_send, over_recv, k, own).wait_send()
+        for k in range(1, pairs):
+            spread(out, own, send, recv, k).wait_send()
     for k in range(seq - 1):
         for q in range(pieces):
             for way in range(2):
                 pl.when(can_send(way, k))(hop(way, k, q).wait_send)
-    pl.when(moves)(transfer.wait_send)
-    own_w.wait()
-    own_h.wait()
-
-
-def gather(hidden, weight, packed, collective_id=0):
+    for m in range(PARTS):
+        pl.when(moves)(transfers[m].wait_send)
+
+
+def fits_whole(seqs, length, width, channels):
+    return seqs == 1 and length % 256 == 0 and length * (width + channels) + channels * width <= 6 << 20
+
+
+def gather(hidden, weight, parts, norm_gain, collective_id=0):
     dp, seq = lax.axis_size("dp"), lax.axis_size("seq")
     seqs, part, width = hidden.shape
+    columns = weight.shape[0] * dp
+    fused = fits_whole(seqs, part * seq, width, columns // 2)
     pieces = 4 if part % 64 == 0 else 1
-    dma = pltpu.SemaphoreType.DMA
-    return pl.pallas_call(
-        functools.partial(gather_kernel, dp, seq),
-        in_specs=any_specs(3),
-        out_specs=any_specs(3),
-        out_shape=[
-            jax.ShapeDtypeStruct((seqs, part * seq, width), hidden.dtype),
-            jax.ShapeDtypeStruct((weight.shape[0] * dp, weight.shape[1]), weight.dtype),
-            jax.ShapeDtypeStruct((packed.shape[0] * dp, packed.shape[1]), packed.dtype),
-        ],
-        scratch_shapes=[
-            dma((2, seq, pieces)), dma((2, seq, pieces)),
-            dma((dp // 2,)), dma((dp // 2,)), dma((dp // 2,)), dma((dp // 2,)),
-            dma((dp // 2,)), dma((dp // 2,)), dma((dp // 2,)), dma((dp // 2,)),
-            dma((2,)), dma((3,)),
-        ],
-        compiler_params=pltpu.CompilerParams(collective_id=collective_id, has_side_effects=True),
+    dma, vmem, pairs = pltpu.SemaphoreType.DMA, pltpu.VMEM, dp // 2
+    shape = jax.ShapeDtypeStruct
+    outs = [shape((seqs, part * seq, width), BF), shape((dp,) + weight.shape, BF)]
+    outs += [shape((dp,) + member.shape, BF) for member in parts]
+    scratch = [dma((2, seq, pieces)), dma((2, seq, pieces))] + [dma((pairs,))] * 4
+    scratch += [dma((PARTS, pairs))] * 4 + [dma((PARTS,)), dma((PARTS,)), dma((2 + PARTS,))]
+    ins, in_specs = [hidden, weight, *parts], any_specs(2 + PARTS)
+    out_specs = any_specs(2 + PARTS)
+    if fused:
+        ins.append(norm_gain.reshape(1, width))
+        in_specs = in_specs + [pl.BlockSpec(memory_space=pltpu.VMEM)]
+        outs += [shape((part * seq, width), BF), shape((part * seq, columns), BF)]
+        scratch += [
+            vmem((dp,) + weight.shape, BF), vmem((part, width), BF), dma, dma,
+        ]
+        out_specs = out_specs + [pl.BlockSpec(memory_space=pltpu.VMEM)] * 2
+    out = pl.pallas_call(
+        functools.partial(gather_kernel, dp, seq, fused),
+        in_specs=in_specs,
+        out_specs=out_specs,
+        out_shape=outs,
+        scratch_shapes=scratch,
+        compiler_params=pltpu.CompilerParams(
+            collective_id=collective_id, has_side_effects=True, vmem_limit_bytes=32 << 20
+        ),
         name="gather_in",
-    )(hidden, weight, packed)
+    )(*ins)
+    hidden = out[0].reshape(-1, width)
+    w_in = out[1].reshape(columns, width)
+    if fused:
+        return hidden, w_in, out[2 : 2 + PARTS], out[-2], out[-1]
+    x = hidden.astype(F32)
+    inv = lax.rsqrt(jnp.mean(x * x, axis=1, keepdims=True) + norm_eps)
+    normed = (x * inv * norm_gain.astype(F32)).astype(BF)
+    return hidden, w_in, out[2:], normed, mm(normed, w_in, NT).astype(BF)
 
 
 def added(ref, *others):
@@ -573,22 +655,38 @@
     return total
 
 
-def scatter_kernel(
-    dp, seq, dn_ref, gw_ref, pk_ref, gain_ref, hid_ref, cot_ref, scale_ref,
-    out_ref, gw_out, pk_out, gain_out,
-    own, come, gw_own, gw_x, gw_r, pk_own, pk_x, pk_r, pk_fin, g_x, g_r, g_z, g_a, g_b,
-    load, z_send, z_recv, w_load, wx_send, wx_recv, w_send, w_recv,
-    p_load, px_send, px_recv, p_send, p_recv, t_sem, gx_sem, g_send, g_recv, gz_send, gz_recv,
-):
+def scatter_kernel(dp, seq, count, fused, *refs):
+    refs = list(refs)
+
+    def take(count):
+        out = refs[:count]
+        del refs[:count]
+        return out
+
+    if fused:
+        dx_ref, dz_ref, normed_ref, w_ref, full_ref = take(5)
+        dn_ref = gw_ref = None
+    else:
+        dn_ref, gw_ref, gain_ref = take(3)
+    parts = take(count)
+    hid_ref, cot_ref, scale_ref = take(3)
+    out_ref, gw_out = take(2)
+    part_outs = take(count)
+    gain_out = take(1)[0]
+    own, come, gw_own, gw_x, gw_r = take(5)
+    p_own, p_x, p_r, p_fin = take(count), take(count), take(count), take(count)
+    g_in, g_x, g_r, g_z, g_a, g_b = take(6)
+    z_load, z_send, z_recv, w_load, wx_send, wx_recv, w_send, w_recv = take(8)
+    p_load, px_send, px_recv, p_send, p_recv, t_send, t_recv, gx_sem, g_send, g_recv, gz_send, gz_recv = take(12)
+
     d, s = place()
     seqs, part, width = out_ref.shape
     pieces = z_send.shape[1]
     piece = part // pieces
-    half = seq // 2
     pairs = dp // 2
     mine, odd = d // 2, lax.rem(d, 2)
-    to_d, to_s = 2 * (d // 2) + s // half, 2 * lax.rem(s, half) + lax.rem(d, 2)
-    from_d, from_s = 2 * (d // 2) + lax.rem(s, 2), half * lax.rem(d, 2) + s // 2
+    to_d, to_s = backward_home(d, s, seq)
+    from_d, from_s = forward_home(d, s, seq)
     moves = jnp.logical_or(to_d != d, to_s != s)
 
     for k in range(1, seq):
@@ -600,34 +698,108 @@
     greet((from_d, from_s), moves)
     pl.semaphore_wait(pltpu.get_barrier_semaphore(), seq - 1 + pairs + jnp.where(moves, 2, 0))
 
-    def swap(src_ref, dst, send, recv, j):
-        rows = dst.shape[1]
-        other = 2 * j + 1 - odd
-        return remote(src_ref.at[pl.ds(other * rows, rows)], dst.at[j], send.at[j], recv.at[j], (mate(d), s))
-
-    def fetch(src_ref, dst, sem, j):
-        rows = dst.shape[1]
-        return pltpu.make_async_copy(src_ref.at[pl.ds((2 * j + odd) * rows, rows)], dst.at[j], sem.at[j])
-
-    def chunk(r):
-        return pltpu.make_async_copy(dn_ref.at[:, pl.ds(r * part, part), :], own.at[r], load.at[r])
-
-    gain_swap = remote(gain_ref, g_x, gx_sem.at[0], gx_sem.at[1], (mate(d), s))
-    gain_swap.start()
-    for j in range(pairs):
-        swap(pk_ref, pk_x, px_send, px_recv, j).start()
-    ends = []
-    for i in range(seq):
-        ends.append(seq - 1 - i // 2 if i % 2 == 0 else i // 2)
-    for r in ends:
-        chunk(r).start()
-    for j in range(pairs):
-        fetch(pk_ref, pk_own, p_load, j).start()
-    for j in range(pairs):
-        swap(gw_ref, gw_x, wx_send, wx_recv, j).start()
-        fetch(gw_ref, gw_own, w_load, j).start()
-    for r in ends:
-        chunk(r).wait()
+    def swap(src, dst, send, recv, j):
+        return remote(src, dst.at[j], send.at[j], recv.at[j], (mate(d), s))
+
+    def part_swap(m, j):
+        return swap(parts[m].at[2 * j + 1 - odd], p_x[m], px_send.at[m], px_recv.at[m], j)
+
+    def part_fetch(m, j):
+        return pltpu.make_async_copy(parts[m].at[2 * j + odd], p_own[m].at[j], p_load.at[m, j])
+
+    for m in range(count):
+        for j in range(pairs):
+            part_swap(m, j).start()
+            part_fetch(m, j).start()
+
+    if fused:
+        d_pre, normed, w_all, x_buf, gw_give, f_sem, x_sem = take(7)
+        channels = dx_ref.shape[1]
+        loads = [
+            pltpu.make_async_copy(dx_ref, d_pre.at[:, pl.ds(0, channels)], f_sem.at[0]),
+            pltpu.make_async_copy(dz_ref, d_pre.at[:, pl.ds(channels, channels)], f_sem.at[1]),
+            pltpu.make_async_copy(w_ref, w_all, f_sem.at[2]),
+            pltpu.make_async_copy(normed_ref, normed, f_sem.at[3]),
+        ]
+        for copy in loads:
+            copy.start()
+        for copy in loads[:3]:
+            copy.wait()
+        g_in[...] = jnp.zeros_like(g_in)
+        w_rows = gw_own.shape[1]
+        half_width = width // 2
+
+        def dn_tasks(first, last):
+            def run(i, carried):
+                r = jnp.where(lax.rem(i, 2) == 0, seq - 1 - i // 2, i // 2)
+                rows = pl.ds(pl.multiple_of(r * part, part), part)
+                fetch = pltpu.make_async_copy(full_ref.at[rows], x_buf, x_sem)
+                fetch.start()
+                for at in range(2):
+                    cols = pl.ds(at * half_width, half_width)
+                    own[r, 0, :, cols] = mm(d_pre[rows, :], w_all[:, cols], NN).astype(BF)
+                fetch.wait()
+
+                def fold(at, carried):
+                    some = pl.ds(pl.multiple_of(at * 64, 64), 64)
+                    x = x_buf[some, :].astype(F32)
+                    inv = lax.rsqrt(jnp.mean(x * x, axis=1, keepdims=True) + norm_eps)
+                    weighted = own[r, 0, some, :].astype(F32) * (x * inv)
+                    g_in[...] += jnp.sum(weighted.reshape(8, 8, width), axis=0)
+                    return carried
+
+                return lax.fori_loop(0, part // 64, fold, carried)
+
+            lax.fori_loop(first, last, run, 0)
+
+        def gw_task(dest, out, j):
+            cols = pl.ds(pl.multiple_of(dest * w_rows, w_rows), w_rows)
+            for at in range(2):
+                some = pl.ds(at * half_width, half_width)
+                out[j, :, some] = mm(d_pre[:, cols], normed[:, some], TN).astype(BF)
+
+        def gw_swap(j):
+            return swap(gw_give.at[j], gw_x, wx_send, wx_recv, j)
+
+        def gw_away():
+            def run(j, carried):
+                gw_task(2 * j + 1 - odd, gw_give, j)
+                gw_swap(j).start()
+                return carried
+
+            lax.fori_loop(0, pairs, run, 0)
+
+        def gw_home():
+            def run(k, carried):
+                j = lax.rem(mine + 1 + k, pairs)
+                gw_task(2 * j + odd, gw_own, j)
+                return carried
+
+            lax.fori_loop(0, pairs, run, 0)
+
+        def gw_ready(j):
+            pass
+    else:
+        def gw_swap(j):
+            return swap(gw_ref.at[2 * j + 1 - odd], gw_x, wx_send, wx_recv, j)
+
+        def gw_fetch(j):
+            return pltpu.make_async_copy(gw_ref.at[2 * j + odd], gw_own.at[j], w_load.at[j])
+
+        def chunk(r):
+            return pltpu.make_async_copy(dn_ref.at[:, pl.ds(r * part, part), :], own.at[r], z_load.at[r])
+
+        for r in range(seq):
+            chunk(r).start()
+        for j in range(pairs):
+            gw_swap(j).start()
+            gw_fetch(j).start()
+        for r in range(seq):
+            chunk(r).wait()
+        g_in[...] = gain_ref[...]
+
+        def gw_ready(j):
+            gw_fetch(j).wait()
 
     def give(way, r, q):
         rows = pl.ds(q * piece, piece)
@@ -640,43 +812,66 @@
         here = come.at[slot, :, rows, :]
         remote(here, here, z_send.at[0, q], z_recv.at[slot, q], (d, s)).wait_recv()
 
-    def pass_on(way, r):
+    def send(way, r, q):
+        before = r + 1 if way == 0 else r - 1
+        if 0 <= before < seq:
+            give(way, before, q).wait_send()
+        give(way, r, q).start()
+
+    def begin():
+        for q in range(pieces):
+            pl.when(s == 0)(give(0, seq - 1, q).start)
+            pl.when(s == seq - 1)(give(1, 0, q).start)
+
+    def pass_on(way, r, q):
         first = s == 0 if way == 0 else s == seq - 1
         sends = s < r if way == 0 else s > r
-        for q in range(pieces):
-            @pl.when(jnp.logical_and(sends, jnp.logical_not(first)))
-            def _():
-                rows = pl.ds(q * piece, piece)
-                landed(r, q)
-                own[r, :, rows, :] = added(own.at[r, :, rows, :], come.at[r, :, rows, :]).astype(BF)
-
-            pl.when(sends)(give(way, r, q).start)
-
-    def round_of(i):
-        pass_on(0, seq - 1 - i)
-        pass_on(1, i)
+        begun = r == (seq - 1 if way == 0 else 0)
+
+        @pl.when(jnp.logical_and(sends, jnp.logical_not(first)))
+        def _():
+            rows = pl.ds(q * piece, piece)
+            landed(r, q)
+            own[r, :, rows, :] = added(own.at[r, :, rows, :], come.at[r, :, rows, :]).astype(BF)
+            send(way, r, q)
+
+        if not begun:
+            pl.when(jnp.logical_and(sends, first))(functools.partial(send, way, r, q))
+
+    def hop(i, q):
+        pass_on(0, seq - 1 - i, q)
+        pass_on(1, i, q)
 
     def onward(part_own, part_r, send, recv, k):
         j = lax.rem(mine + k, pairs)
         return remote(part_own.at[j], part_r.at[k - 1], send.at[k], recv.at[k], (lax.rem(d + 2 * k, dp), s))
 
-    def join(src_ref, part_own, part_x, part_r, sem, xs, xr, send, recv):
+    def part_onward(m, k):
+        return onward(p_own[m], p_r[m], p_send.at[m], p_recv.at[m], k)
+
+    def gw_onward(k):
+        return onward(gw_own, gw_r, w_send, w_recv, k)
+
+    def part_join():
+        for m in range(count):
+            for k in range(1, pairs + 1):
+                j = lax.rem(mine + k, pairs)
+                part_fetch(m, j).wait()
+                part_swap(m, j).wait_recv()
+                if k < pairs:
+                    p_own[m][j] = added(p_own[m].at[j], p_x[m].at[j]).astype(BF)
+                    part_onward(m, k).start()
+
+    def gw_join():
         for k in range(1, pairs + 1):
             j = lax.rem(mine + k, pairs)
-            fetch(src_ref, part_own, sem, j).wait()
-            swap(src_ref, part_x, xs, xr, j).wait_recv()
+            gw_ready(j)
+            gw_swap(j).wait_recv()
             if k < pairs:
-                part_own[j] = added(part_own.at[j], part_x.at[j]).astype(BF)
-                onward(part_own, part_r, send, recv, k).start()
-
-    def finish(part_own, part_x, part_r, send, recv):
-        for k in range(1, pairs):
-            onward(part_own, part_r, send, recv, k).wait_recv()
-        return added(part_own.at[mine], part_x.at[mine], *[part_r.at[k] for k in range(pairs - 1)])
-
-    round_of(0) if seq == 2 else None
-    gain_swap.wait_recv()
-    g_a[...] = gain_ref[...] + g_x[...]
+                gw_own[j] = added(gw_own.at[j], gw_x.at[j]).astype(BF)
+                gw_onward(k).start()
+
+    gain_swap = remote(g_in, g_x, gx_sem.at[0], gx_sem.at[1], (mate(d), s))
 
     def gain_near(k):
         return remote(g_a, g_r.at[k - 1], g_send.at[k], g_recv.at[k], (lax.rem(d + 2 * k, dp), s))
@@ -684,114 +879,192 @@
     def gain_far(k):
         return remote(g_b, g_z.at[k - 1], gz_send.at[k], gz_recv.at[k], (d, lax.rem(s + k, seq)))
 
+    def gain_middle():
+        gain_swap.wait_recv()
+        g_a[...] = g_in[...] + g_x[...]
+        for k in range(1, pairs):
+            gain_near(k).start()
+
+    def gain_last():
+        for k in range(1, pairs):
+            gain_near(k).wait_recv()
+        g_b[...] = added(g_a, *[g_r.at[k] for k in range(pairs - 1)])
+        for k in range(1, seq):
+            gain_far(k).start()
+
+    backs = [remote(p_fin[m], part_outs[m], t_send.at[m], t_recv.at[m], (to_d, to_s)) for m in range(count)]
+    stays = [pltpu.make_async_copy(p_fin[m], part_outs[m], t_send.at[count + m]) for m in range(count)]
+
+    def part_finish():
+        for m in range(count):
+            for k in range(1, pairs):
+                part_onward(m, k).wait_recv()
+            rest = [p_r[m].at[k] for k in range(pairs - 1)]
+            p_fin[m][...] = added(p_own[m].at[mine], p_x[m].at[mine], *rest).astype(BF)
+            pl.when(moves)(backs[m].start)
+            pl.when(jnp.logical_not(moves))(stays[m].start)
+
+    if fused:
+        dn_tasks(0, 2)
+        begin()
+        part_join()
+        loads[3].wait()
+        gw_away()
+        dn_tasks(2, seq)
+        gain_swap.start()
+        gw_home()
+    else:
+        begin()
+        part_join()
+        gain_swap.start()
+    gw_join()
+    later = [gain_middle, gain_last, part_finish]
+    for i in range(seq - 1):
+        for q in range(pieces):
+            hop(i, q)
+            if later and q == pieces - 1:
+                later.pop(0)()
+    for task in later:
+        task()
+
     for k in range(1, pairs):
-        gain_near(k).start()
-    join(pk_ref, pk_own, pk_x, pk_r, p_load, px_send, px_recv, p_send, p_recv)
-    if seq > 2:
-        round_of(0)
-    join(gw_ref, gw_own, gw_x, gw_r, w_load, wx_send, wx_recv, w_send, w_recv)
-    for k in range(1, pairs):
-        gain_near(k).wait_recv()
-    g_b[...] = added(g_a, *[g_r.at[k] for k in range(pairs - 1)])
-    for k in range(1, seq):
-        gain_far(k).start()
-    for i in range(1, seq - 2):
-        round_of(i)
-    pk_fin[...] = finish(pk_own, pk_x, pk_r, p_send, p_recv).astype(BF)
-    back = remote(pk_fin, pk_out, t_sem.at[0], t_sem.at[1], (to_d, to_s))
-    stay = pltpu.make_async_copy(pk_fin, pk_out, t_sem.at[2])
-    pl.when(moves)(back.start)
-    pl.when(jnp.logical_not(moves))(stay.start)
-    if seq > 2:
-        round_of(seq - 2)
-    gw_out[...] = finish(gw_own, gw_x, gw_r, w_send, w_recv)
+        gw_onward(k).wait_recv()
+    gw_out[...] = added(gw_own.at[mine], gw_x.at[mine], *[gw_r.at[k] for k in range(pairs - 1)])
     for k in range(1, seq):
         gain_far(k).wait_recv()
     gain_out[...] = added(g_b, *[g_z.at[k] for k in range(seq - 1)])
 
+    some = math.gcd(piece, 64)
     for q in range(pieces):
         pl.when(s > 0)(functools.partial(landed, s, q))
         pl.when(s < seq - 1)(functools.partial(landed, seq, q))
-        rows = pl.ds(q * piece, piece)
-        from_left = jnp.where(s > 0, come[s, :, rows, :].astype(F32), 0.0)
-        from_right = jnp.where(s < seq - 1, come[seq, :, rows, :].astype(F32), 0.0)
-        total = own[s, :, rows, :].astype(F32) + from_left + from_right
-        x = hid_ref[:, rows, :].astype(F32)
-        inv = lax.rsqrt(jnp.mean(x * x, axis=2, keepdims=True) + norm_eps)
-        scaled = total * scale_ref[...].astype(F32)[None]
-        out_ref[:, rows, :] = (
-            cot_ref[:, rows, :].astype(F32)
-            + inv * scaled
-            - x * (inv * inv * inv) * jnp.mean(x * scaled, axis=2, keepdims=True)
-        ).astype(BF)
+
+        def settle(at, carried):
+            rows = pl.ds(pl.multiple_of(q * piece + at * some, some), some)
+            from_left = jnp.where(s > 0, come[s, :, rows, :].astype(F32), 0.0)
+            from_right = jnp.where(s < seq - 1, come[seq, :, rows, :].astype(F32), 0.0)
+            total = own[s, :, rows, :].astype(F32) + from_left + from_right
+            x = hid_ref[:, rows, :].astype(F32)
+            inv = lax.rsqrt(jnp.mean(x * x, axis=2, keepdims=True) + norm_eps)
+            scaled = total * scale_ref[...].astype(F32)[None]
+            out_ref[:, rows, :] = (
+                cot_ref[:, rows, :].astype(F32)
+                + inv * scaled
+                - x * (inv * inv * inv) * jnp.mean(x * scaled, axis=2, keepdims=True)
+            ).astype(BF)
+            return carried
+
+        lax.fori_loop(0, piece // some, settle, 0)
 
     for q in range(pieces):
-        for r in range(1, seq):
-            pl.when(s < r)(give(0, r, q).wait_send)
-        for r in range(seq - 1):
-            pl.when(s > r)(give(1, r, q).wait_send)
+        pl.when(s < seq - 1)(give(0, s + 1, q).wait_send)
+        pl.when(s > 0)(give(1, s - 1, q).wait_send)
     gain_swap.wait_send()
     for j in range(pairs):
-        swap(pk_ref, pk_x, px_send, px_recv, j).wait_send()
-        swap(gw_ref, gw_x, wx_send, wx_recv, j).wait_send()
+        gw_swap(j).wait_send()
+        for m in range(count):
+            part_swap(m, j).wait_send()
     for k in range(1, pairs):
-        onward(pk_own, pk_r, p_send, p_recv, k).wait_send()
-        onward(gw_own, gw_r, w_send, w_recv, k).wait_send()
+        gw_onward(k).wait_send()
         gain_near(k).wait_send()
+        for m in range(count):
+            part_onward(m, k).wait_send()
     for k in range(1, seq):
         gain_far(k).wait_send()
-    pl.when(moves)(back.wait_send)
-    pl.when(moves)(remote(pk_fin, pk_out, t_sem.at[0], t_sem.at[1], (to_d, to_s)).wait_recv)
-    pl.when(jnp.logical_not(moves))(stay.wait)
-
-
-def scatter(d_normed, grad_in_w, packed_grads, gain, hidden_in, cotangent, norm_gain, collective_id=1):
+    for m in range(count):
+        pl.when(moves)(backs[m].wait_send)
+        pl.when(moves)(remote(p_fin[m], part_outs[m], t_send.at[m], t_recv.at[m], (to_d, to_s)).wait_recv)
+        pl.when(jnp.logical_not(moves))(stays[m].wait)
+
+
+def scatter(d_x, d_z, normed, w_in, hidden, parts, hidden_in, cotangent, norm_gain, collective_id=1):
     dp, seq = lax.axis_size("dp"), lax.axis_size("seq")
     seqs, part, width = hidden_in.shape
-    w_rows, p_rows = grad_in_w.shape[0] // dp, packed_grads.shape[0] // dp
-    cols = packed_grads.shape[1]
+    tokens, channels = d_x.shape
+    w_rows = 2 * channels // dp
+    fused = fits_whole(seqs, part * seq, width, channels)
     pieces = 4 if part % 64 == 0 else 1
-    pairs = dp // 2
-    dma, vmem = pltpu.SemaphoreType.DMA, pltpu.VMEM
+    pairs, count = dp // 2, len(parts)
+    dma, vmem, shape = pltpu.SemaphoreType.DMA, pltpu.VMEM, jax.ShapeDtypeStruct
     here = pl.BlockSpec(memory_space=pltpu.VMEM)
-    return pl.pallas_call(
-        functools.partial(scatter_kernel, dp, seq),
-        in_specs=any_specs(3) + [here] * 4,
-        out_specs=[here] * 4,
-        out_shape=[
-            jax.ShapeDtypeStruct((seqs, part, width), BF),
-            jax.ShapeDtypeStruct((w_rows, width), F32),
-            jax.ShapeDtypeStruct((p_rows, cols), BF),
-            jax.ShapeDtypeStruct(gain.shape, F32),
-        ],
+    if fused:
+        ins, in_specs = [d_x, d_z, normed, w_in, hidden], any_specs(5)
+        extra = [
+            vmem((tokens, 2 * channels), BF), vmem((tokens, width), BF), vmem((2 * channels, width), BF),
+            vmem((part, width), BF), vmem((pairs, w_rows, width), BF), dma((4,)), dma,
+        ]
+        gain_shape = (8, width)
+    else:
+        d_pre = jnp.concatenate([d_x, d_z], axis=1)
+        x = hidden.astype(F32)
+        d_normed = mm(d_pre, w_in, NN)
+        inv = lax.rsqrt(jnp.mean(x * x, axis=1, keepdims=True) + norm_eps)
+        gain = jnp.sum(d_normed * x * inv, axis=0).reshape(8, -1)
+        ins = [
+            d_normed.astype(BF).reshape(seqs, -1, width),
+            mm(d_pre, normed, TN).astype(BF).reshape(dp, w_rows, width), gain,
+        ]
+        in_specs, extra = any_specs(2) + [here], []
+        gain_shape = gain.shape
+    part_shapes = [member.shape[1:] for member in parts]
+    token_shape = (seqs, part, width)
+
+    def each(count):
+        return [vmem((count,) + member, BF) for member in part_shapes]
+
+    out = pl.pallas_call(
+        functools.partial(scatter_kernel, dp, seq, len(parts), fused),
+        in_specs=in_specs + any_specs(count) + [here] * 3,
+        out_specs=[here] * (3 + count),
+        out_shape=[shape(token_shape, BF), shape((w_rows, width), F32)]
+        + [shape(member, BF) for member in part_shapes]
+        + [shape(gain_shape, F32)],
         scratch_shapes=[
-            vmem((seq, seqs, part, width), BF), vmem((seq + 1, seqs, part, width), BF),
+            vmem((seq,) + token_shape, BF), vmem((seq + 1,) + token_shape, BF),
             vmem((pairs, w_rows, width), BF), vmem((pairs, w_rows, width), BF), vmem((pairs - 1, w_rows, width), BF),
-            vmem((pairs, p_rows, cols), BF), vmem((pairs, p_rows, cols), BF), vmem((pairs - 1, p_rows, cols), BF),
-            vmem((p_rows, cols), BF),
-            vmem(gain.shape, F32), vmem((pairs - 1,) + gain.shape, F32), vmem((seq - 1,) + gain.shape, F32),
-            vmem(gain.shape, F32), vmem(gain.shape, F32),
+            *each(pairs), *each(pairs), *each(pairs - 1), *[vmem(member, BF) for member in part_shapes],
+            vmem(gain_shape, F32), vmem(gain_shape, F32), vmem((pairs - 1,) + gain_shape, F32),
+            vmem((seq - 1,) + gain_shape, F32), vmem(gain_shape, F32), vmem(gain_shape, F32),
             dma((seq,)), dma((seq, pieces)), dma((seq + 1, pieces)),
             dma((pairs,)), dma((pairs,)), dma((pairs,)), dma((pairs,)), dma((pairs,)),
-            dma((pairs,)), dma((pairs,)), dma((pairs,)), dma((pairs,)), dma((pairs,)),
-            dma((3,)), dma((2,)), dma((pairs,)), dma((pairs,)), dma((seq,)), dma((seq,)),
+            *[dma((count, pairs))] * 5, dma((2 * count,)), dma((count,)),
+            dma((2,)), dma((pairs,)), dma((pairs,)), dma((seq,)), dma((seq,)),
+            *extra,
         ],
         compiler_params=pltpu.CompilerParams(
-            collective_id=collective_id, has_side_effects=True, vmem_limit_bytes=60 << 20
+            collective_id=collective_id, has_side_effects=True, vmem_limit_bytes=63 << 20
         ),
         name="scatter_out",
-    )(d_normed, grad_in_w, packed_grads, gain, hidden_in, cotangent, norm_gain)
-
-
-def reduce_kernel(
-    seq, wide_ref, thin_ref, wide_out, thin_out, wide_x, thin_x, wide_s, thin_s,
-    xw_send, xw_recv, xt_send, xt_recv, sw_send, sw_recv, st_send, st_recv,
-):
+    )(*ins, *parts, hidden_in, cotangent, norm_gain.reshape(1, width))
+    gain = jnp.sum(out[-1], axis=0) if fused else out[-1].reshape(width)
+    return out[0], out[1], out[2 : 2 + count], gain
+
+
+def reduce_kernel(dp, seq, grads, *refs):
+    refs = list(refs)
+
+    def take(count):
+        out = refs[:count]
+        del refs[:count]
+        return out
+
+    wide_ref, thin_ref = take(2)
+    g_ref = take(1)[0] if grads else None
+    wide_out, thin_out = take(2)
+    g_out = take(1)[0] if grads else None
+    wide_x, thin_x, wide_s, thin_s = take(4)
+    xw_send, xw_recv, xt_send, xt_recv, sw_send, sw_recv, st_send, st_recv = take(8)
     d, s = place()
     rows = wide_ref.shape[0] // seq
+    pairs = dp // 2
+    mine, odd = d // 2, lax.rem(d, 2)
     for k in range(1, seq):
         greet((d, lax.rem(s + k, seq)))
-    pl.semaphore_wait(pltpu.get_barrier_semaphore(), seq - 1)
+    if grads:
+        for k in range(1, pairs):
+            greet((lax.rem(d + 2 * k, dp), s))
+        greet((mate(d), s))
+    pl.semaphore_wait(pltpu.get_barrier_semaphore(), seq - 1 + (pairs if grads else 0))
 
     def piece(ref, which):
         return ref.at[pl.ds(pl.multiple_of(which * rows, rows), rows)]
@@ -821,6 +1094,29 @@
     for k in order:
         for copy in ask(k):
             copy.start()
+    if grads:
+        g_own, g_x, g_r, g_load, gx_send, gx_recv, g_send, g_recv = take(8)
+
+        def swap(j):
+            return remote(g_ref.at[2 * j + 1 - odd], g_x.at[j], gx_send.at[j], gx_recv.at[j], (mate(d), s))
+
+        def fetch(j):
+            return pltpu.make_async_copy(g_ref.at[2 * j + odd], g_own.at[j], g_load.at[j])
+
+        def onward(k):
+            to = lax.rem(d + 2 * k, dp)
+            return remote(g_own.at[to // 2], g_r.at[k - 1], g_send.at[k], g_recv.at[k], (to, s))
+
+        for j in range(pairs):
+            swap(j).start()
+            fetch(j).start()
+        for k in range(1, pairs + 1):
+            j = lax.rem(mine + k, pairs)
+            fetch(j).wait()
+            swap(j).wait_recv()
+            if k < pairs:
+                g_own[j] = added(g_own.at[j], g_x.at[j]).astype(BF)
+                onward(k).start()
     for k in order:
         for copy in ask(k):
             copy.wait_recv()
@@ -837,6 +1133,14 @@
             copy.start()
     wide_out[start, :] = total.astype(BF)
     thin_out[s] = thin
+    if grads:
+        for k in range(1, pairs):
+            onward(k).wait_recv()
+        g_out[...] = added(g_own.at[mine], g_x.at[mine], *[g_r.at[k] for k in range(pairs - 1)]).astype(BF)
+        for j in range(pairs):
+            swap(j).wait_send()
+        for k in range(1, pairs):
+            onward(k).wait_send()
     for k in order:
         for copy in told(k):
             copy.wait_recv()
@@ -845,28 +1149,44 @@
             copy.wait_send()
 
 
-def reduce_over_seq(wide_part, thin_part, collective_id):
-    seq = lax.axis_size("seq")
+def reduce_over_seq(wide_part, thin_part, collective_id, grads=None):
+    dp, seq = lax.axis_size("dp"), lax.axis_size("seq")
     tokens, cols = wide_part.shape
     thin_part = jnp.swapaxes(thin_part.reshape(-1, seq, tokens // seq), 0, 1)
-    dma, vmem = pltpu.SemaphoreType.DMA, pltpu.VMEM
+    dma, vmem, shape = pltpu.SemaphoreType.DMA, pltpu.VMEM, jax.ShapeDtypeStruct
     here = pl.BlockSpec(memory_space=pltpu.VMEM)
-    rows, few = tokens // seq, thin_part.shape[1:]
-    wide_sum, thin_sum = pl.pallas_call(
-        functools.partial(reduce_kernel, seq),
-        in_specs=[here] * 2,
-        out_specs=[here] * 2,
-        out_shape=[
-            jax.ShapeDtypeStruct((tokens, cols), BF),
-            jax.ShapeDtypeStruct(thin_part.shape, F32),
-        ],
-        scratch_shapes=[
-            vmem((seq - 1, rows, cols), BF), vmem((seq - 1,) + few, F32), vmem((rows, cols), BF), vmem(few, F32),
-        ] + [dma((seq - 1,))] * 8,
-        compiler_params=pltpu.CompilerParams(collective_id=collective_id, has_side_effects=True),
+    rows, few, pairs = tokens // seq, thin_part.shape[1:], dp // 2
+    ins, in_specs = [wide_part.astype(BF), thin_part], [here] * 2
+    outs = [shape((tokens, cols), BF), shape(thin_part.shape, F32)]
+    scratch = [
+        vmem((seq - 1, rows, cols), BF), vmem((seq - 1,) + few, F32), vmem((rows, cols), BF), vmem(few, F32),
+    ] + [dma((seq - 1,))] * 8
+    if grads is not None:
+        ins, in_specs = ins + [grads], in_specs + any_specs(1)
+        outs.append(shape(grads.shape[1:], BF))
+        scratch += [vmem((pairs,) + grads.shape[1:], BF)] * 2 + [vmem((pairs - 1,) + grads.shape[1:], BF)]
+        scratch += [dma((pairs,))] * 5
+    out = pl.pallas_call(
+        functools.partial(reduce_kernel, dp, seq, grads is not None),
+        in_specs=in_specs,
+        out_specs=[here] * len(outs),
+        out_shape=outs,
+        scratch_shapes=scratch,
+        compiler_params=pltpu.CompilerParams(
+            collective_id=collective_id, has_side_effects=True, vmem_limit_bytes=24 << 20
+        ),
         name="reduce_seq",
-    )(wide_part.astype(BF), thin_part)
-    return wide_sum, jnp.swapaxes(thin_sum, 0, 1).reshape(-1, tokens)
+    )(*ins)
+    return (out[0], jnp.swapaxes(out[1], 0, 1).reshape(-1, tokens)) + tuple(out[2:])
+
+
+def homes_back(dp, seq):
+    pairs = []
+    for d in range(dp):
+        for s in range(seq):
+            home_d, home_s = 2 * (d // 2) + s % 2, (seq // 2) * (d % 2) + s // 2
+            pairs.append((home_d * seq + home_s, d * seq + s))
+    return pairs
 
 
 def local(
@@ -891,34 +1211,21 @@
     channels = rows * dp
     lag_max = KCONV - 1
 
-    small = jnp.concatenate(
-        [x_weight, dt_weight, conv_weight.T, conv_bias[:, None], dt_bias[:, None], skip_gain[:, None]], axis=1
-    )
-    used = small.shape[1]
-    padded_cols = -(-used // LANES) * LANES
-    packed = jnp.concatenate([out_weight, jnp.pad(small, ((0, 0), (0, padded_cols - used)))], axis=1)
-
-    hidden, w_in, packed = gather(hidden_in, in_weight, packed)
-    hidden = hidden.reshape(tokens, width)
-    cot, hidden = lax.optimization_barrier((out_cotangent, hidden))
+    vectors = [conv_weight, conv_bias[None], dt_bias[None], skip_gain[None]]
+    vectors = jnp.pad(jnp.concatenate(vectors, axis=0), ((0, 16 - KCONV - 3), (0, 0)))
+    parts = [out_weight, x_weight, dt_weight, vectors]
+    hidden, w_in, parts, normed, pre = gather(hidden_in, in_weight, parts, norm_gain)
+    cot, pre = lax.optimization_barrier((out_cotangent, pre))
     cot = lax.all_gather(cot, "seq", axis=1, tiled=True).reshape(tokens, width)
 
-    w_out = packed[:, :width]
-    tail = packed[:, width:]
-    w_x = tail[:, : R + 2 * N]
-    w_dt = tail[:, R + 2 * N : 2 * R + 2 * N]
-    vectors = tail[:, 2 * R + 2 * N : used].astype(F32).T
+    w_out, w_x, w_dt = (part.reshape(channels, part.shape[2]) for part in parts[:3])
+    vectors = jnp.swapaxes(parts[3], 0, 1).reshape(16, channels).astype(F32)
     taps, conv_shift, rate_shift, skip = vectors[:KCONV], vectors[KCONV], vectors[KCONV + 1], vectors[KCONV + 2]
 
     begins, places = token_begins(doc_lengths, length)
     keep = (places[None, :] != begins).astype(F32).reshape(tokens, 1)
     valid = [(places[None, :] - (lag_max - w) >= begins)[:, :, None] for w in range(KCONV)]
 
-    gain = norm_gain.astype(F32)
-    x_full = hidden.astype(F32)
-    inv_rms = lax.rsqrt(jnp.mean(x_full * x_full, axis=1, keepdims=True) + norm_eps)
-    normed = (x_full * inv_rms * gain).astype(BF)
-    pre = mm(normed, w_in, NT).astype(BF)
     x_inner = pre[:, :channels].reshape(seqs, length, channels)
 
     padded = jnp.pad(x_inner, ((0, 0), (lag_max, 0), (0, 0)))
@@ -950,7 +1257,9 @@
     dq, dk = dq.reshape(tokens, N), dk.reshape(tokens, N)
     d_norm = -jnp.sum(d_norm, axis=1, keepdims=True)
     d_keys = dk + 2.0 * key * d_norm
-    d_row, thin = reduce_over_seq(d_row, jnp.concatenate([d_keys.T, dq.T], axis=0), 3)
+    grad_out = mm(gated, cot, TN).astype(BF).reshape(dp, rows, width)
+    d_row, thin, grad_out = reduce_over_seq(d_row, jnp.concatenate([d_keys.T, dq.T], axis=0), 3, grad_out)
+    grad_out = lax.ppermute(grad_out, ("dp", "seq"), homes_back(dp, seq))
     d_proj = jnp.concatenate([d_row, thin.T.astype(BF)], axis=1)
     d_conv_out = mm(d_proj, w_x, NT) + rest
     d_conv = (d_conv_out * silu_slope(conv_flat)).reshape(seqs, length, channels)
@@ -963,48 +1272,29 @@
         masked = jnp.where(valid[w], d_conv, 0.0)
         tap_grads.append(jnp.sum(masked * window, axis=(0, 1)))
         d_x_inner = d_x_inner + jnp.pad(masked, ((0, 0), (0, lag), (0, 0)))[:, lag:, :] * taps[w]
-    d_pre = jnp.concatenate([d_x_inner.reshape(tokens, channels).astype(BF), d_z], axis=1)
-
-    grad_w_out = mm(gated, cot, TN)
     vector_grads = jnp.stack(
-        tap_grads
-        + [
-            jnp.sum(d_conv, axis=(0, 1)),
-            jnp.sum(sums[:8], axis=0),
-            jnp.sum(sums[8:], axis=0),
-        ],
-        axis=1,
+        tap_grads + [jnp.sum(d_conv, axis=(0, 1)), jnp.sum(sums[:8], axis=0), jnp.sum(sums[8:], axis=0)], axis=0
     )
-    small_grads = jnp.concatenate([mm(xc_low, d_proj, TN), grad_dt, vector_grads], axis=1)
-    packed_grads = jnp.concatenate([grad_w_out, jnp.pad(small_grads, ((0, 0), (0, padded_cols - used)))], axis=1)
-    d_normed = mm(d_pre, w_in, NN)
-    gain_local = jnp.sum(d_normed * x_full * inv_rms, axis=0)
-    grad_in, grad_in_weight, packed_grads, grad_norm_gain = scatter(
-        d_normed.astype(BF).reshape(seqs, length, width),
-        mm(d_pre, normed, TN).astype(BF),
-        packed_grads.astype(BF),
-        gain_local.reshape(8, width // 8),
-        hidden_in,
-        out_cotangent,
-        norm_gain.reshape(1, width),
+    vector_grads = jnp.pad(vector_grads, ((0, 16 - KCONV - 3), (0, 0))).reshape(16, dp, rows)
+    grads = [part.astype(BF).reshape(dp, rows, -1) for part in (mm(xc_low, d_proj, TN), grad_dt)]
+    grads.append(jnp.swapaxes(vector_grads, 0, 1).astype(BF))
+    grad_in, grad_in_weight, grads, grad_norm_gain = scatter(
+        d_x_inner.reshape(tokens, channels).astype(BF), d_z, normed, w_in, hidden, grads,
+        hidden_in, out_cotangent, norm_gain,
     )
-    grad_norm_gain = grad_norm_gain.reshape(width)
-    packed_grads = packed_grads.astype(F32)
-    grad_out_weight = packed_grads[:, :width]
-    tail = packed_grads[:, width:]
-
-    base = 2 * R + 2 * N
+    grad_x, grad_dt, grad_vectors = (part.astype(F32) for part in grads)
+    grad_out_weight = grad_out.astype(F32)
     return (
         output,
         grad_in,
         grad_norm_gain,
         grad_in_weight,
-        tail[:, base : base + KCONV].T,
-        tail[:, base + KCONV],
-        tail[:, : R + 2 * N],
-        tail[:, R + 2 * N : base],
-        tail[:, base + KCONV + 1],
-        tail[:, base + KCONV + 2],
+        grad_vectors[:KCONV],
+        grad_vectors[KCONV],
+        grad_x,
+        grad_dt,
+        grad_vectors[KCONV + 1],
+        grad_vectors[KCONV + 2],
         grad_out_weight,
     )
 

time: 561 us -> 502 us (0.89)
  matrix products: 75.9 us -> 31.9 us
  local copies, waits for them, and re-layouts: 58.1 us -> 38 us
  Pallas kernels: 372 us -> 384 us
  other arithmetic: 29.8 us -> 23.9 us
    dot_general x10 -> x7, matrix products: 75.9 us -> 31.9 us  [mm(): lax.dot_general(left, right, (dims, ((), ())), preferred_element_type=F32)]
    pallas_call x4, Pallas kernels: 272 us -> 284 us  [the longest x1 111 us: scatter(): pl.pallas_call(functools.partial(scatter_kernel, dp, seq, len(parts), fus...]
    pallas_call x1 -> x0, local copies, waits for them, and re-layouts: 7.6 us -> none  [gather(): pl.pallas_call(functools.partial(gather_kernel, dp, seq), in_specs=any_sp...]
    slice x5 -> x1, local copies, waits for them, and re-layouts: 7.88 us -> 1.4 us  [local(): grad_vectors[:KCONV]]
    another operation x7 -> x8, local copies, waits for them, and re-layouts: 6.38 us -> 0.1 us  [local(): jnp.stack(tap_grads + [jnp.sum(d_conv, axis=(0, 1)), jnp.sum(sums[:8], ax...]
    unnamed x73 -> x60, local copies, waits for them, and re-layouts: 18.3 us -> 22.2 us
  transfers between devices with their start and end apart: 2 -> 3, of which waited for: 0 -> 0; matrix products, arithmetic and copies ran while one was open for 26% -> 14% of each run, Pallas kernels for 53% -> 58%
where the time goes in v5:
time: 502 us; the launch traced here: 496 us
  Pallas kernels  384 us (76%)
  local copies, waits for them, and re-layouts  38 us (8%)
  matrix products  31.9 us (6%)
  other arithmetic  23.9 us (5%)
  between operations  14.8 us (3%)
    pallas_call x1, Pallas kernels, scatter(): pl.pallas_call(functools.partial(scatter_kernel, dp, seq, len(parts), fus...  111 us
    pallas_call x1, Pallas kernels, gather(): pl.pallas_call(functools.partial(gather_kernel, dp, seq, fused), in_specs...  98.3 us
    pallas_call x2, Pallas kernels, reduce_over_seq(): pl.pallas_call(functools.partial(reduce_kernel, dp, seq, grads is not Non...  74 us
    pallas_call x1, Pallas kernels, scan_backward(): pl.pallas_call(backward_kernel, grid=(seqs, blocks), in_specs=[rows, rows...  67.4 us
    pallas_call x1, Pallas kernels, scan_forward(): pl.pallas_call(forward_kernel, grid=(seqs, blocks), in_specs=[rows, row_s...  32.6 us
    dot_general x7, matrix products, mm(): lax.dot_general(left, right, (dims, ((), ())), preferred_element_type=F32)  31.9 us
    unnamed x60, local copies, waits for them, and re-layouts  22.2 us
  transfers between devices with their start and end apart: 3, of which 0 were waited for; matrix products, arithmetic and copies ran while one was open for 14% of the time, Pallas kernels for 58%

profile of v5, /device:TPU:9, one launch (start us, length us, event | category | flops | bytes accessed | tf_op | source)
XLA Modules:
  0.0 496.3 jit_solution(9887094468857601107)
XLA Ops:
  13.8 98.3 %gather_in.1 = (bf16[1,1024,2048]{2,1,0:T(8,128)(2,1)S(1)}, bf16[8,256,2048]{2,1,0:T(8,128)(2,1)}, bf16[8,128,2048]{2,1,0:T(8,128)(2,1)S(1)}, bf16[8,128,160]{2,...) custom-call(bf16[1,256,2048]{2,1,0:T(8,128)(2,1)S(1)} %copy-done.5, ...), custom_call_target="tpu_custom_call" | custom-call | tf_op jit(solution)/shard_map/gather_in/pallas_call | solution.py:630
  112.1 1.9 copy-done
  114.1 1.9 copy-done.6
  116.0 1.9 copy-done.7
  117.9 2.0 copy-done.17
  122.3 2.0 slice_bitcast_fusion
  124.4 4.9 fusion.27
  131.2 41.1 %reduce_seq.2 = (bf16[1024,128]{1,0:T(8,128)(2,1)S(1)}, f32[4,32,256]{2,1,0:T(8,128)S(1)}) custom-call(bf16[1024,128]{1,0:T(8,128)(2,1)S(1)} %convolution_convert_fusion.1.refs_0_, f32[4,32,256]{2,1,0:T(8,128)S(1)} %fusion.36.refs_1_), custom_call_target="tpu_custom_call" | custom-call | tf_op jit(solution)/shard_map/reduce_seq/pallas_call | solution.py:1169
  173.5 3.9 broadcast_in_dim.123.key_ref
  177.4 3.9 broadcast_in_dim.124.query_ref
  181.7 32.6 %scan_forward.1 = (bf16[16384,1024]{1,0:T(8,128)(2,1)}, f32[1024,1024]{1,0:T(8,128)S(1)}, bf16[1024,1024]{1,0:T(8,128)(2,1)S(1)}) custom-call(bf16[1024,1024]{1,0:T(8,128)(2,1)S(1)} %get-tuple-element.118.xc_ref, bf16[1024,2048]{1,0:T(8,128)(2,1)S(1)} %copy-done.2, bf16[1024,128]{1,0:T(8,128)(2,1)S(1)} %copy-done.11, ...), custom_call_target="tpu_custom_call" | custom-call | flops 1006632960 | bytes 46137344 | tf_op jit(solution)/shard_map/scan_forward/pallas_call | solution.py:320
  214.3 2.0 copy-done.8
  217.6 6.1 %convert_bitcast_fusion = bf16[1,1024,2048]{2,1,0:T(8,128)(2,1)} fusion(bf16[1024,1024]{1,0:T(8,128)(2,1)S(1)} %get-tuple-element.50, bf16[1024,2048]{1,0:T(8,128)(2,1)S(1)} %bitcast.140), kind=kOutput, calls=%fused_computation.48 | convolution fusion | flops 4297064448 | bytes 10485760 | tf_op jit(solution)/shard_map/dot_general | solution.py:38
  223.8 10.2 %fusion.22.dg_ref = f32[1024,1024]{1,0:T(8,128)} fusion(bf16[1024,2048]{1,0:T(8,128)(2,1)} %bitcast.139, bf16[1,1024,2048]{2,1,0:T(8,128)(2,1)} %all-gather.2.cloned.1.call-done), kind=kOutput, calls=%fused_computation.33 | convolution fusion | flops 4294967296 | bytes 12582912 | tf_op jit(solution)/shard_map/dot_general | solution.py:38
  234.0 67.4 %scan_backward.1 = (bf16[1024,1024]{1,0:T(8,128)(2,1)S(1)}, f32[1024,1024]{1,0:T(8,128)}, f32[128,128]{1,0:T(8,128)S(1)}, f32[128,128]{1,0:T(8,128)S(1)}, f32[10...) custom-call(f32[1024,1024]{1,0:T(8,128)} %fusion.22.dg_ref, ...), custom_call_target="tpu_custom_call" | custom-call | flops 1677721600 | bytes 58720256 | tf_op jit(solution)/shard_map/scan_backward/pallas_call | solution.py:357
  303.8 7.4 %fusion.31 = bf16[1024,2048]{1,0:T(8,128)(2,1)S(1)} fusion(bf16[1024,1024]{1,0:T(8,128)(2,1)} %copy-done.19, bf16[1,1024,2048]{2,1,0:T(8,128)(2,1)} %all-gather.2.cloned.1.call-done), kind=kOutput, calls=%fused_computation.50 | convolution fusion | flops 4297064448 | bytes 10485760 | tf_op jit(solution)/shard_map/dot_general | solution.py:38
  311.2 32.9 %reduce_seq.3 = (bf16[1024,128]{1,0:T(8,128)(2,1)S(1)}, f32[4,32,256]{2,1,0:T(8,128)S(1)}, bf16[128,2048]{1,0:T(8,128)(2,1)S(1)}) custom-call(bf16[1024,128]{1,0:T(8,128)(2,1)S(1)} %convert_element_type.144.refs_0_, f32[4,32,256]{2,1,0:T(8,128)S(1)} %bitcast.136, bf16[8,128,2048]{2,1,0:T(8,128)(2,1)S(1)} %bitcast.132), custom_call_target="tpu_custom_call" | custom-call | tf_op jit(solution)/shard_map/reduce_seq/pallas_call | solution.py:1169
  344.3 3.3 collective-permute-start
  347.7 5.7 %fusion.52 = (bf16[1024]{0:T(1024)(128)(2,1)S(1)}, bf16[1024]{0:T(1024)(128)(2,1)S(1)}, f32[1024,1024]{1,0:T(8,128)S(1)}) fusion(bf16[1024,2048]{1,0:T(8,128)(2,1)} %copy-done, pred[1024]{0:T(1024)(128)(4,1)S(1)} %get-tuple-element.131, f32[1,1024,1024]{2,1,0:T(8,128)} %copy-done.24, f32[1024,1024]{1,0:T(8,128)} %get-tuple-element.61, ...), kind=kOutput, calls=%fused_computation.101 | convolution fusion | flops 350877696 | bytes 15340544 | tf_op jit(solution)/shard_map/dot_general | solution.py:38
  353.4 2.9 fusion.16
  356.3 3.9 fusion.34.refs_0_
  363.3 111.4 %scatter_out.1 = (bf16[1,256,2048]{2,1,0:T(8,128)(2,1)}, f32[256,2048]{1,0:T(8,128)}, bf16[128,160]{1,0:T(8,128)(2,1)}, bf16[128,128]{1,0:T(8,128)(2,1)}, bf16[16,128]{1,0:T(8,128)(2,1)}, /*index=5*/f32[8,2048]{1,0:T(8,128)}) custom-call(bf16[1024,1024]{1,0:T(8,128)(2,1)} %fusion.34.refs_0_, bf16[1024,1024]{1,0:T(8,128)(2,1)} %copy-done.9, ...), custom_call_target="tpu_custom_call" | custom-call | tf_op jit(solution)/shard_map/scatter_out/pallas_call | solution.py:1015
  481.8 2.2 convert_element_type.159
  484.0 2.9 add_convert_fusion
  (111 shorter events, 28.6 us)
Async XLA Ops:
  7.2 216.6 %all-gather.2.cloned.1.call-start = ((), (), s32[]{:S(2)}) async-start(), calls=%async_computation.2 | async-start | bytes 5242880 | tf_op jit(solution)/shard_map/all_gather | solution.py:1219
  8.8 120.4 %copy-start.15 = (bf16[1,2048]{1,0:T(2,128)(2,1)}, bf16[1,2048]{1,0:T(2,128)(2,1)S(1)}, u32[]{:S(2)}) copy-start(bf16[1,2048]{1,0:T(2,128)(2,1)S(1)} %reshape.264.refs_6_.refs_10_) | copy-start | bytes 12292
  112.1 2.0 copy-start
  114.1 1.9 copy-start.6
  116.0 1.9 copy-start.7
  117.9 2.0 copy-start.17
  119.9 10.1 %copy-start.20 = (bf16[8,128,160]{2,1,0:T(8,128)(2,1)}, bf16[8,128,160]{2,1,0:T(8,128)(2,1)S(1)}, u32[]{:S(2)}) copy-start(bf16[8,128,160]{2,1,0:T(8,128)(2,1)S(1)} %get-tuple-element.46) | copy-start | bytes 983044
  119.9 364.1 %reduce-scatter.2.cloned.1.call-start = ((), (), s32[]{:S(2)}) async-start(), calls=%async_computation.1 | async-start | bytes 5242880 | tf_op jit(solution)/shard_map/reduce_scatter | solution.py:1251
  121.3 3.0 copy-start.1
  124.3 4.9 copy-start.22
  129.2 2.0 copy-start.24
  129.3 52.4 %copy-start.3 = (bf16[1024,1024]{1,0:T(8,128)(2,1)}, bf16[1024,1024]{1,0:T(8,128)(2,1)S(1)}, u32[]{:S(2)}) copy-start(bf16[1024,1024]{1,0:T(8,128)(2,1)S(1)} %get-tuple-element.118.xc_ref) | copy-start | bytes 6291460
  173.4 8.2 %copy-start.2 = (bf16[1024,2048]{1,0:T(8,128)(2,1)S(1)}, bf16[1024,2048]{1,0:T(8,128)(2,1)}, u32[]{:S(2)}) copy-start(bf16[1024,2048]{1,0:T(8,128)(2,1)} %copy-done) | copy-start | bytes 12582916
  173.5 8.2 %copy-start.11 = (bf16[1024,128]{1,0:T(8,128)(2,1)S(1)}, bf16[1024,128]{1,0:T(8,128)(2,1)}, u32[]{:S(2)}) copy-start(bf16[1024,128]{1,0:T(8,128)(2,1)} %copy-done.10) | copy-start | bytes 786436
  181.7 35.9 %copy-start.18 = (bf16[8,128,2048]{2,1,0:T(8,128)(2,1)S(1)}, bf16[8,128,2048]{2,1,0:T(8,128)(2,1)}, u32[]{:S(2)}) copy-start(bf16[8,128,2048]{2,1,0:T(8,128)(2,1)} %copy-done.17) | copy-start | bytes 12582916
  214.3 2.0 copy-start.8
  223.7 10.2 %copy-start.12 = (bf16[1024,128]{1,0:T(8,128)(2,1)S(1)}, bf16[1024,128]{1,0:T(8,128)(2,1)}, u32[]{:S(2)}) copy-start(bf16[1024,128]{1,0:T(8,128)(2,1)} %copy-done.10) | copy-start | bytes 786436
  301.4 1.3 copy-start.9
  311.2 36.5 %copy-start.21 = (bf16[8,128,160]{2,1,0:T(8,128)(2,1)S(1)}, bf16[8,128,160]{2,1,0:T(8,128)(2,1)}, u32[]{:S(2)}) copy-start(bf16[8,128,160]{2,1,0:T(8,128)(2,1)} %copy-done.20) | copy-start | bytes 983044
  344.3 137.5 %collective-permute-start = (bf16[128,2048]{1,0:T(8,128)(2,1)S(1)}, bf16[128,2048]{1,0:T(8,128)(2,1)}, u32[]{:S(2)}, u32[]{:S(2)}) collective-permute-start(bf16[128,2048]{1,0:T(8,128)(2,1)S(1)} %get-tuple-element.74), channel_id=1, source_target_pairs={{0,0},{4,1},{1,2},{5,3},{2,4},{6,5},{3,6},{7,7},{8,8},{12,9},{9,10... | collective-permute-start | bytes 1572872 | tf_op jit(solution)/shard_map/ppermute | solution.py:1262
  347.7 5.7 %copy-start.23 = (bf16[1,1024,1024]{2,1,0:T(8,128)(2,1)S(1)}, bf16[1,1024,1024]{2,1,0:T(8,128)(2,1)}, u32[]{:S(2)}) copy-start(bf16[1,1024,1024]{2,1,0:T(8,128)(2,1)} %copy-done.22) | copy-start | bytes 6291460
  356.3 4.0 copy-start.4
  474.8 13.1 %copy-start.25 = (f32[256,2048]{1,0:T(8,128)S(1)}, f32[256,2048]{1,0:T(8,128)}, u32[]{:S(2)}) copy-start(f32[256,2048]{1,0:T(8,128)} %get-tuple-element.150) | copy-start | bytes 6291460
  481.8 5.1 %copy-start.26 = (bf16[1,256,2048]{2,1,0:T(8,128)(2,1)S(1)}, bf16[1,256,2048]{2,1,0:T(8,128)(2,1)}, u32[]{:S(2)}) copy-start(bf16[1,256,2048]{2,1,0:T(8,128)(2,1)} %get-tuple-element.148) | copy-start | bytes 3145732
  (6 other events, 6.3 us)
Sparse Core Ops, SparseCore 0:
  120.1 92.5 all-gather.1
  223.8 79.4 reduce-scatter.1

commit v6 on v5

--- a/solution.py
+++ b/solution.py
@@ -675,7 +675,7 @@
     gain_out = take(1)[0]
     own, come, gw_own, gw_x, gw_r = take(5)
     p_own, p_x, p_r, p_fin = take(count), take(count), take(count), take(count)
-    g_in, g_x, g_r, g_z, g_a, g_b = take(6)
+    g_in, g_one, g_x, g_r, g_z, g_a, g_b = take(7)
     z_load, z_send, z_recv, w_load, wx_send, wx_recv, w_send, w_recv = take(8)
     p_load, px_send, px_recv, p_send, p_recv, t_send, t_recv, gx_sem, g_send, g_recv, gz_send, gz_recv = take(12)
 
@@ -812,35 +812,27 @@
         here = come.at[slot, :, rows, :]
         remote(here, here, z_send.at[0, q], z_recv.at[slot, q], (d, s)).wait_recv()
 
-    def send(way, r, q):
-        before = r + 1 if way == 0 else r - 1
-        if 0 <= before < seq:
-            give(way, before, q).wait_send()
-        give(way, r, q).start()
-
     def begin():
         for q in range(pieces):
             pl.when(s == 0)(give(0, seq - 1, q).start)
             pl.when(s == seq - 1)(give(1, 0, q).start)
 
-    def pass_on(way, r, q):
-        first = s == 0 if way == 0 else s == seq - 1
-        sends = s < r if way == 0 else s > r
-        begun = r == (seq - 1 if way == 0 else 0)
-
-        @pl.when(jnp.logical_and(sends, jnp.logical_not(first)))
-        def _():
-            rows = pl.ds(q * piece, piece)
-            landed(r, q)
-            own[r, :, rows, :] = added(own.at[r, :, rows, :], come.at[r, :, rows, :]).astype(BF)
-            send(way, r, q)
-
-        if not begun:
-            pl.when(jnp.logical_and(sends, first))(functools.partial(send, way, r, q))
-
-    def hop(i, q):
-        pass_on(0, seq - 1 - i, q)
-        pass_on(1, i, q)
+    def hop(turn, q):
+        rows = pl.ds(q * piece, piece)
+        for way in range(2):
+            far = s if way == 0 else seq - 1 - s
+            i = turn - far
+            r = seq - 1 - i if way == 0 else i
+            before = r + 1 if way == 0 else r - 1
+            sends = jnp.logical_and(i >= 0, s < r if way == 0 else s > r)
+
+            @pl.when(jnp.logical_and(sends, far > 0))
+            def _():
+                landed(r, q)
+                own[r, :, rows, :] = added(own.at[r, :, rows, :], come.at[r, :, rows, :]).astype(BF)
+
+            pl.when(jnp.logical_and(sends, i > 0))(give(way, before, q).wait_send)
+            pl.when(jnp.logical_and(sends, far + i > 0))(give(way, r, q).start)
 
     def onward(part_own, part_r, send, recv, k):
         j = lax.rem(mine + k, pairs)
@@ -871,7 +863,7 @@
                 gw_own[j] = added(gw_own.at[j], gw_x.at[j]).astype(BF)
                 gw_onward(k).start()
 
-    gain_swap = remote(g_in, g_x, gx_sem.at[0], gx_sem.at[1], (mate(d), s))
+    gain_swap = remote(g_one, g_x, gx_sem.at[0], gx_sem.at[1], (mate(d), s))
 
     def gain_near(k):
         return remote(g_a, g_r.at[k - 1], g_send.at[k], g_recv.at[k], (lax.rem(d + 2 * k, dp), s))
@@ -881,7 +873,7 @@
 
     def gain_middle():
         gain_swap.wait_recv()
-        g_a[...] = g_in[...] + g_x[...]
+        g_a[...] = g_one[...] + g_x[...]
         for k in range(1, pairs):
             gain_near(k).start()
 
@@ -910,14 +902,15 @@
         part_join()
         loads[3].wait()
         gw_away()
+        gw_home()
+        gw_join()
         dn_tasks(2, seq)
-        gain_swap.start()
-        gw_home()
     else:
         begin()
         part_join()
-        gain_swap.start()
-    gw_join()
+        gw_join()
+    g_one[...] = jnp.sum(g_in[...], axis=0, keepdims=True)
+    gain_swap.start()
     later = [gain_middle, gain_last, part_finish]
     for i in range(seq - 1):
         for q in range(pieces):
@@ -993,21 +986,19 @@
             vmem((tokens, 2 * channels), BF), vmem((tokens, width), BF), vmem((2 * channels, width), BF),
             vmem((part, width), BF), vmem((pairs, w_rows, width), BF), dma((4,)), dma,
         ]
-        gain_shape = (8, width)
     else:
         d_pre = jnp.concatenate([d_x, d_z], axis=1)
         x = hidden.astype(F32)
         d_normed = mm(d_pre, w_in, NN)
         inv = lax.rsqrt(jnp.mean(x * x, axis=1, keepdims=True) + norm_eps)
-        gain = jnp.sum(d_normed * x * inv, axis=0).reshape(8, -1)
+        gain = jnp.pad(jnp.sum(d_normed * x * inv, axis=0)[None], ((0, 7), (0, 0)))
         ins = [
             d_normed.astype(BF).reshape(seqs, -1, width),
             mm(d_pre, normed, TN).astype(BF).reshape(dp, w_rows, width), gain,
         ]
         in_specs, extra = any_specs(2) + [here], []
-        gain_shape = gain.shape
     part_shapes = [member.shape[1:] for member in parts]
-    token_shape = (seqs, part, width)
+    token_shape, one = (seqs, part, width), (1, width)
 
     def each(count):
         return [vmem((count,) + member, BF) for member in part_shapes]
@@ -1018,13 +1009,13 @@
         out_specs=[here] * (3 + count),
         out_shape=[shape(token_shape, BF), shape((w_rows, width), F32)]
         + [shape(member, BF) for member in part_shapes]
-        + [shape(gain_shape, F32)],
+        + [shape(one, F32)],
         scratch_shapes=[
             vmem((seq,) + token_shape, BF), vmem((seq + 1,) + token_shape, BF),
             vmem((pairs, w_rows, width), BF), vmem((pairs, w_rows, width), BF), vmem((pairs - 1, w_rows, width), BF),
             *each(pairs), *each(pairs), *each(pairs - 1), *[vmem(member, BF) for member in part_shapes],
-            vmem(gain_shape, F32), vmem(gain_shape, F32), vmem((pairs - 1,) + gain_shape, F32),
-            vmem((seq - 1,) + gain_shape, F32), vmem(gain_shape, F32), vmem(gain_shape, F32),
+            vmem((8, width), F32), vmem(one, F32), vmem(one, F32), vmem((pairs - 1,) + one, F32),
+            vmem((seq - 1,) + one, F32), vmem(one, F32), vmem(one, F32),
             dma((seq,)), dma((seq, pieces)), dma((seq + 1, pieces)),
             dma((pairs,)), dma((pairs,)), dma((pairs,)), dma((pairs,)), dma((pairs,)),
             *[dma((count, pairs))] * 5, dma((2 * count,)), dma((count,)),
@@ -1036,8 +1027,7 @@
         ),
         name="scatter_out",
     )(*ins, *parts, hidden_in, cotangent, norm_gain.reshape(1, width))
-    gain = jnp.sum(out[-1], axis=0) if fused else out[-1].reshape(width)
-    return out[0], out[1], out[2 : 2 + count], gain
+    return out[0], out[1], out[2 : 2 + count], out[-1].reshape(width)
 
 
 def reduce_kernel(dp, seq, grads, *refs):

time: 502 us -> 491 us (0.978)
  Pallas kernels: 384 us -> 373 us
    pallas_call x1, Pallas kernels: 111 us -> 101 us  [scatter(): pl.pallas_call(functools.partial(scatter_kernel, dp, seq, len(parts), fus...]
    unnamed x60 -> x63, local copies, waits for them, and re-layouts: 22.2 us -> 22.8 us
  transfers between devices with their start and end apart: 3 -> 3, of which waited for: 0 -> 0; matrix products, arithmetic and copies ran while one was open for 14% -> 14% of each run, Pallas kernels for 58% -> 57%
where the time goes in v6:
time: 491 us; the launch traced here: 485 us
  Pallas kernels  373 us (76%)
  local copies, waits for them, and re-layouts  38.6 us (8%)
  matrix products  31.9 us (6%)
  other arithmetic  22.4 us (5%)
  between operations  14.9 us (3%)
    pallas_call x1, Pallas kernels, scatter(): pl.pallas_call(functools.partial(scatter_kernel, dp, seq, len(parts), fus...  101 us
    pallas_call x1, Pallas kernels, gather(): pl.pallas_call(functools.partial(gather_kernel, dp, seq, fused), in_specs...  98.3 us
    pallas_call x2, Pallas kernels, reduce_over_seq(): pl.pallas_call(functools.partial(reduce_kernel, dp, seq, grads is not Non...  74.1 us
    pallas_call x1, Pallas kernels, scan_backward(): pl.pallas_call(backward_kernel, grid=(seqs, blocks), in_specs=[rows, rows...  67.4 us
    pallas_call x1, Pallas kernels, scan_forward(): pl.pallas_call(forward_kernel, grid=(seqs, blocks), in_specs=[rows, row_s...  32.6 us
    dot_general x7, matrix products, mm(): lax.dot_general(left, right, (dims, ((), ())), preferred_element_type=F32)  31.9 us
    unnamed x63, local copies, waits for them, and re-layouts  22.8 us
  transfers between devices with their start and end apart: 3, of which 0 were waited for; matrix products, arithmetic and copies ran while one was open for 14% of the time, Pallas kernels for 57%

profile of v6, /device:TPU:9, one launch (start us, length us, event | category | flops | bytes accessed | tf_op | source)
XLA Modules:
  0.0 484.9 jit_solution(4390372243090895483)
XLA Ops:
  13.8 98.3 %gather_in.1 = (bf16[1,1024,2048]{2,1,0:T(8,128)(2,1)S(1)}, bf16[8,256,2048]{2,1,0:T(8,128)(2,1)}, bf16[8,128,2048]{2,1,0:T(8,128)(2,1)S(1)}, bf16[8,128,160]{2,...) custom-call(bf16[1,256,2048]{2,1,0:T(8,128)(2,1)S(1)} %copy-done.5, ...), custom_call_target="tpu_custom_call" | custom-call | tf_op jit(solution)/shard_map/gather_in/pallas_call | solution.py:630
  112.1 1.9 copy-done
  114.1 1.9 copy-done.6
  116.0 1.9 copy-done.7
  117.9 2.0 copy-done.17
  122.3 2.0 slice_bitcast_fusion
  124.3 4.9 %fusion.27 = (bf16[1024,1024]{1,0:T(8,128)(2,1)S(1)}, f32[1,1024,1024]{2,1,0:T(8,128)S(1)}) fusion(f32[1024]{0:T(1024)S(1)} %bitcast.156, bf16[1024,2048]{1,0:T(8,128)(2,1)S(1)} %copy-done.1, pred[1024]{0:T(1024)(128)(4,1)S(1)} %get-tuple-element.131, f32[1024]{0:T(1024)S(1)} %bitcast.158, pred[1024]{0:T(1024)(128)(4,1)S(1)} %get-tuple-element.132, ...), kind=kLoop, calls=%fused_computation.41 | loop fusion | flops 22020096 | bytes 10510336 | tf_op jit(solution)/shard_map/convert_element_type | solution.py:1227
  131.2 41.1 %reduce_seq.2 = (bf16[1024,128]{1,0:T(8,128)(2,1)S(1)}, f32[4,32,256]{2,1,0:T(8,128)S(1)}) custom-call(bf16[1024,128]{1,0:T(8,128)(2,1)S(1)} %convolution_convert_fusion.1.refs_0_, f32[4,32,256]{2,1,0:T(8,128)S(1)} %fusion.36.refs_1_), custom_call_target="tpu_custom_call" | custom-call | tf_op jit(solution)/shard_map/reduce_seq/pallas_call | solution.py:1159
  173.5 3.9 broadcast_in_dim.123.key_ref
  177.3 3.9 broadcast_in_dim.124.query_ref
  181.7 32.6 %scan_forward.1 = (bf16[16384,1024]{1,0:T(8,128)(2,1)}, f32[1024,1024]{1,0:T(8,128)S(1)}, bf16[1024,1024]{1,0:T(8,128)(2,1)S(1)}) custom-call(bf16[1024,1024]{1,0:T(8,128)(2,1)S(1)} %get-tuple-element.118.xc_ref, bf16[1024,2048]{1,0:T(8,128)(2,1)S(1)} %copy-done.2, bf16[1024,128]{1,0:T(8,128)(2,1)S(1)} %copy-done.11, ...), custom_call_target="tpu_custom_call" | custom-call | flops 1006632960 | bytes 46137344 | tf_op jit(solution)/shard_map/scan_forward/pallas_call | solution.py:320
  214.3 2.0 copy-done.8
  217.6 6.1 %convert_bitcast_fusion = bf16[1,1024,2048]{2,1,0:T(8,128)(2,1)} fusion(bf16[1024,1024]{1,0:T(8,128)(2,1)S(1)} %get-tuple-element.50, bf16[1024,2048]{1,0:T(8,128)(2,1)S(1)} %bitcast.141), kind=kOutput, calls=%fused_computation.48 | convolution fusion | flops 4297064448 | bytes 10485760 | tf_op jit(solution)/shard_map/dot_general | solution.py:38
  223.7 10.2 %fusion.22.dg_ref = f32[1024,1024]{1,0:T(8,128)} fusion(bf16[1024,2048]{1,0:T(8,128)(2,1)} %bitcast.140, bf16[1,1024,2048]{2,1,0:T(8,128)(2,1)} %all-gather.2.cloned.1.call-done), kind=kOutput, calls=%fused_computation.33 | convolution fusion | flops 4294967296 | bytes 12582912 | tf_op jit(solution)/shard_map/dot_general | solution.py:38
  233.9 67.4 %scan_backward.1 = (bf16[1024,1024]{1,0:T(8,128)(2,1)S(1)}, f32[1024,1024]{1,0:T(8,128)}, f32[128,128]{1,0:T(8,128)S(1)}, f32[128,128]{1,0:T(8,128)S(1)}, f32[10...) custom-call(f32[1024,1024]{1,0:T(8,128)} %fusion.22.dg_ref, ...), custom_call_target="tpu_custom_call" | custom-call | flops 1677721600 | bytes 58720256 | tf_op jit(solution)/shard_map/scan_backward/pallas_call | solution.py:357
  303.7 7.4 %fusion.31 = bf16[1024,2048]{1,0:T(8,128)(2,1)S(1)} fusion(bf16[1024,1024]{1,0:T(8,128)(2,1)} %copy-done.19, bf16[1,1024,2048]{2,1,0:T(8,128)(2,1)} %all-gather.2.cloned.1.call-done), kind=kOutput, calls=%fused_computation.50 | convolution fusion | flops 4297064448 | bytes 10485760 | tf_op jit(solution)/shard_map/dot_general | solution.py:38
  311.1 33.0 %reduce_seq.3 = (bf16[1024,128]{1,0:T(8,128)(2,1)S(1)}, f32[4,32,256]{2,1,0:T(8,128)S(1)}, bf16[128,2048]{1,0:T(8,128)(2,1)S(1)}) custom-call(bf16[1024,128]{1,0:T(8,128)(2,1)S(1)} %convert_element_type.144.refs_0_, f32[4,32,256]{2,1,0:T(8,128)S(1)} %bitcast.137, bf16[8,128,2048]{2,1,0:T(8,128)(2,1)S(1)} %bitcast.133), custom_call_target="tpu_custom_call" | custom-call | tf_op jit(solution)/shard_map/reduce_seq/pallas_call | solution.py:1159
  344.3 3.4 collective-permute-start
  347.7 5.7 %fusion.52 = (bf16[1024]{0:T(1024)(128)(2,1)S(1)}, bf16[1024]{0:T(1024)(128)(2,1)S(1)}, f32[1024,1024]{1,0:T(8,128)S(1)}) fusion(bf16[1024,2048]{1,0:T(8,128)(2,1)} %copy-done, pred[1024]{0:T(1024)(128)(4,1)S(1)} %get-tuple-element.131, f32[1,1024,1024]{2,1,0:T(8,128)} %copy-done.24, f32[1024,1024]{1,0:T(8,128)} %get-tuple-element.61, ...), kind=kOutput, calls=%fused_computation.101 | convolution fusion | flops 350877696 | bytes 15340544 | tf_op jit(solution)/shard_map/dot_general | solution.py:38
  353.4 2.9 fusion.16
  356.3 4.0 fusion.34.refs_0_
  363.4 100.8 %scatter_out.1 = (bf16[1,256,2048]{2,1,0:T(8,128)(2,1)}, f32[256,2048]{1,0:T(8,128)}, bf16[128,160]{1,0:T(8,128)(2,1)}, bf16[128,128]{1,0:T(8,128)(2,1)}, bf16[16,128]{1,0:T(8,128)(2,1)}, /*index=5*/f32[1,2048]{1,0:T(1,128)}) custom-call(bf16[1024,1024]{1,0:T(8,128)(2,1)} %fusion.34.refs_0_, bf16[1024,1024]{1,0:T(8,128)(2,1)} %copy-done.9, ...), custom_call_target="tpu_custom_call" | custom-call | tf_op jit(solution)/shard_map/scatter_out/pallas_call | solution.py:1006
  469.8 2.2 convert_element_type.159
  472.0 2.9 add_convert_fusion
  (113 shorter events, 27.8 us)
Async XLA Ops:
  7.2 216.6 %all-gather.2.cloned.1.call-start = ((), (), s32[]{:S(2)}) async-start(), calls=%async_computation.2 | async-start | bytes 5242880 | tf_op jit(solution)/shard_map/all_gather | solution.py:1209
  8.8 120.4 %copy-start.15 = (bf16[1,2048]{1,0:T(2,128)(2,1)}, bf16[1,2048]{1,0:T(2,128)(2,1)S(1)}, u32[]{:S(2)}) copy-start(bf16[1,2048]{1,0:T(2,128)(2,1)S(1)} %reshape.267.refs_6_.refs_10_) | copy-start | bytes 12292
  112.1 2.0 copy-start
  114.1 1.9 copy-start.6
  116.0 1.9 copy-start.7
  117.9 2.0 copy-start.17
  119.9 10.1 %copy-start.20 = (bf16[8,128,160]{2,1,0:T(8,128)(2,1)}, bf16[8,128,160]{2,1,0:T(8,128)(2,1)S(1)}, u32[]{:S(2)}) copy-start(bf16[8,128,160]{2,1,0:T(8,128)(2,1)S(1)} %get-tuple-element.46) | copy-start | bytes 983044
  119.9 352.1 %reduce-scatter.2.cloned.1.call-start = ((), (), s32[]{:S(2)}) async-start(), calls=%async_computation.1 | async-start | bytes 5242880 | tf_op jit(solution)/shard_map/reduce_scatter | solution.py:1241
  121.3 3.0 copy-start.1
  124.3 4.9 %copy-start.22 = (bf16[1,1024,1024]{2,1,0:T(8,128)(2,1)}, bf16[1,1024,1024]{2,1,0:T(8,128)(2,1)S(1)}, u32[]{:S(2)}) copy-start(bf16[1,1024,1024]{2,1,0:T(8,128)(2,1)S(1)} %slice_bitcast_fusion) | copy-start | bytes 6291460
  129.2 2.0 copy-start.24
  129.3 52.4 %copy-start.3 = (bf16[1024,1024]{1,0:T(8,128)(2,1)}, bf16[1024,1024]{1,0:T(8,128)(2,1)S(1)}, u32[]{:S(2)}) copy-start(bf16[1024,1024]{1,0:T(8,128)(2,1)S(1)} %get-tuple-element.118.xc_ref) | copy-start | bytes 6291460
  173.4 8.2 %copy-start.2 = (bf16[1024,2048]{1,0:T(8,128)(2,1)S(1)}, bf16[1024,2048]{1,0:T(8,128)(2,1)}, u32[]{:S(2)}) copy-start(bf16[1024,2048]{1,0:T(8,128)(2,1)} %copy-done) | copy-start | bytes 12582916
  173.5 8.2 %copy-start.11 = (bf16[1024,128]{1,0:T(8,128)(2,1)S(1)}, bf16[1024,128]{1,0:T(8,128)(2,1)}, u32[]{:S(2)}) copy-start(bf16[1024,128]{1,0:T(8,128)(2,1)} %copy-done.10) | copy-start | bytes 786436
  181.7 35.9 %copy-start.18 = (bf16[8,128,2048]{2,1,0:T(8,128)(2,1)S(1)}, bf16[8,128,2048]{2,1,0:T(8,128)(2,1)}, u32[]{:S(2)}) copy-start(bf16[8,128,2048]{2,1,0:T(8,128)(2,1)} %copy-done.17) | copy-start | bytes 12582916
  214.3 2.0 copy-start.8
  223.7 10.2 %copy-start.12 = (bf16[1024,128]{1,0:T(8,128)(2,1)S(1)}, bf16[1024,128]{1,0:T(8,128)(2,1)}, u32[]{:S(2)}) copy-start(bf16[1024,128]{1,0:T(8,128)(2,1)} %copy-done.10) | copy-start | bytes 786436
  311.1 36.6 %copy-start.21 = (bf16[8,128,160]{2,1,0:T(8,128)(2,1)S(1)}, bf16[8,128,160]{2,1,0:T(8,128)(2,1)}, u32[]{:S(2)}) copy-start(bf16[8,128,160]{2,1,0:T(8,128)(2,1)} %copy-done.20) | copy-start | bytes 983044
  344.3 125.5 %collective-permute-start = (bf16[128,2048]{1,0:T(8,128)(2,1)S(1)}, bf16[128,2048]{1,0:T(8,128)(2,1)}, u32[]{:S(2)}, u32[]{:S(2)}) collective-permute-start(bf16[128,2048]{1,0:T(8,128)(2,1)S(1)} %get-tuple-element.74), channel_id=1, source_target_pairs={{0,0},{4,1},{1,2},{5,3},{2,4},{6,5},{3,6},{7,7},{8,8},{12,9},{9,10... | collective-permute-start | bytes 1572872 | tf_op jit(solution)/shard_map/ppermute | solution.py:1252
  347.7 5.7 %copy-start.23 = (bf16[1,1024,1024]{2,1,0:T(8,128)(2,1)S(1)}, bf16[1,1024,1024]{2,1,0:T(8,128)(2,1)}, u32[]{:S(2)}) copy-start(bf16[1,1024,1024]{2,1,0:T(8,128)(2,1)} %copy-done.22) | copy-start | bytes 6291460
  356.3 4.0 copy-start.4
  464.2 11.7 %copy-start.27 = (f32[1,2048]{1,0:T(1,128)S(1)}, f32[1,2048]{1,0:T(1,128)}, u32[]{:S(2)}) copy-start(f32[1,2048]{1,0:T(1,128)} %get-tuple-element.69) | copy-start | bytes 24580
  464.2 12.3 %copy-start.25 = (f32[256,2048]{1,0:T(8,128)S(1)}, f32[256,2048]{1,0:T(8,128)}, u32[]{:S(2)}) copy-start(f32[256,2048]{1,0:T(8,128)} %get-tuple-element.150) | copy-start | bytes 6291460
  469.8 5.1 %copy-start.26 = (bf16[1,256,2048]{2,1,0:T(8,128)(2,1)S(1)}, bf16[1,256,2048]{2,1,0:T(8,128)(2,1)}, u32[]{:S(2)}) copy-start(bf16[1,256,2048]{2,1,0:T(8,128)(2,1)} %get-tuple-element.148) | copy-start | bytes 3145732
  (7 other events, 7.6 us)
Sparse Core Ops, SparseCore 0:
  120.1 92.5 all-gather.1
  223.8 79.3 reduce-scatter.1

commit v7 on v6

--- a/solution.py
+++ b/solution.py
@@ -510,6 +510,30 @@
     own_w.start()
     own_h.start()
 
+    for k in range(1, seq - 1):
+        for q in range(pieces):
+            for way in range(2):
+                pl.when(s - k >= 0 if way == 0 else s + k < seq)(functools.partial(landed, way, k, q))
+                pl.when(can_send(way, k))(hop(way, k, q).start)
+    own_w.wait()
+    own_h.wait()
+    w_flow = (w_out, w_ref, w_send, w_recv, f_send, f_recv)
+    part_flows = [
+        (slots[m], slots[m].at[d], p_send.at[m], p_recv.at[m], q_send.at[m], q_recv.at[m]) for m in range(PARTS)
+    ]
+
+    def relay(out, own, send, recv, over_send, over_recv):
+        for k in range(1, pairs):
+            here = out.at[source(k)]
+            remote(here, here, send.at[k], recv.at[k], (d, s)).wait_recv()
+            across(out, over_send, over_recv, k).start()
+
+    def complete(out, own, send, recv, over_send, over_recv):
+        for k in range(pairs):
+            here = out.at[lax.rem(mate(d) - 2 * k + dp, dp)]
+            remote(here, here, over_send.at[k], over_recv.at[k], (d, s)).wait_recv()
+
+    relay(*w_flow)
     for m in range(PARTS):
         slot = slots[m].at[d]
         pl.when(moves)(remote(parts[m], slot, t_send.at[m], t_recv.at[m], (to_d, to_s)).wait_recv)
@@ -518,26 +542,11 @@
             spread(slots[m], slot, p_send.at[m], p_recv.at[m], k).start()
         across(slots[m], q_send.at[m], q_recv.at[m], 0, slot).start()
 
-    for k in range(1, seq - 1):
-        for q in range(pieces):
-            for way in range(2):
-                pl.when(s - k >= 0 if way == 0 else s + k < seq)(functools.partial(landed, way, k, q))
-                pl.when(can_send(way, k))(hop(way, k, q).start)
-    own_w.wait()
-    own_h.wait()
-    flows = [(w_out, w_ref, w_send, w_recv, f_send, f_recv)]
-    flows += [
-        (slots[m], slots[m].at[d], p_send.at[m], p_recv.at[m], q_send.at[m], q_recv.at[m]) for m in range(PARTS)
-    ]
-    for out, own, send, recv, over_send, over_recv in flows:
-        for k in range(1, pairs):
-            here = out.at[source(k)]
-            remote(here, here, send.at[k], recv.at[k], (d, s)).wait_recv()
-            across(out, over_send, over_recv, k).start()
-    for out, own, send, recv, over_send, over_recv in flows:
-        for k in range(pairs):
-            here = out.at[lax.rem(mate(d) - 2 * k + dp, dp)]
-            remote(here, here, over_send.at[k], over_recv.at[k], (d, s)).wait_recv()
+    complete(*w_flow)
+
+    def relay_parts():
+        for flow in part_flows:
+            relay(*flow)
 
     last = seq - 1
     if fused:
@@ -575,6 +584,7 @@
             k = (m + 1) // 2
             way = lax.rem(m, 2)
             which = jnp.where(way == 0, s - k, s + k)
+            pl.when(m == 2 * seq - 3)(relay_parts)
 
             @pl.when(jnp.logical_and(which >= 0, which < seq))
             def _():
@@ -587,8 +597,11 @@
         for q in range(pieces):
             for way in range(2):
                 pl.when(s - last >= 0 if way == 0 else s + last < seq)(functools.partial(landed, way, last, q))
-
-    for out, own, send, recv, over_send, over_recv in flows:
+        relay_parts()
+
+    for flow in part_flows:
+        complete(*flow)
+    for out, own, send, recv, over_send, over_recv in [w_flow, *part_flows]:
         for k in range(pairs):
             across(out, over_send, over_recv, k, own).wait_send()
         for k in range(1, pairs):
@@ -634,7 +647,7 @@
         out_shape=outs,
         scratch_shapes=scratch,
         compiler_params=pltpu.CompilerParams(
-            collective_id=collective_id, has_side_effects=True, vmem_limit_bytes=32 << 20
+            collective_id=collective_id, has_side_effects=True, vmem_limit_bytes=44 << 20
         ),
         name="gather_in",
     )(*ins)

time: 491 us -> 483 us (0.984)
  local copies, waits for them, and re-layouts: 38.6 us -> 32.8 us
    unnamed x63 -> x57, local copies, waits for them, and re-layouts: 22.8 us -> 16.9 us
  transfers between devices with their start and end apart: 3 -> 3, of which waited for: 0 -> 0; matrix products, arithmetic and copies ran while one was open for 14% -> 14% of each run, Pallas kernels for 57% -> 58%
where the time goes in v7:
time: 483 us; the launch traced here: 476 us
  Pallas kernels  371 us (77%)
  local copies, waits for them, and re-layouts  32.8 us (7%)
  matrix products  31.6 us (7%)
  other arithmetic  22.4 us (5%)
  between operations  14.8 us (3%)
    pallas_call x1, Pallas kernels, scatter(): pl.pallas_call(functools.partial(scatter_kernel, dp, seq, len(parts), fus...  102 us
    pallas_call x1, Pallas kernels, gather(): pl.pallas_call(functools.partial(gather_kernel, dp, seq, fused), in_specs...  95.9 us
    pallas_call x2, Pallas kernels, reduce_over_seq(): pl.pallas_call(functools.partial(reduce_kernel, dp, seq, grads is not Non...  73.1 us
    pallas_call x1, Pallas kernels, scan_backward(): pl.pallas_call(backward_kernel, grid=(seqs, blocks), in_specs=[rows, rows...  67.5 us
    pallas_call x1, Pallas kernels, scan_forward(): pl.pallas_call(forward_kernel, grid=(seqs, blocks), in_specs=[rows, row_s...  32.6 us
    dot_general x7, matrix products, mm(): lax.dot_general(left, right, (dims, ((), ())), preferred_element_type=F32)  31.6 us
    unnamed x57, local copies, waits for them, and re-layouts  16.9 us
  transfers between devices with their start and end apart: 3, of which 0 were waited for; matrix products, arithmetic and copies ran while one was open for 14% of the time, Pallas kernels for 58%

profile of v7, /device:TPU:9, one launch (start us, length us, event | category | flops | bytes accessed | tf_op | source)
XLA Modules:
  0.0 476.4 jit_solution(18261252090984403391)
XLA Ops:
  13.8 95.9 %gather_in.1 = (bf16[1,1024,2048]{2,1,0:T(8,128)(2,1)S(1)}, bf16[8,256,2048]{2,1,0:T(8,128)(2,1)}, bf16[8,128,2048]{2,1,0:T(8,128)(2,1)}, bf16[8,128,160]{2,1,0:...) custom-call(bf16[1,256,2048]{2,1,0:T(8,128)(2,1)S(1)} %copy-done.4, ...), custom_call_target="tpu_custom_call" | custom-call | tf_op jit(solution)/shard_map/gather_in/pallas_call | solution.py:643
  109.7 1.9 copy-done.5
  114.0 2.0 slice_bitcast_fusion
  116.1 4.9 %fusion.27 = (bf16[1024,1024]{1,0:T(8,128)(2,1)S(1)}, f32[1,1024,1024]{2,1,0:T(8,128)S(1)}) fusion(f32[1024]{0:T(1024)S(1)} %bitcast.154, bf16[1024,2048]{1,0:T(8,128)(2,1)S(1)} %copy-done, pred[1024]{0:T(1024)(128)(4,1)S(1)} %get-tuple-element.131, f32[1024]{0:T(1024)S(1)} %bitcast.156, pred[1024]{0:T(1024)(128)(4,1)S(1)} %get-tuple-element.132, ...), kind=kLoop, calls=%fused_computation.41 | loop fusion | flops 22020096 | bytes 10510336 | tf_op jit(solution)/shard_map/convert_element_type | solution.py:1240
  122.9 40.7 %reduce_seq.2 = (bf16[1024,128]{1,0:T(8,128)(2,1)S(1)}, f32[4,32,256]{2,1,0:T(8,128)S(1)}) custom-call(bf16[1024,128]{1,0:T(8,128)(2,1)S(1)} %convolution_convert_fusion.1.refs_0_, f32[4,32,256]{2,1,0:T(8,128)S(1)} %fusion.36.refs_1_), custom_call_target="tpu_custom_call" | custom-call | tf_op jit(solution)/shard_map/reduce_seq/pallas_call | solution.py:1172
  164.8 3.9 broadcast_in_dim.123.key_ref
  168.7 3.9 broadcast_in_dim.124.query_ref
  173.1 32.6 %scan_forward.1 = (bf16[16384,1024]{1,0:T(8,128)(2,1)}, f32[1024,1024]{1,0:T(8,128)S(1)}, bf16[1024,1024]{1,0:T(8,128)(2,1)S(1)}) custom-call(bf16[1024,1024]{1,0:T(8,128)(2,1)S(1)} %get-tuple-element.118.xc_ref, bf16[1024,2048]{1,0:T(8,128)(2,1)S(1)} %copy-done.1, bf16[1024,128]{1,0:T(8,128)(2,1)S(1)} %copy-done.9, ...), custom_call_target="tpu_custom_call" | custom-call | flops 1006632960 | bytes 46137344 | tf_op jit(solution)/shard_map/scan_forward/pallas_call | solution.py:320
  205.7 2.0 copy-done.6
  209.0 6.1 %convert_bitcast_fusion = bf16[1,1024,2048]{2,1,0:T(8,128)(2,1)} fusion(bf16[1024,1024]{1,0:T(8,128)(2,1)S(1)} %get-tuple-element.50, bf16[1024,2048]{1,0:T(8,128)(2,1)S(1)} %bitcast.168), kind=kOutput, calls=%fused_computation.48 | convolution fusion | flops 4297064448 | bytes 10485760 | tf_op jit(solution)/shard_map/dot_general | solution.py:38
  215.1 10.0 %fusion.22.dg_ref = f32[1024,1024]{1,0:T(8,128)} fusion(bf16[1024,2048]{1,0:T(8,128)(2,1)} %bitcast.167, bf16[1,1024,2048]{2,1,0:T(8,128)(2,1)} %all-gather.2.cloned.1.call-done), kind=kOutput, calls=%fused_computation.33 | convolution fusion | flops 4294967296 | bytes 12582912 | tf_op jit(solution)/shard_map/dot_general | solution.py:38
  225.1 67.5 %scan_backward.1 = (bf16[1024,1024]{1,0:T(8,128)(2,1)S(1)}, f32[1024,1024]{1,0:T(8,128)}, f32[128,128]{1,0:T(8,128)S(1)}, f32[128,128]{1,0:T(8,128)S(1)}, f32[10...) custom-call(f32[1024,1024]{1,0:T(8,128)} %fusion.22.dg_ref, ...), custom_call_target="tpu_custom_call" | custom-call | flops 1677721600 | bytes 58720256 | tf_op jit(solution)/shard_map/scan_backward/pallas_call | solution.py:357
  295.0 7.4 %fusion.31 = bf16[1024,2048]{1,0:T(8,128)(2,1)S(1)} fusion(bf16[1024,1024]{1,0:T(8,128)(2,1)} %copy-done.15, bf16[1,1024,2048]{2,1,0:T(8,128)(2,1)} %all-gather.2.cloned.1.call-done), kind=kOutput, calls=%fused_computation.50 | convolution fusion | flops 4297064448 | bytes 10485760 | tf_op jit(solution)/shard_map/dot_general | solution.py:38
  302.5 32.4 %reduce_seq.3 = (bf16[1024,128]{1,0:T(8,128)(2,1)S(1)}, f32[4,32,256]{2,1,0:T(8,128)S(1)}, bf16[128,2048]{1,0:T(8,128)(2,1)S(1)}) custom-call(bf16[1024,128]{1,0:T(8,128)(2,1)S(1)} %convert_element_type.144.refs_0_, f32[4,32,256]{2,1,0:T(8,128)S(1)} %bitcast.137, bf16[8,128,2048]{2,1,0:T(8,128)(2,1)S(1)} %bitcast.133), custom_call_target="tpu_custom_call" | custom-call | tf_op jit(solution)/shard_map/reduce_seq/pallas_call | solution.py:1172
  335.0 3.1 collective-permute-start
  338.1 5.7 %fusion.52 = (bf16[1024]{0:T(1024)(128)(2,1)S(1)}, bf16[1024]{0:T(1024)(128)(2,1)S(1)}, f32[1024,1024]{1,0:T(8,128)S(1)}) fusion(bf16[1024,2048]{1,0:T(8,128)(2,1)} %get-tuple-element.45.z_ref, pred[1024]{0:T(1024)(128)(4,1)S(1)} %get-tuple-element.131, f32[1,1024,1024]{2,1,0:T(8,128)} %copy-done.20, f32[1024,1024]{1,0:T(8,128)} %get-tuple-element.61, ...), kind=kOutput, calls=%fused_computation.101 | convolution fusion | flops 350877696 | bytes 15340544 | tf_op jit(solution)/shard_map/dot_general | solution.py:38
  343.8 2.9 fusion.16
  346.7 3.9 fusion.34.refs_0_
  353.8 101.9 %scatter_out.1 = (bf16[1,256,2048]{2,1,0:T(8,128)(2,1)}, f32[256,2048]{1,0:T(8,128)}, bf16[128,160]{1,0:T(8,128)(2,1)}, bf16[128,128]{1,0:T(8,128)(2,1)}, bf16[16,128]{1,0:T(8,128)(2,1)}, /*index=5*/f32[1,2048]{1,0:T(1,128)}) custom-call(bf16[1024,1024]{1,0:T(8,128)(2,1)} %fusion.34.refs_0_, bf16[1024,1024]{1,0:T(8,128)(2,1)} %copy-done.7, ...), custom_call_target="tpu_custom_call" | custom-call | tf_op jit(solution)/shard_map/scatter_out/pallas_call | solution.py:1019
  455.7 1.4 slice.126
  457.7 1.6 copy.54
  459.3 1.4 convert_element_type.158
  461.2 2.2 convert_element_type.159
  463.5 2.9 add_convert_fusion
  (107 shorter events, 23.4 us)
Async XLA Ops:
  7.2 207.9 %all-gather.2.cloned.1.call-start = ((), (), s32[]{:S(2)}) async-start(), calls=%async_computation.2 | async-start | bytes 5242880 | tf_op jit(solution)/shard_map/all_gather | solution.py:1222
  8.8 112.1 %copy-start.13 = (bf16[1,2048]{1,0:T(2,128)(2,1)}, bf16[1,2048]{1,0:T(2,128)(2,1)S(1)}, u32[]{:S(2)}) copy-start(bf16[1,2048]{1,0:T(2,128)(2,1)S(1)} %reshape.267.refs_6_.refs_10_) | copy-start | bytes 12292
  9.5 1.2 copy-start.4
  109.7 1.9 copy-start.5
  111.6 10.1 %copy-start.16 = (bf16[8,128,160]{2,1,0:T(8,128)(2,1)}, bf16[8,128,160]{2,1,0:T(8,128)(2,1)S(1)}, u32[]{:S(2)}) copy-start(bf16[8,128,160]{2,1,0:T(8,128)(2,1)S(1)} %get-tuple-element.46) | copy-start | bytes 983044
  111.6 351.8 %reduce-scatter.2.cloned.1.call-start = ((), (), s32[]{:S(2)}) async-start(), calls=%async_computation.1 | async-start | bytes 5242880 | tf_op jit(solution)/shard_map/reduce_scatter | solution.py:1254
  113.1 3.0 copy-start
  116.0 4.9 %copy-start.18 = (bf16[1,1024,1024]{2,1,0:T(8,128)(2,1)}, bf16[1,1024,1024]{2,1,0:T(8,128)(2,1)S(1)}, u32[]{:S(2)}) copy-start(bf16[1,1024,1024]{2,1,0:T(8,128)(2,1)S(1)} %slice_bitcast_fusion) | copy-start | bytes 6291460
  121.0 42.7 %copy-start.20 = (f32[1,1024,1024]{2,1,0:T(8,128)}, f32[1,1024,1024]{2,1,0:T(8,128)S(1)}, u32[]{:S(2)}) copy-start(f32[1,1024,1024]{2,1,0:T(8,128)S(1)} %get-tuple-element.119) | copy-start | bytes 12582916
  121.0 52.1 %copy-start.2 = (bf16[1024,1024]{1,0:T(8,128)(2,1)}, bf16[1024,1024]{1,0:T(8,128)(2,1)S(1)}, u32[]{:S(2)}) copy-start(bf16[1024,1024]{1,0:T(8,128)(2,1)S(1)} %get-tuple-element.118.xc_ref) | copy-start | bytes 6291460
  164.8 8.3 %copy-start.1 = (bf16[1024,2048]{1,0:T(8,128)(2,1)S(1)}, bf16[1024,2048]{1,0:T(8,128)(2,1)}, u32[]{:S(2)}) copy-start(bf16[1024,2048]{1,0:T(8,128)(2,1)} %get-tuple-element.45.z_ref) | copy-start | bytes 12582916
  164.8 8.3 %copy-start.9 = (bf16[1024,128]{1,0:T(8,128)(2,1)S(1)}, bf16[1024,128]{1,0:T(8,128)(2,1)}, u32[]{:S(2)}) copy-start(bf16[1024,128]{1,0:T(8,128)(2,1)} %copy-done.8) | copy-start | bytes 786436
  173.1 35.9 %copy-start.24 = (bf16[8,128,2048]{2,1,0:T(8,128)(2,1)S(1)}, bf16[8,128,2048]{2,1,0:T(8,128)(2,1)}, u32[]{:S(2)}) copy-start(bf16[8,128,2048]{2,1,0:T(8,128)(2,1)} %get-tuple-element.51) | copy-start | bytes 12582916
  205.7 2.0 copy-start.6
  207.7 1.3 copy-start.15
  215.1 10.1 %copy-start.10 = (bf16[1024,128]{1,0:T(8,128)(2,1)S(1)}, bf16[1024,128]{1,0:T(8,128)(2,1)}, u32[]{:S(2)}) copy-start(bf16[1024,128]{1,0:T(8,128)(2,1)} %copy-done.8) | copy-start | bytes 786436
  292.7 1.3 copy-start.7
  302.4 35.7 %copy-start.17 = (bf16[8,128,160]{2,1,0:T(8,128)(2,1)S(1)}, bf16[8,128,160]{2,1,0:T(8,128)(2,1)}, u32[]{:S(2)}) copy-start(bf16[8,128,160]{2,1,0:T(8,128)(2,1)} %copy-done.16) | copy-start | bytes 983044
  335.0 126.2 %collective-permute-start = (bf16[128,2048]{1,0:T(8,128)(2,1)S(1)}, bf16[128,2048]{1,0:T(8,128)(2,1)}, u32[]{:S(2)}, u32[]{:S(2)}) collective-permute-start(bf16[128,2048]{1,0:T(8,128)(2,1)S(1)} %get-tuple-element.74), channel_id=1, source_target_pairs={{0,0},{4,1},{1,2},{5,3},{2,4},{6,5},{3,6},{7,7},{8,8},{12,9},{9,10... | collective-permute-start | bytes 1572872 | tf_op jit(solution)/shard_map/ppermute | solution.py:1265
  338.1 5.7 %copy-start.19 = (bf16[1,1024,1024]{2,1,0:T(8,128)(2,1)S(1)}, bf16[1,1024,1024]{2,1,0:T(8,128)(2,1)}, u32[]{:S(2)}) copy-start(bf16[1,1024,1024]{2,1,0:T(8,128)(2,1)} %copy-done.18) | copy-start | bytes 6291460
  346.7 4.0 copy-start.3
  455.6 11.7 %copy-start.23 = (f32[1,2048]{1,0:T(1,128)S(1)}, f32[1,2048]{1,0:T(1,128)}, u32[]{:S(2)}) copy-start(f32[1,2048]{1,0:T(1,128)} %get-tuple-element.69) | copy-start | bytes 24580
  455.6 12.3 %copy-start.21 = (f32[256,2048]{1,0:T(8,128)S(1)}, f32[256,2048]{1,0:T(8,128)}, u32[]{:S(2)}) copy-start(f32[256,2048]{1,0:T(8,128)} %get-tuple-element.150) | copy-start | bytes 6291460
  461.2 5.1 %copy-start.22 = (bf16[1,256,2048]{2,1,0:T(8,128)(2,1)S(1)}, bf16[1,256,2048]{2,1,0:T(8,128)(2,1)}, u32[]{:S(2)}) copy-start(bf16[1,256,2048]{2,1,0:T(8,128)(2,1)} %get-tuple-element.148) | copy-start | bytes 3145732
  (4 other events, 3.7 us)
Sparse Core Ops, SparseCore 0:
  111.8 92.5 all-gather.1
  215.2 79.8 reduce-scatter.1

commit v8 on v7

--- a/solution.py
+++ b/solution.py
@@ -702,29 +702,6 @@
     from_d, from_s = forward_home(d, s, seq)
     moves = jnp.logical_or(to_d != d, to_s != s)
 
-    for k in range(1, seq):
-        greet((d, lax.rem(s + k, seq)))
-    for k in range(1, pairs):
-        greet((lax.rem(d + 2 * k, dp), s))
-    greet((mate(d), s))
-    greet((to_d, to_s), moves)
-    greet((from_d, from_s), moves)
-    pl.semaphore_wait(pltpu.get_barrier_semaphore(), seq - 1 + pairs + jnp.where(moves, 2, 0))
-
-    def swap(src, dst, send, recv, j):
-        return remote(src, dst.at[j], send.at[j], recv.at[j], (mate(d), s))
-
-    def part_swap(m, j):
-        return swap(parts[m].at[2 * j + 1 - odd], p_x[m], px_send.at[m], px_recv.at[m], j)
-
-    def part_fetch(m, j):
-        return pltpu.make_async_copy(parts[m].at[2 * j + odd], p_own[m].at[j], p_load.at[m, j])
-
-    for m in range(count):
-        for j in range(pairs):
-            part_swap(m, j).start()
-            part_fetch(m, j).start()
-
     if fused:
         d_pre, normed, w_all, x_buf, gw_give, f_sem, x_sem = take(7)
         channels = dx_ref.shape[1]
@@ -736,21 +713,56 @@
         ]
         for copy in loads:
             copy.start()
+
+    for k in range(1, seq):
+        greet((d, lax.rem(s + k, seq)))
+    for k in range(1, pairs):
+        greet((lax.rem(d + 2 * k, dp), s))
+    greet((mate(d), s))
+    greet((to_d, to_s), moves)
+    greet((from_d, from_s), moves)
+    pl.semaphore_wait(pltpu.get_barrier_semaphore(), seq - 1 + pairs + jnp.where(moves, 2, 0))
+
+    def swap(src, dst, send, recv, j):
+        return remote(src, dst.at[j], send.at[j], recv.at[j], (mate(d), s))
+
+    def part_swap(m, j):
+        return swap(parts[m].at[2 * j + 1 - odd], p_x[m], px_send.at[m], px_recv.at[m], j)
+
+    def part_fetch(m, j):
+        return pltpu.make_async_copy(parts[m].at[2 * j + odd], p_own[m].at[j], p_load.at[m, j])
+
+    for m in range(count):
+        for j in range(pairs):
+            part_swap(m, j).start()
+            part_fetch(m, j).start()
+
+    if fused:
         for copy in loads[:3]:
             copy.wait()
         g_in[...] = jnp.zeros_like(g_in)
         w_rows = gw_own.shape[1]
         half_width = width // 2
 
+        def chunk_of(i):
+            return jnp.where(lax.rem(i, 2) == 0, seq - 1 - i // 2, i // 2)
+
         def dn_tasks(first, last):
             def run(i, carried):
-                r = jnp.where(lax.rem(i, 2) == 0, seq - 1 - i // 2, i // 2)
+                r = chunk_of(i)
                 rows = pl.ds(pl.multiple_of(r * part, part), part)
-                fetch = pltpu.make_async_copy(full_ref.at[rows], x_buf, x_sem)
-                fetch.start()
                 for at in range(2):
                     cols = pl.ds(at * half_width, half_width)
                     own[r, 0, :, cols] = mm(d_pre[rows, :], w_all[:, cols], NN).astype(BF)
+                return carried
+
+            lax.fori_loop(first, last, run, 0)
+
+        def gain_tasks(first, last):
+            def run(i, carried):
+                r = chunk_of(i)
+                fetch = pltpu.make_async_copy(full_ref.at[pl.ds(pl.multiple_of(r * part, part), part)], x_buf, x_sem)
+                fetch.start()
                 fetch.wait()
 
                 def fold(at, carried):
@@ -917,7 +929,9 @@
         gw_away()
         gw_home()
         gw_join()
+        gain_tasks(0, 2)
         dn_tasks(2, seq)
+        gain_tasks(2, seq)
     else:
         begin()
         part_join()

time: 483 us -> 479 us (level)
  Pallas kernels: 371 us -> 366 us
  transfers between devices with their start and end apart: 3 -> 3, of which waited for: 0 -> 0; matrix products, arithmetic and copies ran while one was open for 14% -> 14% of each run, Pallas kernels for 58% -> 57%
where the time goes in v8:
time: 479 us; the launch traced here: 472 us
  Pallas kernels  366 us (76%)
  local copies, waits for them, and re-layouts  32.8 us (7%)
  matrix products  31.6 us (7%)
  other arithmetic  22.4 us (5%)
  between operations  14.8 us (3%)
    pallas_call x1, Pallas kernels, scatter(): pl.pallas_call(functools.partial(scatter_kernel, dp, seq, len(parts), fus...  97.3 us
    pallas_call x1, Pallas kernels, gather(): pl.pallas_call(functools.partial(gather_kernel, dp, seq, fused), in_specs...  95.9 us
    pallas_call x2, Pallas kernels, reduce_over_seq(): pl.pallas_call(functools.partial(reduce_kernel, dp, seq, grads is not Non...  73.1 us
    pallas_call x1, Pallas kernels, scan_backward(): pl.pallas_call(backward_kernel, grid=(seqs, blocks), in_specs=[rows, rows...  67.5 us
    pallas_call x1, Pallas kernels, scan_forward(): pl.pallas_call(forward_kernel, grid=(seqs, blocks), in_specs=[rows, row_s...  32.6 us
    dot_general x7, matrix products, mm(): lax.dot_general(left, right, (dims, ((), ())), preferred_element_type=F32)  31.6 us
    unnamed x57, local copies, waits for them, and re-layouts  16.9 us
  transfers between devices with their start and end apart: 3, of which 0 were waited for; matrix products, arithmetic and copies ran while one was open for 14% of the time, Pallas kernels for 57%

profile of v8, /device:TPU:9, one launch (start us, length us, event | category | flops | bytes accessed | tf_op | source)
XLA Modules:
  0.0 471.9 jit_solution(1944611736626655933)
XLA Ops:
  13.8 95.9 %gather_in.1 = (bf16[1,1024,2048]{2,1,0:T(8,128)(2,1)S(1)}, bf16[8,256,2048]{2,1,0:T(8,128)(2,1)}, bf16[8,128,2048]{2,1,0:T(8,128)(2,1)}, bf16[8,128,160]{2,1,0:...) custom-call(bf16[1,256,2048]{2,1,0:T(8,128)(2,1)S(1)} %copy-done.4, ...), custom_call_target="tpu_custom_call" | custom-call | tf_op jit(solution)/shard_map/gather_in/pallas_call | solution.py:643
  109.7 1.9 copy-done.5
  114.0 2.0 slice_bitcast_fusion
  116.1 4.9 %fusion.27 = (bf16[1024,1024]{1,0:T(8,128)(2,1)S(1)}, f32[1,1024,1024]{2,1,0:T(8,128)S(1)}) fusion(f32[1024]{0:T(1024)S(1)} %bitcast.154, bf16[1024,2048]{1,0:T(8,128)(2,1)S(1)} %copy-done, pred[1024]{0:T(1024)(128)(4,1)S(1)} %get-tuple-element.131, f32[1024]{0:T(1024)S(1)} %bitcast.156, pred[1024]{0:T(1024)(128)(4,1)S(1)} %get-tuple-element.132, ...), kind=kLoop, calls=%fused_computation.41 | loop fusion | flops 22020096 | bytes 10510336 | tf_op jit(solution)/shard_map/convert_element_type | solution.py:1254
  122.9 40.7 %reduce_seq.2 = (bf16[1024,128]{1,0:T(8,128)(2,1)S(1)}, f32[4,32,256]{2,1,0:T(8,128)S(1)}) custom-call(bf16[1024,128]{1,0:T(8,128)(2,1)S(1)} %convolution_convert_fusion.1.refs_0_, f32[4,32,256]{2,1,0:T(8,128)S(1)} %fusion.36.refs_1_), custom_call_target="tpu_custom_call" | custom-call | tf_op jit(solution)/shard_map/reduce_seq/pallas_call | solution.py:1186
  164.8 3.9 broadcast_in_dim.123.key_ref
  168.7 3.9 broadcast_in_dim.124.query_ref
  173.1 32.6 %scan_forward.1 = (bf16[16384,1024]{1,0:T(8,128)(2,1)}, f32[1024,1024]{1,0:T(8,128)S(1)}, bf16[1024,1024]{1,0:T(8,128)(2,1)S(1)}) custom-call(bf16[1024,1024]{1,0:T(8,128)(2,1)S(1)} %get-tuple-element.118.xc_ref, bf16[1024,2048]{1,0:T(8,128)(2,1)S(1)} %copy-done.1, bf16[1024,128]{1,0:T(8,128)(2,1)S(1)} %copy-done.9, ...), custom_call_target="tpu_custom_call" | custom-call | flops 1006632960 | bytes 46137344 | tf_op jit(solution)/shard_map/scan_forward/pallas_call | solution.py:320
  205.7 2.0 copy-done.6
  209.0 6.1 %convert_bitcast_fusion = bf16[1,1024,2048]{2,1,0:T(8,128)(2,1)} fusion(bf16[1024,1024]{1,0:T(8,128)(2,1)S(1)} %get-tuple-element.50, bf16[1024,2048]{1,0:T(8,128)(2,1)S(1)} %bitcast.168), kind=kOutput, calls=%fused_computation.48 | convolution fusion | flops 4297064448 | bytes 10485760 | tf_op jit(solution)/shard_map/dot_general | solution.py:38
  215.1 10.0 %fusion.22.dg_ref = f32[1024,1024]{1,0:T(8,128)} fusion(bf16[1024,2048]{1,0:T(8,128)(2,1)} %bitcast.167, bf16[1,1024,2048]{2,1,0:T(8,128)(2,1)} %all-gather.2.cloned.1.call-done), kind=kOutput, calls=%fused_computation.33 | convolution fusion | flops 4294967296 | bytes 12582912 | tf_op jit(solution)/shard_map/dot_general | solution.py:38
  225.1 67.5 %scan_backward.1 = (bf16[1024,1024]{1,0:T(8,128)(2,1)S(1)}, f32[1024,1024]{1,0:T(8,128)}, f32[128,128]{1,0:T(8,128)S(1)}, f32[128,128]{1,0:T(8,128)S(1)}, f32[10...) custom-call(f32[1024,1024]{1,0:T(8,128)} %fusion.22.dg_ref, ...), custom_call_target="tpu_custom_call" | custom-call | flops 1677721600 | bytes 58720256 | tf_op jit(solution)/shard_map/scan_backward/pallas_call | solution.py:357
  295.0 7.4 %fusion.31 = bf16[1024,2048]{1,0:T(8,128)(2,1)S(1)} fusion(bf16[1024,1024]{1,0:T(8,128)(2,1)} %copy-done.15, bf16[1,1024,2048]{2,1,0:T(8,128)(2,1)} %all-gather.2.cloned.1.call-done), kind=kOutput, calls=%fused_computation.50 | convolution fusion | flops 4297064448 | bytes 10485760 | tf_op jit(solution)/shard_map/dot_general | solution.py:38
  302.5 32.4 %reduce_seq.3 = (bf16[1024,128]{1,0:T(8,128)(2,1)S(1)}, f32[4,32,256]{2,1,0:T(8,128)S(1)}, bf16[128,2048]{1,0:T(8,128)(2,1)S(1)}) custom-call(bf16[1024,128]{1,0:T(8,128)(2,1)S(1)} %convert_element_type.144.refs_0_, f32[4,32,256]{2,1,0:T(8,128)S(1)} %bitcast.137, bf16[8,128,2048]{2,1,0:T(8,128)(2,1)S(1)} %bitcast.133), custom_call_target="tpu_custom_call" | custom-call | tf_op jit(solution)/shard_map/reduce_seq/pallas_call | solution.py:1186
  335.0 3.1 collective-permute-start
  338.1 5.7 %fusion.52 = (bf16[1024]{0:T(1024)(128)(2,1)S(1)}, bf16[1024]{0:T(1024)(128)(2,1)S(1)}, f32[1024,1024]{1,0:T(8,128)S(1)}) fusion(bf16[1024,2048]{1,0:T(8,128)(2,1)} %get-tuple-element.45.z_ref, pred[1024]{0:T(1024)(128)(4,1)S(1)} %get-tuple-element.131, f32[1,1024,1024]{2,1,0:T(8,128)} %copy-done.20, f32[1024,1024]{1,0:T(8,128)} %get-tuple-element.61, ...), kind=kOutput, calls=%fused_computation.101 | convolution fusion | flops 350877696 | bytes 15340544 | tf_op jit(solution)/shard_map/dot_general | solution.py:38
  343.8 2.9 fusion.16
  346.7 3.9 fusion.34.refs_0_
  353.8 97.3 %scatter_out.1 = (bf16[1,256,2048]{2,1,0:T(8,128)(2,1)}, f32[256,2048]{1,0:T(8,128)}, bf16[128,160]{1,0:T(8,128)(2,1)}, bf16[128,128]{1,0:T(8,128)(2,1)}, bf16[16,128]{1,0:T(8,128)(2,1)}, /*index=5*/f32[1,2048]{1,0:T(1,128)}) custom-call(bf16[1024,1024]{1,0:T(8,128)(2,1)} %fusion.34.refs_0_, bf16[1024,1024]{1,0:T(8,128)(2,1)} %copy-done.7, ...), custom_call_target="tpu_custom_call" | custom-call | tf_op jit(solution)/shard_map/scatter_out/pallas_call | solution.py:1033
  451.1 1.4 slice.126
  453.2 1.6 copy.54
  454.8 1.4 convert_element_type.158
  456.7 2.2 convert_element_type.159
  458.9 2.9 add_convert_fusion
  (107 shorter events, 23.4 us)
Async XLA Ops:
  7.2 207.9 %all-gather.2.cloned.1.call-start = ((), (), s32[]{:S(2)}) async-start(), calls=%async_computation.2 | async-start | bytes 5242880 | tf_op jit(solution)/shard_map/all_gather | solution.py:1236
  8.8 112.1 %copy-start.13 = (bf16[1,2048]{1,0:T(2,128)(2,1)}, bf16[1,2048]{1,0:T(2,128)(2,1)S(1)}, u32[]{:S(2)}) copy-start(bf16[1,2048]{1,0:T(2,128)(2,1)S(1)} %reshape.267.refs_6_.refs_10_) | copy-start | bytes 12292
  9.5 1.2 copy-start.4
  109.7 1.9 copy-start.5
  111.6 10.1 %copy-start.16 = (bf16[8,128,160]{2,1,0:T(8,128)(2,1)}, bf16[8,128,160]{2,1,0:T(8,128)(2,1)S(1)}, u32[]{:S(2)}) copy-start(bf16[8,128,160]{2,1,0:T(8,128)(2,1)S(1)} %get-tuple-element.46) | copy-start | bytes 983044
  111.6 347.3 %reduce-scatter.2.cloned.1.call-start = ((), (), s32[]{:S(2)}) async-start(), calls=%async_computation.1 | async-start | bytes 5242880 | tf_op jit(solution)/shard_map/reduce_scatter | solution.py:1268
  113.1 3.0 copy-start
  116.0 4.9 %copy-start.18 = (bf16[1,1024,1024]{2,1,0:T(8,128)(2,1)}, bf16[1,1024,1024]{2,1,0:T(8,128)(2,1)S(1)}, u32[]{:S(2)}) copy-start(bf16[1,1024,1024]{2,1,0:T(8,128)(2,1)S(1)} %slice_bitcast_fusion) | copy-start | bytes 6291460
  121.0 42.7 %copy-start.20 = (f32[1,1024,1024]{2,1,0:T(8,128)}, f32[1,1024,1024]{2,1,0:T(8,128)S(1)}, u32[]{:S(2)}) copy-start(f32[1,1024,1024]{2,1,0:T(8,128)S(1)} %get-tuple-element.119) | copy-start | bytes 12582916
  121.0 52.1 %copy-start.2 = (bf16[1024,1024]{1,0:T(8,128)(2,1)}, bf16[1024,1024]{1,0:T(8,128)(2,1)S(1)}, u32[]{:S(2)}) copy-start(bf16[1024,1024]{1,0:T(8,128)(2,1)S(1)} %get-tuple-element.118.xc_ref) | copy-start | bytes 6291460
  164.8 8.3 %copy-start.1 = (bf16[1024,2048]{1,0:T(8,128)(2,1)S(1)}, bf16[1024,2048]{1,0:T(8,128)(2,1)}, u32[]{:S(2)}) copy-start(bf16[1024,2048]{1,0:T(8,128)(2,1)} %get-tuple-element.45.z_ref) | copy-start | bytes 12582916
  164.8 8.3 %copy-start.9 = (bf16[1024,128]{1,0:T(8,128)(2,1)S(1)}, bf16[1024,128]{1,0:T(8,128)(2,1)}, u32[]{:S(2)}) copy-start(bf16[1024,128]{1,0:T(8,128)(2,1)} %copy-done.8) | copy-start | bytes 786436
  173.1 35.9 %copy-start.24 = (bf16[8,128,2048]{2,1,0:T(8,128)(2,1)S(1)}, bf16[8,128,2048]{2,1,0:T(8,128)(2,1)}, u32[]{:S(2)}) copy-start(bf16[8,128,2048]{2,1,0:T(8,128)(2,1)} %get-tuple-element.51) | copy-start | bytes 12582916
  205.7 2.0 copy-start.6
  207.7 1.3 copy-start.15
  215.1 10.1 %copy-start.10 = (bf16[1024,128]{1,0:T(8,128)(2,1)S(1)}, bf16[1024,128]{1,0:T(8,128)(2,1)}, u32[]{:S(2)}) copy-start(bf16[1024,128]{1,0:T(8,128)(2,1)} %copy-done.8) | copy-start | bytes 786436
  292.7 1.3 copy-start.7
  302.4 35.7 %copy-start.17 = (bf16[8,128,160]{2,1,0:T(8,128)(2,1)S(1)}, bf16[8,128,160]{2,1,0:T(8,128)(2,1)}, u32[]{:S(2)}) copy-start(bf16[8,128,160]{2,1,0:T(8,128)(2,1)} %copy-done.16) | copy-start | bytes 983044
  335.0 121.7 %collective-permute-start = (bf16[128,2048]{1,0:T(8,128)(2,1)S(1)}, bf16[128,2048]{1,0:T(8,128)(2,1)}, u32[]{:S(2)}, u32[]{:S(2)}) collective-permute-start(bf16[128,2048]{1,0:T(8,128)(2,1)S(1)} %get-tuple-element.74), channel_id=1, source_target_pairs={{0,0},{4,1},{1,2},{5,3},{2,4},{6,5},{3,6},{7,7},{8,8},{12,9},{9,10... | collective-permute-start | bytes 1572872 | tf_op jit(solution)/shard_map/ppermute | solution.py:1279
  338.1 5.7 %copy-start.19 = (bf16[1,1024,1024]{2,1,0:T(8,128)(2,1)S(1)}, bf16[1,1024,1024]{2,1,0:T(8,128)(2,1)}, u32[]{:S(2)}) copy-start(bf16[1,1024,1024]{2,1,0:T(8,128)(2,1)} %copy-done.18) | copy-start | bytes 6291460
  346.7 4.0 copy-start.3
  451.1 11.7 %copy-start.23 = (f32[1,2048]{1,0:T(1,128)S(1)}, f32[1,2048]{1,0:T(1,128)}, u32[]{:S(2)}) copy-start(f32[1,2048]{1,0:T(1,128)} %get-tuple-element.69) | copy-start | bytes 24580
  451.1 12.3 %copy-start.21 = (f32[256,2048]{1,0:T(8,128)S(1)}, f32[256,2048]{1,0:T(8,128)}, u32[]{:S(2)}) copy-start(f32[256,2048]{1,0:T(8,128)} %get-tuple-element.150) | copy-start | bytes 6291460
  456.7 5.1 %copy-start.22 = (bf16[1,256,2048]{2,1,0:T(8,128)(2,1)S(1)}, bf16[1,256,2048]{2,1,0:T(8,128)(2,1)}, u32[]{:S(2)}) copy-start(bf16[1,256,2048]{2,1,0:T(8,128)(2,1)} %get-tuple-element.148) | copy-start | bytes 3145732
  (4 other events, 3.7 us)
Sparse Core Ops, SparseCore 0:
  111.8 92.5 all-gather.1
  215.2 79.8 reduce-scatter.1

commit v9 on v8

--- a/solution.py
+++ b/solution.py
@@ -334,7 +334,7 @@
         cost_estimate=pl.CostEstimate(
             flops=tokens * channels * N * 60, bytes_accessed=tokens * channels * 44, transcendentals=0
         ),
-        compiler_params=pltpu.CompilerParams(vmem_limit_bytes=40 << 20),
+        compiler_params=pltpu.CompilerParams(vmem_limit_bytes=28 << 20),
         name="scan_forward",
     )(xc, pre, rate, key_lanes, query_lanes, keep_lanes, ksum_lanes, w_dt, vectors)
 
@@ -383,7 +383,7 @@
         cost_estimate=pl.CostEstimate(
             flops=tokens * channels * N * 100, bytes_accessed=tokens * channels * 56, transcendentals=0
         ),
-        compiler_params=pltpu.CompilerParams(vmem_limit_bytes=48 << 20),
+        compiler_params=pltpu.CompilerParams(vmem_limit_bytes=36 << 20),
         name="scan_backward",
     )(d_gated, y, xc, pre, rate, key_lanes, query_lanes, keep_lanes, ksum_lanes, w_dt, vectors, states, states)
 

time: 479 us -> 486 us (1.015)
  local copies, waits for them, and re-layouts: 32.8 us -> 41.7 us
    unnamed x57 -> x79, local copies, waits for them, and re-layouts: 16.9 us -> 22.4 us
  transfers between devices with their start and end apart: 3 -> 3, of which waited for: 0 -> 0; matrix products, arithmetic and copies ran while one was open for 14% -> 15% of each run, Pallas kernels for 57% -> 56%
where the time goes in v9:
time: 486 us; the launch traced here: 479 us
  Pallas kernels  364 us (75%)
  local copies, waits for them, and re-layouts  41.7 us (9%)
  matrix products  30.5 us (6%)
  other arithmetic  24.3 us (5%)
  between operations  14.9 us (3%)
    pallas_call x1, Pallas kernels, scatter(): pl.pallas_call(functools.partial(scatter_kernel, dp, seq, len(parts), fus...  97 us
    pallas_call x1, Pallas kernels, gather(): pl.pallas_call(functools.partial(gather_kernel, dp, seq, fused), in_specs...  95.9 us
    pallas_call x2, Pallas kernels, reduce_over_seq(): pl.pallas_call(functools.partial(reduce_kernel, dp, seq, grads is not Non...  72.5 us
    pallas_call x1, Pallas kernels, scan_backward(): pl.pallas_call(backward_kernel, grid=(seqs, blocks), in_specs=[rows, rows...  67.3 us
    pallas_call x1, Pallas kernels, scan_forward(): pl.pallas_call(forward_kernel, grid=(seqs, blocks), in_specs=[rows, row_s...  31.2 us
    dot_general x7, matrix products, mm(): lax.dot_general(left, right, (dims, ((), ())), preferred_element_type=F32)  30.5 us
    unnamed x79, local copies, waits for them, and re-layouts  22.4 us
  transfers between devices with their start and end apart: 3, of which 0 were waited for; matrix products, arithmetic and copies ran while one was open for 15% of the time, Pallas kernels for 56%

profile of v9, /device:TPU:9, one launch (start us, length us, event | category | flops | bytes accessed | tf_op | source)
XLA Modules:
  0.0 478.9 jit_solution(1361002229003236796)
XLA Ops:
  13.8 95.9 %gather_in.1 = (bf16[1,1024,2048]{2,1,0:T(8,128)(2,1)S(1)}, bf16[8,256,2048]{2,1,0:T(8,128)(2,1)}, bf16[8,128,2048]{2,1,0:T(8,128)(2,1)}, bf16[8,128,160]{2,1,0:...) custom-call(bf16[1,256,2048]{2,1,0:T(8,128)(2,1)S(1)} %copy-done.4, ...), custom_call_target="tpu_custom_call" | custom-call | tf_op jit(solution)/shard_map/gather_in/pallas_call | solution.py:643
  109.7 1.9 copy-done.5
  114.1 2.0 slice_bitcast_fusion
  116.1 4.9 %fusion.27 = (bf16[1024,1024]{1,0:T(8,128)(2,1)S(1)}, f32[1,1024,1024]{2,1,0:T(8,128)S(1)}) fusion(f32[1024]{0:T(1024)S(1)} %bitcast.154, bf16[1024,2048]{1,0:T(8,128)(2,1)S(1)} %copy-done.2, pred[1024]{0:T(1024)(128)(4,1)S(1)} %get-tuple-element.131, f32[1024]{0:T(1024)S(1)} %bitcast.156, pred[1024]{0:T(1024)(128)(4,1)S(1)} %get-tuple-element.132, ...), kind=kLoop, calls=%fused_computation.41 | loop fusion | flops 22020096 | bytes 10510336 | tf_op jit(solution)/shard_map/convert_element_type | solution.py:1254
  123.0 40.8 %reduce_seq.2 = (bf16[1024,128]{1,0:T(8,128)(2,1)S(1)}, f32[4,32,256]{2,1,0:T(8,128)S(1)}) custom-call(bf16[1024,128]{1,0:T(8,128)(2,1)S(1)} %convolution_convert_fusion.1.refs_0_, f32[4,32,256]{2,1,0:T(8,128)S(1)} %fusion.36.refs_1_), custom_call_target="tpu_custom_call" | custom-call | tf_op jit(solution)/shard_map/reduce_seq/pallas_call | solution.py:1186
  165.5 4.5 broadcast_in_dim.123.key_ref
  170.0 4.5 broadcast_in_dim.124.query_ref
  174.9 31.2 %scan_forward.1 = (bf16[16384,1024]{1,0:T(8,128)(2,1)}, f32[1024,1024]{1,0:T(8,128)S(1)}, bf16[1024,1024]{1,0:T(8,128)(2,1)S(1)}) custom-call(bf16[1024,1024]{1,0:T(8,128)(2,1)S(1)} %get-tuple-element.118.xc_ref, bf16[1024,2048]{1,0:T(8,128)(2,1)S(1)} %copy-done.3, bf16[1024,128]{1,0:T(8,128)(2,1)S(1)} %copy-done.9, ...), custom_call_target="tpu_custom_call" | custom-call | flops 1006632960 | bytes 46137344 | tf_op jit(solution)/shard_map/scan_forward/pallas_call | solution.py:320
  206.2 2.0 copy-done.6
  209.5 6.1 %convert_bitcast_fusion = bf16[1,1024,2048]{2,1,0:T(8,128)(2,1)} fusion(bf16[1024,1024]{1,0:T(8,128)(2,1)S(1)} %get-tuple-element.50, bf16[1024,2048]{1,0:T(8,128)(2,1)S(1)} %bitcast.168), kind=kOutput, calls=%fused_computation.48 | convolution fusion | flops 4297064448 | bytes 10485760 | tf_op jit(solution)/shard_map/dot_general | solution.py:38
  215.6 7.6 %fusion.22.dg_ref = f32[1024,1024]{1,0:T(8,128)S(1)} fusion(bf16[1024,2048]{1,0:T(8,128)(2,1)} %bitcast.167, bf16[1,1024,2048]{2,1,0:T(8,128)(2,1)} %all-gather.2.cloned.1.call-done), kind=kOutput, calls=%fused_computation.33 | convolution fusion | flops 4294967296 | bytes 12582912 | tf_op jit(solution)/shard_map/dot_general | solution.py:38
  223.3 67.3 %scan_backward.1 = (bf16[1024,1024]{1,0:T(8,128)(2,1)S(1)}, f32[1024,1024]{1,0:T(8,128)S(1)}, f32[128,128]{1,0:T(8,128)S(1)}, f32[128,128]{1,0:T(8,128)S(1)}, f3...) custom-call(f32[1024,1024]{1,0:T(8,128)S(1)} %fusion.22.dg_ref, ...), custom_call_target="tpu_custom_call" | custom-call | flops 1677721600 | bytes 58720256 | tf_op jit(solution)/shard_map/scan_backward/pallas_call | solution.py:357
  293.5 1.9 copy-done.21
  299.8 7.4 %fusion.31 = bf16[1024,2048]{1,0:T(8,128)(2,1)S(1)} fusion(bf16[1024,1024]{1,0:T(8,128)(2,1)} %copy-done.22, bf16[1,1024,2048]{2,1,0:T(8,128)(2,1)} %all-gather.2.cloned.1.call-done), kind=kOutput, calls=%fused_computation.50 | convolution fusion | flops 4297064448 | bytes 10485760 | tf_op jit(solution)/shard_map/dot_general | solution.py:38
  307.2 31.7 %reduce_seq.3 = (bf16[1024,128]{1,0:T(8,128)(2,1)S(1)}, f32[4,32,256]{2,1,0:T(8,128)S(1)}, bf16[128,2048]{1,0:T(8,128)(2,1)S(1)}) custom-call(bf16[1024,128]{1,0:T(8,128)(2,1)S(1)} %convert_element_type.144.refs_0_, f32[4,32,256]{2,1,0:T(8,128)S(1)} %bitcast.137, bf16[8,128,2048]{2,1,0:T(8,128)(2,1)S(1)} %bitcast.133), custom_call_target="tpu_custom_call" | custom-call | tf_op jit(solution)/shard_map/reduce_seq/pallas_call | solution.py:1186
  340.5 2.9 collective-permute-start
  343.4 6.1 %fusion.52 = (bf16[1024]{0:T(1024)(128)(2,1)S(1)}, bf16[1024]{0:T(1024)(128)(2,1)S(1)}, f32[1024,1024]{1,0:T(8,128)S(1)}) fusion(bf16[1024,2048]{1,0:T(8,128)(2,1)} %get-tuple-element.45.z_ref, pred[1024]{0:T(1024)(128)(4,1)S(1)} %get-tuple-element.131, f32[1,1024,1024]{2,1,0:T(8,128)} %copy-done.29, f32[1024,1024]{1,0:T(8,128)} %copy-done.21, ...), kind=kOutput, calls=%fused_computation.101 | convolution fusion | flops 350877696 | bytes 15340544 | tf_op jit(solution)/shard_map/dot_general | solution.py:38
  349.5 2.9 fusion.16
  352.4 3.9 fusion.34.refs_0_
  357.7 2.0 copy.52
  361.2 97.0 %scatter_out.1 = (bf16[1,256,2048]{2,1,0:T(8,128)(2,1)}, f32[256,2048]{1,0:T(8,128)}, bf16[128,160]{1,0:T(8,128)(2,1)}, bf16[128,128]{1,0:T(8,128)(2,1)}, bf16[16,128]{1,0:T(8,128)(2,1)}, /*index=5*/f32[1,2048]{1,0:T(1,128)}) custom-call(bf16[1024,1024]{1,0:T(8,128)(2,1)} %fusion.34.refs_0_, bf16[1024,1024]{1,0:T(8,128)(2,1)} %copy-done.7, ...), custom_call_target="tpu_custom_call" | custom-call | tf_op jit(solution)/shard_map/scatter_out/pallas_call | solution.py:1033
  460.3 1.6 copy.54
  463.8 2.2 convert_element_type.159
  466.0 2.9 add_convert_fusion
  (129 shorter events, 32.8 us)
Async XLA Ops:
  7.2 208.4 %all-gather.2.cloned.1.call-start = ((), (), s32[]{:S(2)}) async-start(), calls=%async_computation.2 | async-start | bytes 5242880 | tf_op jit(solution)/shard_map/all_gather | solution.py:1236
  8.8 112.2 %copy-start.16 = (bf16[1,2048]{1,0:T(2,128)(2,1)}, bf16[1,2048]{1,0:T(2,128)(2,1)S(1)}, u32[]{:S(2)}) copy-start(bf16[1,2048]{1,0:T(2,128)(2,1)S(1)} %reshape.267.refs_6_.refs_10_) | copy-start | bytes 12292
  111.7 10.1 %copy-start.23 = (bf16[8,128,160]{2,1,0:T(8,128)(2,1)}, bf16[8,128,160]{2,1,0:T(8,128)(2,1)S(1)}, u32[]{:S(2)}) copy-start(bf16[8,128,160]{2,1,0:T(8,128)(2,1)S(1)} %get-tuple-element.46) | copy-start | bytes 983044
  111.7 354.3 %reduce-scatter.2.cloned.1.call-start = ((), (), s32[]{:S(2)}) async-start(), calls=%async_computation.1 | async-start | bytes 5242880 | tf_op jit(solution)/shard_map/reduce_scatter | solution.py:1268
  113.1 3.0 copy-start.2
  116.1 4.9 %copy-start.27 = (bf16[1,1024,1024]{2,1,0:T(8,128)(2,1)}, bf16[1,1024,1024]{2,1,0:T(8,128)(2,1)S(1)}, u32[]{:S(2)}) copy-start(bf16[1,1024,1024]{2,1,0:T(8,128)(2,1)S(1)} %slice_bitcast_fusion) | copy-start | bytes 6291460
  121.0 2.0 copy-start.29
  165.5 9.4 %copy-start.3 = (bf16[1024,2048]{1,0:T(8,128)(2,1)S(1)}, bf16[1024,2048]{1,0:T(8,128)(2,1)}, u32[]{:S(2)}) copy-start(bf16[1024,2048]{1,0:T(8,128)(2,1)} %get-tuple-element.45.z_ref) | copy-start | bytes 12582916
  165.5 9.4 %copy-start.9 = (bf16[1024,128]{1,0:T(8,128)(2,1)S(1)}, bf16[1024,128]{1,0:T(8,128)(2,1)}, u32[]{:S(2)}) copy-start(bf16[1024,128]{1,0:T(8,128)(2,1)} %copy-done.8) | copy-start | bytes 786436
  170.0 36.2 %copy-start = (bf16[1024,16,128]{2,1,0:T(8,128)(2,1)}, bf16[1024,16,128]{2,1,0:T(8,128)(2,1)S(1)}, u32[]{:S(2)}) copy-start(bf16[1024,16,128]{2,1,0:T(8,128)(2,1)S(1)} %broadcast_in_dim.123.key_ref) | copy-start | bytes 12582916
  174.5 31.7 %copy-start.1 = (bf16[1024,16,128]{2,1,0:T(8,128)(2,1)}, bf16[1024,16,128]{2,1,0:T(8,128)(2,1)S(1)}, u32[]{:S(2)}) copy-start(bf16[1024,16,128]{2,1,0:T(8,128)(2,1)S(1)} %broadcast_in_dim.124.query_ref) | copy-start | bytes 12582916
  174.9 34.5 %copy-start.35 = (bf16[8,128,2048]{2,1,0:T(8,128)(2,1)S(1)}, bf16[8,128,2048]{2,1,0:T(8,128)(2,1)}, u32[]{:S(2)}) copy-start(bf16[8,128,2048]{2,1,0:T(8,128)(2,1)} %get-tuple-element.51) | copy-start | bytes 12582916
  206.2 2.0 copy-start.6
  215.6 7.6 %copy-start.10 = (bf16[1024,128]{1,0:T(8,128)(2,1)S(1)}, bf16[1024,128]{1,0:T(8,128)(2,1)}, u32[]{:S(2)}) copy-start(bf16[1024,128]{1,0:T(8,128)(2,1)} %copy-done.8) | copy-start | bytes 786436
  307.2 36.2 %copy-start.24 = (bf16[8,128,160]{2,1,0:T(8,128)(2,1)S(1)}, bf16[8,128,160]{2,1,0:T(8,128)(2,1)}, u32[]{:S(2)}) copy-start(bf16[8,128,160]{2,1,0:T(8,128)(2,1)} %copy-done.23) | copy-start | bytes 983044
  340.5 123.3 %collective-permute-start = (bf16[128,2048]{1,0:T(8,128)(2,1)S(1)}, bf16[128,2048]{1,0:T(8,128)(2,1)}, u32[]{:S(2)}, u32[]{:S(2)}) collective-permute-start(bf16[128,2048]{1,0:T(8,128)(2,1)S(1)} %get-tuple-element.74), channel_id=1, source_target_pairs={{0,0},{4,1},{1,2},{5,3},{2,4},{6,5},{3,6},{7,7},{8,8},{12,9},{9,10... | collective-permute-start | bytes 1572872 | tf_op jit(solution)/shard_map/ppermute | solution.py:1279
  343.4 6.1 %copy-start.28 = (bf16[1,1024,1024]{2,1,0:T(8,128)(2,1)S(1)}, bf16[1,1024,1024]{2,1,0:T(8,128)(2,1)}, u32[]{:S(2)}) copy-start(bf16[1,1024,1024]{2,1,0:T(8,128)(2,1)} %copy-done.27) | copy-start | bytes 6291460
  352.4 3.9 copy-start.26
  352.4 3.9 copy-start.33
  356.3 3.3 copy-start.13
  356.3 4.1 copy-start.19
  458.2 11.7 %copy-start.34 = (f32[1,2048]{1,0:T(1,128)S(1)}, f32[1,2048]{1,0:T(1,128)}, u32[]{:S(2)}) copy-start(f32[1,2048]{1,0:T(1,128)} %get-tuple-element.69) | copy-start | bytes 24580
  458.2 12.3 %copy-start.30 = (f32[256,2048]{1,0:T(8,128)S(1)}, f32[256,2048]{1,0:T(8,128)}, u32[]{:S(2)}) copy-start(f32[256,2048]{1,0:T(8,128)} %get-tuple-element.150) | copy-start | bytes 6291460
  463.8 5.1 %copy-start.31 = (bf16[1,256,2048]{2,1,0:T(8,128)(2,1)S(1)}, bf16[1,256,2048]{2,1,0:T(8,128)(2,1)}, u32[]{:S(2)}) copy-start(bf16[1,256,2048]{2,1,0:T(8,128)(2,1)} %get-tuple-element.148) | copy-start | bytes 3145732
  (15 other events, 15.7 us)
Sparse Core Ops, SparseCore 0:
  111.8 92.5 all-gather.1
  215.7 79.6 reduce-scatter.1

commit v10 on v9

--- a/solution.py
+++ b/solution.py
@@ -334,7 +334,7 @@
         cost_estimate=pl.CostEstimate(
             flops=tokens * channels * N * 60, bytes_accessed=tokens * channels * 44, transcendentals=0
         ),
-        compiler_params=pltpu.CompilerParams(vmem_limit_bytes=28 << 20),
+        compiler_params=pltpu.CompilerParams(vmem_limit_bytes=46 << 20),
         name="scan_forward",
     )(xc, pre, rate, key_lanes, query_lanes, keep_lanes, ksum_lanes, w_dt, vectors)
 
@@ -383,7 +383,7 @@
         cost_estimate=pl.CostEstimate(
             flops=tokens * channels * N * 100, bytes_accessed=tokens * channels * 56, transcendentals=0
         ),
-        compiler_params=pltpu.CompilerParams(vmem_limit_bytes=36 << 20),
+        compiler_params=pltpu.CompilerParams(vmem_limit_bytes=54 << 20),
         name="scan_backward",
     )(d_gated, y, xc, pre, rate, key_lanes, query_lanes, keep_lanes, ksum_lanes, w_dt, vectors, states, states)
 

time: 486 us -> 482 us (level)
  local copies, waits for them, and re-layouts: 41.7 us -> 30.9 us
  Pallas kernels: 364 us -> 369 us
    unnamed x79 -> x89, local copies, waits for them, and re-layouts: 22.4 us -> 13.7 us
  transfers between devices with their start and end apart: 3 -> 3, of which waited for: 0 -> 0; matrix products, arithmetic and copies ran while one was open for 15% -> 15% of each run, Pallas kernels for 56% -> 57%
where the time goes in v10:
time: 482 us; the launch traced here: 475 us
  Pallas kernels  369 us (77%)
  matrix products  31.2 us (6%)
  local copies, waits for them, and re-layouts  30.9 us (6%)
  other arithmetic  25.2 us (5%)
  between operations  15.2 us (3%)
    pallas_call x1, Pallas kernels, scatter(): pl.pallas_call(functools.partial(scatter_kernel, dp, seq, len(parts), fus...  98.2 us
    pallas_call x1, Pallas kernels, gather(): pl.pallas_call(functools.partial(gather_kernel, dp, seq, fused), in_specs...  95.9 us
    pallas_call x2, Pallas kernels, reduce_over_seq(): pl.pallas_call(functools.partial(reduce_kernel, dp, seq, grads is not Non...  72.5 us
    pallas_call x1, Pallas kernels, scan_backward(): pl.pallas_call(backward_kernel, grid=(seqs, blocks), in_specs=[rows, rows...  69.8 us
    pallas_call x1, Pallas kernels, scan_forward(): pl.pallas_call(forward_kernel, grid=(seqs, blocks), in_specs=[rows, row_s...  32.7 us
    dot_general x7, matrix products, mm(): lax.dot_general(left, right, (dims, ((), ())), preferred_element_type=F32)  31.2 us
    unnamed x89, local copies, waits for them, and re-layouts  13.7 us
  transfers between devices with their start and end apart: 3, of which 0 were waited for; matrix products, arithmetic and copies ran while one was open for 15% of the time, Pallas kernels for 57%

profile of v10, /device:TPU:9, one launch (start us, length us, event | category | flops | bytes accessed | tf_op | source)
XLA Modules:
  0.0 475.3 jit_solution(1111297083647870103)
XLA Ops:
  13.8 95.9 %gather_in.1 = (bf16[1,1024,2048]{2,1,0:T(8,128)(2,1)S(1)}, bf16[8,256,2048]{2,1,0:T(8,128)(2,1)}, bf16[8,128,2048]{2,1,0:T(8,128)(2,1)}, bf16[8,128,160]{2,1,0:...) custom-call(bf16[1,256,2048]{2,1,0:T(8,128)(2,1)S(1)} %copy-done.2, ...), custom_call_target="tpu_custom_call" | custom-call | tf_op jit(solution)/shard_map/gather_in/pallas_call | solution.py:643
  109.7 1.9 copy-done.5
  114.4 1.8 slice_bitcast_fusion
  116.2 4.9 %fusion.27 = (bf16[1024,1024]{1,0:T(8,128)(2,1)S(1)}, f32[1,1024,1024]{2,1,0:T(8,128)S(1)}) fusion(f32[1024]{0:T(1024)S(1)} %bitcast.154, bf16[1024,2048]{1,0:T(8,128)(2,1)S(1)} %copy-done.18, pred[1024]{0:T(1024)(128)(4,1)S(1)} %get-tuple-element.131, f32[1024]{0:T(1024)S(1)} %bitcast.156, pred[1024]{0:T(1024)(128)(4,1)S(1)} %get-tuple-element.132, ...), kind=kLoop, calls=%fused_computation.41 | loop fusion | flops 22020096 | bytes 10510336 | tf_op jit(solution)/shard_map/convert_element_type | solution.py:1254
  123.1 40.9 %reduce_seq.2 = (bf16[1024,128]{1,0:T(8,128)(2,1)S(1)}, f32[4,32,256]{2,1,0:T(8,128)S(1)}) custom-call(bf16[1024,128]{1,0:T(8,128)(2,1)S(1)} %convolution_convert_fusion.1.refs_0_, f32[4,32,256]{2,1,0:T(8,128)S(1)} %fusion.36.refs_1_), custom_call_target="tpu_custom_call" | custom-call | tf_op jit(solution)/shard_map/reduce_seq/pallas_call | solution.py:1186
  165.2 3.9 broadcast_in_dim.123.key_ref
  169.1 3.9 broadcast_in_dim.124.query_ref
  173.4 32.7 %scan_forward.1 = (bf16[16384,1024]{1,0:T(8,128)(2,1)}, f32[1024,1024]{1,0:T(8,128)}, bf16[1024,1024]{1,0:T(8,128)(2,1)S(1)}) custom-call(bf16[1024,1024]{1,0:T(8,128)(2,1)S(1)} %get-tuple-element.118.xc_ref, bf16[1024,2048]{1,0:T(8,128)(2,1)} %get-tuple-element.45.z_ref, bf16[1024,128]{1,0:T(8,128)(2,1)S(1)} %copy-done.8, ...), custom_call_target="tpu_custom_call" | custom-call | flops 1006632960 | bytes 46137344 | tf_op jit(solution)/shard_map/scan_forward/pallas_call | solution.py:320
  207.5 6.0 %convert_bitcast_fusion = bf16[1,1024,2048]{2,1,0:T(8,128)(2,1)} fusion(bf16[1024,1024]{1,0:T(8,128)(2,1)S(1)} %get-tuple-element.50, bf16[1024,2048]{1,0:T(8,128)(2,1)S(1)} %bitcast.168), kind=kOutput, calls=%fused_computation.48 | convolution fusion | flops 4297064448 | bytes 10485760 | tf_op jit(solution)/shard_map/dot_general | solution.py:38
  213.6 10.2 %fusion.22.dg_ref = f32[1024,1024]{1,0:T(8,128)} fusion(bf16[1024,2048]{1,0:T(8,128)(2,1)} %bitcast.167, bf16[1,1024,2048]{2,1,0:T(8,128)(2,1)} %all-gather.2.cloned.1.call-done), kind=kOutput, calls=%fused_computation.33 | convolution fusion | flops 4294967296 | bytes 12582912 | tf_op jit(solution)/shard_map/dot_general | solution.py:38
  223.8 69.8 %scan_backward.1 = (bf16[1024,1024]{1,0:T(8,128)(2,1)}, f32[1024,1024]{1,0:T(8,128)}, f32[128,128]{1,0:T(8,128)}, f32[128,128]{1,0:T(8,128)}, f32[1024,128]{1,0:...) custom-call(f32[1024,1024]{1,0:T(8,128)} %fusion.22.dg_ref, ...), custom_call_target="tpu_custom_call" | custom-call | flops 1677721600 | bytes 58720256 | tf_op jit(solution)/shard_map/scan_backward/pallas_call | solution.py:357
  298.6 7.0 %fusion.31 = bf16[1024,2048]{1,0:T(8,128)(2,1)S(1)} fusion(bf16[1024,1024]{1,0:T(8,128)(2,1)S(1)} %copy-done.15, bf16[1,1024,2048]{2,1,0:T(8,128)(2,1)} %all-gather.2.cloned.1.call-done), kind=kOutput, calls=%fused_computation.50 | convolution fusion | flops 4297064448 | bytes 10485760 | tf_op jit(solution)/shard_map/dot_general | solution.py:38
  305.6 31.6 %reduce_seq.3 = (bf16[1024,128]{1,0:T(8,128)(2,1)S(1)}, f32[4,32,256]{2,1,0:T(8,128)S(1)}, bf16[128,2048]{1,0:T(8,128)(2,1)S(1)}) custom-call(bf16[1024,128]{1,0:T(8,128)(2,1)S(1)} %convert_element_type.144.refs_0_, f32[4,32,256]{2,1,0:T(8,128)S(1)} %bitcast.137, bf16[8,128,2048]{2,1,0:T(8,128)(2,1)S(1)} %bitcast.133), custom_call_target="tpu_custom_call" | custom-call | tf_op jit(solution)/shard_map/reduce_seq/pallas_call | solution.py:1186
  337.4 3.3 collective-permute-start
  340.7 5.5 %fusion.52 = (bf16[1024]{0:T(1024)(128)(2,1)S(1)}, bf16[1024]{0:T(1024)(128)(2,1)S(1)}, f32[1024,1024]{1,0:T(8,128)S(1)}) fusion(bf16[1024,2048]{1,0:T(8,128)(2,1)} %get-tuple-element.45.z_ref, pred[1024]{0:T(1024)(128)(4,1)S(1)} %copy-done.32, f32[1,1024,1024]{2,1,0:T(8,128)} %copy-done.21, f32[1024,1024]{1,0:T(8,128)} %get-tuple-element.61, ...), kind=kOutput, calls=%fused_computation.101 | convolution fusion | flops 350877696 | bytes 15340544 | tf_op jit(solution)/shard_map/dot_general | solution.py:38
  346.3 2.9 fusion.16
  349.2 3.9 fusion.34.refs_0_
  356.2 98.2 %scatter_out.1 = (bf16[1,256,2048]{2,1,0:T(8,128)(2,1)}, f32[256,2048]{1,0:T(8,128)}, bf16[128,160]{1,0:T(8,128)(2,1)}, bf16[128,128]{1,0:T(8,128)(2,1)}, bf16[16,128]{1,0:T(8,128)(2,1)}, /*index=5*/f32[1,2048]{1,0:T(1,128)}) custom-call(bf16[1024,1024]{1,0:T(8,128)(2,1)} %fusion.34.refs_0_, bf16[1024,1024]{1,0:T(8,128)(2,1)} %get-tuple-element.62.refs_1_, ...), custom_call_target="tpu_custom_call" | custom-call | tf_op jit(solution)/shard_map/scatter_out/pallas_call | solution.py:1033
  454.4 1.4 slice.126
  456.5 1.6 copy.54
  458.1 1.4 convert_element_type.158
  460.0 2.2 convert_element_type.159
  462.2 2.9 add_convert_fusion
  466.7 1.3 copy.70
  (139 shorter events, 25.0 us)
Async XLA Ops:
  7.2 206.4 %all-gather.2.cloned.1.call-start = ((), (), s32[]{:S(2)}) async-start(), calls=%async_computation.2 | async-start | bytes 5242880 | tf_op jit(solution)/shard_map/all_gather | solution.py:1236
  8.8 112.2 %copy-start.12 = (bf16[1,2048]{1,0:T(2,128)(2,1)}, bf16[1,2048]{1,0:T(2,128)(2,1)S(1)}, u32[]{:S(2)}) copy-start(bf16[1,2048]{1,0:T(2,128)(2,1)S(1)} %reshape.267.refs_6_.refs_10_) | copy-start | bytes 12292
  111.7 10.2 %copy-start.16 = (bf16[8,128,160]{2,1,0:T(8,128)(2,1)}, bf16[8,128,160]{2,1,0:T(8,128)(2,1)S(1)}, u32[]{:S(2)}) copy-start(bf16[8,128,160]{2,1,0:T(8,128)(2,1)S(1)} %get-tuple-element.46) | copy-start | bytes 983044
  111.7 61.7 %copy-start.6 = (bf16[8,128,128]{2,1,0:T(8,128)(2,1)}, bf16[8,128,128]{2,1,0:T(8,128)(2,1)S(1)}, u32[]{:S(2)}) copy-start(bf16[8,128,128]{2,1,0:T(8,128)(2,1)S(1)} %get-tuple-element.49) | copy-start | bytes 786436
  111.7 350.5 %reduce-scatter.2.cloned.1.call-start = ((), (), s32[]{:S(2)}) async-start(), calls=%async_computation.1 | async-start | bytes 5242880 | tf_op jit(solution)/shard_map/reduce_scatter | solution.py:1268
  114.3 6.8 %copy-start.31 = (pred[1024]{0:T(1024)(128)(4,1)}, pred[1024]{0:T(1024)(128)(4,1)S(1)}, u32[]{:S(2)}) copy-start(pred[1024]{0:T(1024)(128)(4,1)S(1)} %get-tuple-element.131) | copy-start | bytes 3076
  114.3 6.8 %copy-start.33 = (pred[1024]{0:T(1024)(128)(4,1)}, pred[1024]{0:T(1024)(128)(4,1)S(1)}, u32[]{:S(2)}) copy-start(pred[1024]{0:T(1024)(128)(4,1)S(1)} %get-tuple-element.132) | copy-start | bytes 3076
  114.3 6.8 %copy-start.35 = (pred[1024]{0:T(1024)(128)(4,1)}, pred[1024]{0:T(1024)(128)(4,1)S(1)}, u32[]{:S(2)}) copy-start(pred[1024]{0:T(1024)(128)(4,1)S(1)} %get-tuple-element.133) | copy-start | bytes 3076
  114.3 6.8 %copy-start.37 = (pred[1024]{0:T(1024)(128)(4,1)}, pred[1024]{0:T(1024)(128)(4,1)S(1)}, u32[]{:S(2)}) copy-start(pred[1024]{0:T(1024)(128)(4,1)S(1)} %get-tuple-element.134) | copy-start | bytes 3076
  114.3 6.7 %copy-start.26 = (f32[1,8,128]{2,0,1:T(1,128)}, f32[1,8,128]{2,0,1:T(1,128)S(1)}, u32[]{:S(2)}) copy-start(f32[1,8,128]{2,0,1:T(1,128)S(1)} %get-tuple-element.125) | copy-start | bytes 12292
  114.4 6.7 %copy-start.28 = (f32[1,8,128]{2,0,1:T(1,128)}, f32[1,8,128]{2,0,1:T(1,128)S(1)}, u32[]{:S(2)}) copy-start(f32[1,8,128]{2,0,1:T(1,128)S(1)} %get-tuple-element.126) | copy-start | bytes 12292
  121.1 52.3 %copy-start = (bf16[1024,1024]{1,0:T(8,128)(2,1)}, bf16[1024,1024]{1,0:T(8,128)(2,1)S(1)}, u32[]{:S(2)}) copy-start(bf16[1024,1024]{1,0:T(8,128)(2,1)S(1)} %get-tuple-element.118.xc_ref) | copy-start | bytes 6291460
  165.2 8.2 %copy-start.11 = (f32[8,1024]{1,0:T(8,128)}, f32[8,1024]{1,0:T(8,128)S(1)}, u32[]{:S(2)}) copy-start(f32[8,1024]{1,0:T(8,128)S(1)} %pad.31.vec_ref) | copy-start | bytes 98308
  165.2 7.8 %copy-start.30 = (f32[1024]{0:T(1024)S(1)}, f32[1024]{0:T(1024)}, u32[]{:S(2)}) copy-start(f32[1024]{0:T(1024)} %get-tuple-element.130) | copy-start | bytes 12292
  165.2 8.2 %copy-start.8 = (bf16[1024,128]{1,0:T(8,128)(2,1)S(1)}, bf16[1024,128]{1,0:T(8,128)(2,1)}, u32[]{:S(2)}) copy-start(bf16[1024,128]{1,0:T(8,128)(2,1)} %copy-done.7) | copy-start | bytes 786436
  173.2 33.0 %copy-start.3 = (f32[1024,128]{1,0:T(8,128)}, f32[1024,128]{1,0:T(8,128)S(1)}, u32[]{:S(2)}) copy-start(f32[1024,128]{1,0:T(8,128)S(1)} %broadcast_in_dim.125.keep_ref) | copy-start | bytes 1572868
  173.4 32.8 %copy-start.4 = (f32[1024,128]{1,0:T(8,128)}, f32[1024,128]{1,0:T(8,128)S(1)}, u32[]{:S(2)}) copy-start(f32[1024,128]{1,0:T(8,128)S(1)} %broadcast_in_dim.126.ksum_ref) | copy-start | bytes 1572868
  173.4 34.1 %copy-start.40 = (bf16[8,128,2048]{2,1,0:T(8,128)(2,1)S(1)}, bf16[8,128,2048]{2,1,0:T(8,128)(2,1)}, u32[]{:S(2)}) copy-start(bf16[8,128,2048]{2,1,0:T(8,128)(2,1)} %get-tuple-element.51) | copy-start | bytes 12582916
  305.6 35.1 %copy-start.17 = (bf16[8,128,160]{2,1,0:T(8,128)(2,1)S(1)}, bf16[8,128,160]{2,1,0:T(8,128)(2,1)}, u32[]{:S(2)}) copy-start(bf16[8,128,160]{2,1,0:T(8,128)(2,1)} %copy-done.16) | copy-start | bytes 983044
  305.6 35.1 %copy-start.32 = (pred[1024]{0:T(1024)(128)(4,1)S(1)}, pred[1024]{0:T(1024)(128)(4,1)}, u32[]{:S(2)}) copy-start(pred[1024]{0:T(1024)(128)(4,1)} %copy-done.31) | copy-start | bytes 3076
  337.4 122.6 %collective-permute-start = (bf16[128,2048]{1,0:T(8,128)(2,1)S(1)}, bf16[128,2048]{1,0:T(8,128)(2,1)}, u32[]{:S(2)}, u32[]{:S(2)}) collective-permute-start(bf16[128,2048]{1,0:T(8,128)(2,1)S(1)} %get-tuple-element.74), channel_id=1, source_target_pairs={{0,0},{4,1},{1,2},{5,3},{2,4},{6,5},{3,6},{7,7},{8,8},{12,9},{9,10... | collective-permute-start | bytes 1572872 | tf_op jit(solution)/shard_map/ppermute | solution.py:1279
  340.7 5.5 %copy-start.20 = (bf16[1,1024,1024]{2,1,0:T(8,128)(2,1)S(1)}, bf16[1,1024,1024]{2,1,0:T(8,128)(2,1)}, u32[]{:S(2)}) copy-start(bf16[1,1024,1024]{2,1,0:T(8,128)(2,1)} %copy-done.19) | copy-start | bytes 6291460
  454.4 11.7 %copy-start.39 = (f32[1,2048]{1,0:T(1,128)S(1)}, f32[1,2048]{1,0:T(1,128)}, u32[]{:S(2)}) copy-start(f32[1,2048]{1,0:T(1,128)} %get-tuple-element.69) | copy-start | bytes 24580
  454.4 12.3 %copy-start.22 = (f32[256,2048]{1,0:T(8,128)S(1)}, f32[256,2048]{1,0:T(8,128)}, u32[]{:S(2)}) copy-start(f32[256,2048]{1,0:T(8,128)} %get-tuple-element.150) | copy-start | bytes 6291460
  (20 other events, 58.9 us)
Sparse Core Ops, SparseCore 0:
  111.8 92.5 all-gather.1
  213.7 79.3 reduce-scatter.1
